TPU v7x, 32 devices: a whole 2x2x4 slice. The times are simulated.
32 devices in a mesh: var: 4 (over x, core), dp: 8 (over z, y).
Axes of the slice: x: 2, y: 2, z: 4, core: 2. Of those that a mesh axis runs over, the one named last changes fastest.
Arguments:
- pixels: bfloat16 [72, 4, 8, 1024], P('var', None, 'dp'), may hold values from -6 to 6
- var_mask: int32 [72], P('var'), may hold values from 0 to 1, as said below
- lengths: int32 [8], P('dp'), may hold values from 64 to 1024, as said below
- condition: bfloat16 [8, 384], P('dp'), may hold values from -6 to 6
- cotangent: float32 [8, 1024, 384], P('dp', 'var'), may hold values from -6 to 6
- master: float32 [5898240], P(('var', 'dp'))
- moment_one: float32 [5898240], P(('var', 'dp')), may hold values from -6 to 6
- moment_two: float32 [5898240], P(('var', 'dp')), may hold values from 0.1024 to 1.6384
Outputs:
- output: float32 [8, 1024, 384], P('dp', 'var')
- pixel_grad: float32 [72, 4, 8, 1024], P('var', None, 'dp')
- grad_norm: float32 [], replicated
- new_master: float32 [5898240], P(('var', 'dp'))
- new_moment_one: float32 [5898240], P(('var', 'dp'))
- new_moment_two: float32 [5898240], P(('var', 'dp'))
- new_copy: bfloat16 [5898240], P(('var', 'dp'))
Inputs may be any that keep to these rules, and one draw needn't show every extreme that they name: `lengths`: each sequence is a fine item of 1024 valid patches or a coarse item of 64 valid patches followed by padding. `var_mask`: variable 0 is always present.
All inputs are finite; a program needn't handle non-finite values.
Results may differ from a plain program's by a relative error of at most 0.022.
The roundings to bfloat16 on the way count: a program that leaves them out, or rounds other values in their place, can miss the bound.
Values may be sent and summed in bfloat16 or wider, within the bound.
No kernel may reach another device: no remote copies, remote signals or barrier semaphores. Data moves between devices by JAX's collectives and lax.ppermute only.
A program may use at most 256 MiB of HBM per device.

v0:
```python
import math

import jax
import jax.numpy as jnp
from jax import lax
from jax.sharding import PartitionSpec as P

D = 384
HEADS = 6
FF = 1536
VARS = 72
PIX = 4
LAYERS = 2
STEP = 3
PARAMS = 5866368


NEG_BIG = -1e30
NORM_EPS = 1e-06
CLIP_COEF = 0.005
LEARN_RATE = 0.06
WEIGHT_DECAY = 0.1
ADAM_EPS = 1e-08
BETA_ONE = 0.5
BETA_TWO = 0.5


def combined_all(value, axis, join):
    pieces = jax.tree.map(lambda part: lax.all_gather(part, axis), value)
    head = jax.tree.map(lambda part: part[0], pieces)
    tail = jax.tree.map(lambda part: part[1:], pieces)
    so_far, _ = lax.scan(lambda so_far, share: (join(so_far, share), None), head, tail)
    return so_far


def shape_list():
    shapes = [(VARS, PIX, D), (D,), (D, 2 * D), (D, D)]
    for layer_idx in range(LAYERS):
        shapes = shapes + [(D, 6 * D), (6 * D,), (D, 3 * D), (D, D), (D, FF), (FF, D)]
    return shapes


def unpack(flat_vec):
    segments = []
    offset = 0
    for extents in shape_list():
        entries = 1
        for extent in extents:
            entries = entries * extent
        segments.append(flat_vec[offset : offset + entries].reshape(extents))
        offset = offset + entries
    return segments


def pack(segments, padded):
    flat_vec = jnp.concatenate([segment.reshape(-1) for segment in segments])
    return jnp.concatenate([flat_vec, jnp.zeros((padded - flat_vec.shape[0],), jnp.float32)])


def matmul(left_mat, right_mat):
    return jnp.dot(left_mat, right_mat, preferred_element_type=jnp.float32)


def contract_rows(left_mat, right_mat):
    return lax.dot_general(
        left_mat, right_mat, (((0,), (0,)), ((), ())), preferred_element_type=jnp.float32
    )


def matmul_nt(left_mat, right_mat):
    return lax.dot_general(
        left_mat, right_mat, (((1,), (1,)), ((), ())), preferred_element_type=jnp.float32
    )


def layer_norm(values):
    centered = values - jnp.mean(values, axis=-1, keepdims=True)
    inverse = lax.rsqrt(jnp.mean(centered * centered, axis=-1, keepdims=True) + NORM_EPS)
    return (centered * inverse, inverse)


def norm_back(grad_normed, normed, inverse):
    mean_grad = jnp.mean(grad_normed, axis=-1, keepdims=True)
    mean_cross = jnp.mean(grad_normed * normed, axis=-1, keepdims=True)
    return inverse * (grad_normed - mean_grad - normed * mean_cross)


def widen(per_head, head_dim):
    return jnp.repeat(per_head, head_dim, axis=-1)


def head_sum(values, head_count):
    return jnp.sum(values.reshape(values.shape[:-1] + (head_count, -1)), axis=-1)


def gelu_tanh(values):
    return jax.nn.gelu(values, approximate=True)


def merge_stats(first, second):
    peak_a, total_a, weighted_a = first
    peak_b, total_b, weighted_b = second
    head_dim = weighted_a.shape[-1] // peak_a.shape[-1]
    highest = jnp.maximum(peak_a, peak_b)
    factor_a = jnp.exp(peak_a - highest)
    factor_b = jnp.exp(peak_b - highest)
    return (
        highest,
        total_a * factor_a + total_b * factor_b,
        weighted_a * widen(factor_a, head_dim) + weighted_b * widen(factor_b, head_dim),
    )


def attend(queries, keys_vals, key_live, head_count, score_scale):
    model_width = queries.shape[1]
    head_dim = model_width // head_count
    outputs = []
    log_sums = []
    for head_idx in range(head_count):
        col_start = head_idx * head_dim
        col_stop = col_start + head_dim
        scores = (
            matmul_nt(queries[:, col_start:col_stop], keys_vals[:, col_start:col_stop])
            * score_scale
        )
        scores = jnp.where(key_live[None, :], scores, NEG_BIG)
        highest = jnp.max(scores, axis=1, keepdims=True)
        exponent = jnp.exp(scores - highest)
        row_total = jnp.sum(exponent, axis=1, keepdims=True)
        probs_low = (exponent / row_total).astype(jnp.bfloat16)
        outputs.append(
            matmul(probs_low, keys_vals[:, model_width + col_start : model_width + col_stop])
        )
        log_sums.append(highest + jnp.log(row_total))
    return (jnp.concatenate(outputs, axis=1), jnp.concatenate(log_sums, axis=1))


def attend_back(queries, keys_vals, log_sums, grad_attended, key_live, head_count, score_scale):
    model_width = queries.shape[1]
    head_dim = model_width // head_count
    grad_queries = []
    grad_keys = []
    grad_values = []
    inner_sums = []
    for head_idx in range(head_count):
        col_start = head_idx * head_dim
        col_stop = col_start + head_dim
        query_head = queries[:, col_start:col_stop]
        key_head = keys_vals[:, col_start:col_stop]
        value_head = keys_vals[:, model_width + col_start : model_width + col_stop]
        scores = matmul_nt(query_head, key_head) * score_scale
        scores = jnp.where(key_live[None, :], scores, NEG_BIG)
        probabilities = jnp.exp(scores - log_sums[:, head_idx : head_idx + 1])
        grad_head = grad_attended[:, col_start:col_stop]
        grad_probs = matmul_nt(grad_head, value_head)
        inner_sum = jnp.sum(probabilities * grad_probs, axis=1, keepdims=True)
        inner_sums.append(inner_sum)
        grad_scores = (probabilities * (grad_probs - inner_sum)).astype(jnp.bfloat16)
        grad_queries.append(matmul(grad_scores, key_head) * score_scale)
        probs_low = probabilities.astype(jnp.bfloat16)
        grad_keys.append(contract_rows(grad_scores, query_head) * score_scale)
        grad_values.append(contract_rows(probs_low, grad_head))
    grad_queries = jnp.concatenate(grad_queries, axis=1)
    inner_sums = jnp.concatenate(inner_sums, axis=1)
    return (
        grad_queries,
        jnp.concatenate(grad_keys, axis=1),
        jnp.concatenate(grad_values, axis=1),
        inner_sums,
    )


def local(pixels, var_mask, lengths, condition, cotangent, master, moment_one, moment_two):
    head_count = HEADS
    head_dim = D // HEADS
    score_scale = head_dim ** (-0.5)
    var_count = lax.axis_size("var")
    var_index = lax.axis_index("var")
    row_count = cotangent.shape[1]
    seq_len = row_count * var_count
    local_vars = pixels.shape[0]
    params = unpack(lax.all_gather(master.astype(jnp.bfloat16), ("var", "dp"), axis=0, tiled=True))
    embed_weight, agg_query, kv_weight, agg_weight = params[:4]
    embed_weight_local = lax.dynamic_slice_in_dim(
        embed_weight, var_index * local_vars, local_vars, 0
    )
    patches = pixels[:, :, 0, :]
    var_valid = var_mask == 1
    head_of = jnp.arange(D) // head_dim
    query_table = jnp.where(
        head_of[:, None] == jnp.arange(head_count)[None, :],
        agg_query[:, None],
        jnp.zeros((), jnp.bfloat16),
    )

    def embed_one(carry, inputs):
        patch_v, weight_v = inputs
        embedded = contract_rows(patch_v, weight_v)
        embedded_low = embedded.astype(jnp.bfloat16)
        kv_low = matmul(embedded_low, kv_weight).astype(jnp.bfloat16)
        var_scores = matmul(kv_low[:, :D], query_table) * score_scale
        return (carry, (embedded_low, kv_low, var_scores))

    unused, (embed_low, kv_local, var_scores) = lax.scan(
        embed_one, 0, (patches, embed_weight_local)
    )
    masked = jnp.where(var_valid[:, None, None], var_scores, NEG_BIG)
    local_peak = jnp.max(masked, axis=0)
    local_weights = jnp.where(var_valid[:, None, None], jnp.exp(var_scores - local_peak), 0.0)
    local_total = jnp.sum(local_weights, axis=0)

    def accumulate(running, inputs):
        weight_v, kv_v = inputs
        return (running + widen(weight_v, head_dim) * kv_v[:, D:].astype(jnp.float32), None)

    local_acc, unused = lax.scan(
        accumulate, jnp.zeros((seq_len, D), jnp.float32), (local_weights, kv_local)
    )
    peak_all, total_all, acc_all = combined_all(
        (local_peak, local_total, local_acc), "var", merge_stats
    )
    agg_all = acc_all / widen(total_all, head_dim)
    lse_all = peak_all + jnp.log(total_all)
    agg_own = lax.dynamic_slice_in_dim(agg_all, var_index * row_count, row_count, 0)
    agg_low = agg_own.astype(jnp.bfloat16)
    residual = matmul(agg_low, agg_weight)
    cond_low = jax.nn.silu(condition.astype(jnp.float32)).astype(jnp.bfloat16)
    key_live = jnp.arange(seq_len) < lengths[0]
    stored = []
    for layer_idx in range(LAYERS):
        ada_weight, ada_bias, qkv_weight, proj_weight, up_weight, down_weight = params[
            4 + 6 * layer_idx : 10 + 6 * layer_idx
        ]
        modulation = (matmul(cond_low, ada_weight)[0] + ada_bias.astype(jnp.float32)).reshape(6, D)
        normed_one, inverse_one = layer_norm(residual)
        hidden_one = (normed_one * (1.0 + modulation[1]) + modulation[0]).astype(jnp.bfloat16)
        qkv_low = matmul(hidden_one, qkv_weight).astype(jnp.bfloat16)
        keys_vals = lax.all_gather(qkv_low[:, D:], "var", axis=0, tiled=True)
        attended, log_sums = attend(qkv_low[:, :D], keys_vals, key_live, head_count, score_scale)
        attended_low = attended.astype(jnp.bfloat16)
        branch_one = matmul(attended_low, proj_weight)
        middle = residual + modulation[2] * branch_one
        normed_two, inverse_two = layer_norm(middle)
        hidden_two = (normed_two * (1.0 + modulation[4]) + modulation[3]).astype(jnp.bfloat16)
        pre_act = matmul(hidden_two, up_weight)
        act_low = gelu_tanh(pre_act).astype(jnp.bfloat16)
        branch_two = matmul(act_low, down_weight)
        kept_keys = keys_vals
        stored.append(
            (
                modulation,
                normed_one,
                inverse_one,
                hidden_one,
                qkv_low,
                kept_keys,
                log_sums,
                attended_low,
                branch_one,
                normed_two,
                inverse_two,
                hidden_two,
                pre_act,
                act_low,
                branch_two,
            )
        )
        residual = middle + modulation[5] * branch_two
    layer_grads = [None] * LAYERS
    grad_out = cotangent[0]
    for layer_idx in reversed(range(LAYERS)):
        ada_weight, ada_bias, qkv_weight, proj_weight, up_weight, down_weight = params[
            4 + 6 * layer_idx : 10 + 6 * layer_idx
        ]
        (
            modulation,
            normed_one,
            inverse_one,
            hidden_one,
            qkv_low,
            kept_keys,
            log_sums,
            attended_low,
            branch_one,
            normed_two,
            inverse_two,
            hidden_two,
            pre_act,
            act_low,
            branch_two,
        ) = stored[layer_idx]
        grad_gate_two = jnp.sum(grad_out * branch_two, axis=0)
        grad_branch_two = (modulation[5] * grad_out).astype(jnp.bfloat16)
        down_grad = contract_rows(act_low, grad_branch_two)
        grad_act = matmul_nt(grad_branch_two, down_weight)
        unused, gelu_pull = jax.vjp(gelu_tanh, pre_act)
        grad_pre = gelu_pull(grad_act)[0].astype(jnp.bfloat16)
        up_grad = contract_rows(hidden_two, grad_pre)
        grad_hidden_two = matmul_nt(grad_pre, up_weight)
        grad_shift_two = jnp.sum(grad_hidden_two, axis=0)
        grad_scale_two = jnp.sum(grad_hidden_two * normed_two, axis=0)
        grad_middle = grad_out + norm_back(
            grad_hidden_two * (1.0 + modulation[4]), normed_two, inverse_two
        )
        grad_gate_one = jnp.sum(grad_middle * branch_one, axis=0)
        grad_branch_one = (modulation[2] * grad_middle).astype(jnp.bfloat16)
        proj_grad = contract_rows(attended_low, grad_branch_one)
        grad_attended = matmul_nt(grad_branch_one, proj_weight).astype(jnp.bfloat16)
        keys_vals = kept_keys
        grad_queries, grad_keys_full, grad_values_full, inner_sums = attend_back(
            qkv_low[:, :D], keys_vals, log_sums, grad_attended, key_live, head_count, score_scale
        )
        grad_keys, grad_values = (
            lax.psum_scatter(
                grad_keys_full.astype(jnp.bfloat16), "var", scatter_dimension=0, tiled=True
            ).astype(jnp.float32),
            lax.psum_scatter(
                grad_values_full.astype(jnp.bfloat16), "var", scatter_dimension=0, tiled=True
            ).astype(jnp.float32),
        )
        grad_qkv = jnp.concatenate([grad_queries, grad_keys, grad_values], axis=1).astype(
            jnp.bfloat16
        )
        qkv_grad = contract_rows(hidden_one, grad_qkv)
        grad_hidden_one = matmul_nt(grad_qkv, qkv_weight)
        grad_shift_one = jnp.sum(grad_hidden_one, axis=0)
        grad_scale_one = jnp.sum(grad_hidden_one * normed_one, axis=0)
        grad_out = grad_middle + norm_back(
            grad_hidden_one * (1.0 + modulation[1]), normed_one, inverse_one
        )
        ada_bias_grad = jnp.concatenate(
            [
                grad_shift_one,
                grad_scale_one,
                grad_gate_one,
                grad_shift_two,
                grad_scale_two,
                grad_gate_two,
            ]
        )
        ada_weight_grad = cond_low[0].astype(jnp.float32)[:, None] * ada_bias_grad[None, :]
        layer_grads[layer_idx] = [
            ada_weight_grad,
            ada_bias_grad,
            qkv_grad,
            proj_grad,
            up_grad,
            down_grad,
        ]
    grad_res_low = grad_out.astype(jnp.bfloat16)
    agg_weight_grad = contract_rows(agg_low, grad_res_low)
    grad_agg_low = matmul_nt(grad_res_low, agg_weight).astype(jnp.bfloat16)
    grad_agg_all = lax.all_gather(grad_agg_low, "var", axis=0, tiled=True).astype(jnp.float32)
    inner_agg = head_sum(grad_agg_all * agg_all, head_count)
    query_float = agg_query.astype(jnp.float32)

    def back_one(carry, inputs):
        kv_grad_sum, query_grad_sum = carry
        embedded_v, kv_v, scores_v, valid_v, patch_v, weight_v = inputs
        probabilities = jnp.where(valid_v, jnp.exp(scores_v - lse_all), 0.0)
        grad_vals = widen(probabilities, head_dim) * grad_agg_all
        grad_probs = head_sum(grad_agg_all * kv_v[:, D:].astype(jnp.float32), head_count)
        grad_scores = widen(probabilities * (grad_probs - inner_agg) * score_scale, head_dim)
        grad_keys_v = grad_scores * query_float
        query_grad_sum = query_grad_sum + jnp.sum(
            grad_scores * kv_v[:, :D].astype(jnp.float32), axis=0
        )
        grad_kv = jnp.concatenate([grad_keys_v, grad_vals], axis=1).astype(jnp.bfloat16)
        kv_grad_sum = kv_grad_sum + contract_rows(embedded_v, grad_kv)
        grad_embed = matmul_nt(grad_kv, kv_weight).astype(jnp.bfloat16)
        weight_grad_v = matmul(patch_v, grad_embed)
        patch_grad_v = matmul_nt(weight_v, grad_embed)
        return ((kv_grad_sum, query_grad_sum), (weight_grad_v, patch_grad_v))

    start_carry = (jnp.zeros((D, 2 * D), jnp.float32), jnp.zeros((D,), jnp.float32))
    (kv_weight_grad, query_grad), (weight_grads_local, patch_grads) = lax.scan(
        back_one,
        start_carry,
        (embed_low, kv_local, var_scores, var_valid, patches, embed_weight_local),
    )
    embed_weight_grad = lax.dynamic_update_slice_in_dim(
        jnp.zeros((VARS, PIX, D), jnp.float32), weight_grads_local, var_index * local_vars, 0
    )
    all_grads = [embed_weight_grad, query_grad, kv_weight_grad, agg_weight_grad]
    for layer_idx in range(LAYERS):
        all_grads = all_grads + layer_grads[layer_idx]
    dp_count = lax.axis_size("dp")
    padded = master.shape[0] * var_count * dp_count
    grad_shard = lax.psum_scatter(
        pack(all_grads, padded), ("var", "dp"), scatter_dimension=0, tiled=True
    )
    squares = lax.psum(jnp.sum(grad_shard * grad_shard), ("var", "dp"))
    grad_norm = jnp.sqrt(squares)
    clip_limit = CLIP_COEF * math.sqrt(PARAMS * seq_len * dp_count)
    clipped = grad_shard * (clip_limit / jnp.maximum(grad_norm, clip_limit))
    new_one = BETA_ONE * moment_one + (1.0 - BETA_ONE) * clipped
    new_two = BETA_TWO * moment_two + (1.0 - BETA_TWO) * clipped * clipped
    ratio = (
        new_one / (1.0 - BETA_ONE**STEP) / (jnp.sqrt(new_two / (1.0 - BETA_TWO**STEP)) + ADAM_EPS)
    )
    new_master = master - LEARN_RATE * (ratio + WEIGHT_DECAY * master)
    return (
        residual[None],
        patch_grads[:, :, None, :],
        grad_norm,
        new_master,
        new_one,
        new_two,
        new_master.astype(jnp.bfloat16),
    )


def solution(mesh):
    in_specs = (
        P("var", None, "dp", None),
        P("var"),
        P("dp"),
        P("dp", None),
        P("dp", "var", None),
        P(("var", "dp")),
        P(("var", "dp")),
        P(("var", "dp")),
    )
    out_specs = (
        P("dp", "var", None),
        P("var", None, "dp", None),
        P(),
        P(("var", "dp")),
        P(("var", "dp")),
        P(("var", "dp")),
        P(("var", "dp")),
    )
    return jax.shard_map(local, mesh=mesh, in_specs=in_specs, out_specs=out_specs, check_vma=False)
```

profile of v0, /device:TPU:0, one launch (start us, length us, event | category | flops | bytes accessed | tf_op | source)
XLA Modules:
  0.0 1569.9 jit_solution(2022036789963166732)
XLA Ops:
  10.6 96.0 %all-gather.8.cloned.1.call-done = bf16[5898240]{0:T(1024)(128)(2,1)} async-done(((bf16[184320]{0:T(1024)(128)(2,1)}), bf16[5898240]{0:T(1024)(128)(2,1)}) %all-gather.8.cloned.1.call-update) | async-done | bytes 11796496 | tf_op jit(solution)/shard_map/all_gather | solution.py:182
  111.5 167.6 %while.62 = (s32[]{:T(128)}, bf16[18,1024,384]{2,1,0:T(8,128)(2,1)}, bf16[18,1024,768]{1,2,0:T(8,128)(2,1)}, f32[18,1024,6]{1,2,0:T(8,128)}, bf16[18,4,1024]{2,1...) while((s32[]{:T(128)}, ...), condition=%wide.region_1.2_spmd.clone.clone, body=%wide.region_0.1_spmd.clone.sunk.clone | while | flops 613034496 | bytes 17940104 | solution.py:204
  280.3 5.4 all-gather
  288.2 5.4 all-gather.1
  297.9 39.2 %while.63 = (s32[]{:T(128)}, f32[1024,384]{0,1:T(8,128)S(1)}, f32[18,1024,6]{1,2,0:T(8,128)S(1)}, bf16[18,1024,768]{1,2,0:T(8,128)(2,1)}) while((s32[]{:T(128)}, f32[1024,384]{0,1:T(8,128)S(1)}, f32[18,1024,6]{1,2,0:T(8,128)S(1)}, bf16[18,1024,768]{1,2,0:T(8,128)(2,1)}) %tuple.198), condition=%wide.region_5.6_spmd.clone.clone, body=%wide.region_4.5_spmd.clone.sunk.clone | while | flops 1572867 | bytes 7151695 | solution.py:216
  339.0 2.8 fusion.334
  341.8 3.2 fusion.335
  345.0 2.9 reshape.444
  347.9 3.0 reshape.446
  350.9 3.0 reshape.443
  357.2 26.5 %all-gather.14.cloned.1.call-done = f32[4096,384]{1,0:T(8,128)} async-done(((f32[1024,384]{1,0:T(8,128)}), f32[4096,384]{1,0:T(8,128)}) %all-gather.14.cloned.1.call-update) | async-done | bytes 6291472 | tf_op jit(solution)/shard_map/all_gather | solution.py:29
  386.7 4.9 slice.508
  391.6 17.1 %while.61 = (s32[]{:T(128)}, f32[1024,6]{0,1:T(8,128)S(1)}, f32[1024,6]{0,1:T(8,128)S(1)}, f32[1024,384]{0,1:T(8,128)}, f32[3,1024,6]{1,2,0:T(8,128)}, /*index=5*/f32[3,1024,6]{1,2,0:T(8,128)}, f32[3,1024,384]{2,1,0:T(8,128)}) while((s32[]{:T(128)}, f32[1024,6]{0,1:T(8,128)S(1)}, f32[1024,6]{0,1:T(8,128)S(1)}, ...), condition=%wide.region_7.8_spmd.clone, body=%wide.region_6.7_spmd.sunk.clone | while | flops 1216514 | bytes 11255901 | solution.py:32
  394.4 2.9 fusion.449
  400.1 2.9 fusion.449
  405.7 2.9 fusion.449
  417.7 4.8 fusion.332
  423.3 2.9 reshape.447
  429.8 7.2 all-gather.10.cloned.1.call-done
  461.8 3.5 reshape.448
  465.3 3.2 slice.473
  520.0 3.3 reshape.460
  523.3 3.2 reshape.459
  547.4 17.8 %reduce-scatter.7.cloned.1.call-done = bf16[256,384]{0,1:T(8,128)(2,1)} async-done(((bf16[1024,384]{0,1:T(8,128)(2,1)}), bf16[256,384]{0,1:T(8,128)(2,1)}) %reduce-scatter.7.cloned.1.call-update) | async-done | bytes 196624 | tf_op jit(solution)/shard_map/reduce_scatter | solution.py:317
  566.9 2.8 multiply_reduce_fusion.15
  578.7 2.9 fusion.319
  607.1 3.2 reshape.456
  612.9 3.2 reshape.455
  634.9 13.4 reduce-scatter.11.cloned.1.call-done
  654.3 2.9 fusion.316
  657.1 8.2 all_gather.39
  667.8 3.1 copy.48
  673.9 241.6 %while.64 = (s32[]{:T(128)}, f32[384,768]{1,0:T(8,128)}, f32[384]{0:T(512)S(1)}, f32[18,4,384]{2,1,0:T(4,128)S(1)}, f32[18,4,1024]{2,1,0:T(4,128)}, /*index=5*/b...) while((s32[]{:T(128)}, f32[384,768]{1,0:T(8,128)}, ...), condition=%wide.region_68.69_spmd.clone.clone, body=%wide.region_65.68_spmd.clone.sunk.clone | while | flops 1225482624 | bytes 37817104 | solution.py:376
  918.1 3.5 broadcast_multiply_fusion
  921.5 2.8 mul.804
  924.3 4.6 mul.797
  932.0 11.4 dynamic-update-slice.2
  945.5 31.2 %dynamic-update-slice.4 = f32[5898240]{0:T(1024)} dynamic-update-slice(f32[5898240]{0:T(1024)} %constant_dynamic-update-slice_fusion.32, f32[884736]{0:T(1024)} %mul.797, s32[]{} %constant.175) | dynamic-update-slice | bytes 7077892
  984.5 16.3 %dynamic-update-slice.11 = f32[5898240]{0:T(1024)} dynamic-update-slice(f32[5898240]{0:T(1024)} %constant_dynamic-update-slice_fusion.26, f32[442368]{0:T(1024)} %reshape.453, s32[]{} %constant.182) | dynamic-update-slice | bytes 3538948
  1003.0 21.2 %dynamic-update-slice.13 = f32[5898240]{0:T(1024)} dynamic-update-slice(f32[5898240]{0:T(1024)} %constant_dynamic-update-slice_fusion.25, f32[589824]{0:T(1024)} %reshape.455, s32[]{} %constant.184) | dynamic-update-slice | bytes 4718596
  1024.2 21.3 %dynamic-update-slice.14 = f32[5898240]{0:T(1024)} dynamic-update-slice(f32[5898240]{0:T(1024)} %dynamic-update-slice.13, f32[589824]{0:T(1024)} %reshape.456, s32[]{} %constant.185) | dynamic-update-slice | bytes 4718596
  1045.6 29.6 %dynamic-update-slice.15 = f32[5898240]{0:T(1024)} dynamic-update-slice(f32[5898240]{0:T(1024)} %dynamic-update-slice.14, f32[884736]{0:T(1024)S(1)} %mul.804, s32[]{} %constant.186) | dynamic-update-slice | bytes 7077892
  1083.0 16.3 %dynamic-update-slice.22 = f32[5898240]{0:T(1024)} dynamic-update-slice(f32[5898240]{0:T(1024)} %constant_dynamic-update-slice_fusion.19, f32[442368]{0:T(1024)} %reshape.457, s32[]{} %constant.193) | dynamic-update-slice | bytes 3538948
  1101.2 21.4 %dynamic-update-slice.24 = f32[5898240]{0:T(1024)} dynamic-update-slice(f32[5898240]{0:T(1024)} %constant_dynamic-update-slice_fusion.18, f32[589824]{0:T(1024)} %reshape.459, s32[]{} %constant.195) | dynamic-update-slice | bytes 4718596
  1122.6 20.2 %dynamic-update-slice.25 = f32[5898240]{0:T(1024)} dynamic-update-slice(f32[5898240]{0:T(1024)} %dynamic-update-slice.24, f32[589824]{0:T(1024)S(1)} %copy-done.29, s32[]{} %constant.196) | dynamic-update-slice | bytes 4718596
  1144.4 371.5 %all-reduce.3.cloned.1.call-done = f32[5898240]{0:T(1024)} async-done(((f32[5898240]{0:T(1024)}), f32[5898240]{0:T(1024)}) %all-reduce.3.cloned.1.call-update) | async-done | bytes 23592976
  1518.7 39.6 %psum.7 = f32[]{:T(128)} all-reduce(f32[]{:T(128)} %multiply_reduce_fusion.12), channel_id=1, replica_groups=mesh['var'=4,'dp'=8] {'var','dp'}, use_global_device_ids=true, to_apply=%region_83.84 | all-reduce | flops 1 | bytes 8 | tf_op jit(solution)/shard_map/psum | solution.py:392
  1559.0 3.0 fusion.326
  (1124 shorter events, 687.7 us)
Async XLA Ops:
  7.2 99.4 %all-gather.8.cloned.1.call-start = ((), (), s32[]{:S(2)}) async-start(), calls=%async_computation.4 | async-start | bytes 12165120 | tf_op jit(solution)/shard_map/all_gather | solution.py:182
  9.1 374.5 %all-gather.14.cloned.1.call-start = ((), (), s32[]{:S(2)}) async-start(), calls=%async_computation.11 | async-start | bytes 7864320 | tf_op jit(solution)/shard_map/all_gather | solution.py:29
  10.6 276.4 %copy-start.179 = (pred[18]{0:T(512)(128)(4,1)}, pred[18]{0:T(512)(128)(4,1)S(1)}, u32[]{:S(2)}) copy-start(pred[18]{0:T(512)(128)(4,1)S(1)} %broadcast_compare_fusion) | copy-start | bytes 58
  279.1 18.0 %copy-start.100 = (bf16[18,4,384]{2,1,0:T(4,128)(2,1)}, bf16[18,4,384]{2,1,0:T(4,128)(2,1)S(1)}, u32[]{:S(2)}) copy-start(bf16[18,4,384]{2,1,0:T(4,128)(2,1)S(1)} %get-tuple-element.1067) | copy-start | bytes 165892
  338.8 98.3 %all-gather.10.cloned.1.call-start = ((), (), s32[]{:S(2)}) async-start(), calls=%async_computation.5 | async-start | bytes 1966080 | tf_op jit(solution)/shard_map/all_gather | solution.py:238
  357.2 57.5 %copy-start.103 = (f32[384]{0:T(512)}, f32[384]{0:T(512)S(1)}, u32[]{:S(2)}) copy-start(f32[384]{0:T(512)S(1)} %get-tuple-element.592) | copy-start | bytes 4612
  417.2 61.2 %all-gather.12.cloned.1.call-start = ((), (), s32[]{:S(2)}) async-start(), calls=%async_computation.6 | async-start | bytes 1966080 | tf_op jit(solution)/shard_map/all_gather | solution.py:238
  438.5 12.1 copy-start.154
  438.8 11.8 copy-start.170
  440.2 10.0 copy-start.155
  440.5 9.7 copy-start.171
  458.6 87.1 %reduce-scatter.5.cloned.1.call-start = ((), (), s32[]{:S(2)}) async-start(), calls=%async_computation.7 | async-start | bytes 983040 | tf_op jit(solution)/shard_map/reduce_scatter | solution.py:314
  479.9 27.4 %copy-start.9 = (f32[256,1024]{1,0:T(8,128)}, f32[256,1024]{1,0:T(8,128)S(1)}, u32[]{:S(2)}) copy-start(f32[256,1024]{1,0:T(8,128)S(1)} %get-tuple-element.561) | copy-start | bytes 3145732
  480.2 27.1 %copy-start.135 = (f32[256]{0:T(256)}, f32[256]{0:T(256)S(1)}, u32[]{:S(2)}) copy-start(f32[256]{0:T(256)S(1)} %log_add_fusion.7) | copy-start | bytes 3076
  481.6 26.8 %copy-start.11 = (f32[256,1024]{1,0:T(8,128)}, f32[256,1024]{1,0:T(8,128)S(1)}, u32[]{:S(2)}) copy-start(f32[256,1024]{1,0:T(8,128)S(1)} %get-tuple-element.559) | copy-start | bytes 3145732
  481.9 26.5 %copy-start.137 = (f32[256]{0:T(256)}, f32[256]{0:T(256)S(1)}, u32[]{:S(2)}) copy-start(f32[256]{0:T(256)S(1)} %log_add_fusion.8) | copy-start | bytes 3076
  483.4 25.8 %copy-start.13 = (f32[256,1024]{1,0:T(8,128)}, f32[256,1024]{1,0:T(8,128)S(1)}, u32[]{:S(2)}) copy-start(f32[256,1024]{1,0:T(8,128)S(1)} %get-tuple-element.557) | copy-start | bytes 3145732
  483.8 25.4 %copy-start.139 = (f32[256]{0:T(256)}, f32[256]{0:T(256)S(1)}, u32[]{:S(2)}) copy-start(f32[256]{0:T(256)S(1)} %log_add_fusion.9) | copy-start | bytes 3076
  485.2 24.7 %copy-start.15 = (f32[256,1024]{1,0:T(8,128)}, f32[256,1024]{1,0:T(8,128)S(1)}, u32[]{:S(2)}) copy-start(f32[256,1024]{1,0:T(8,128)S(1)} %get-tuple-element.555) | copy-start | bytes 3145732
  485.5 24.4 %copy-start.141 = (f32[256]{0:T(256)}, f32[256]{0:T(256)S(1)}, u32[]{:S(2)}) copy-start(f32[256]{0:T(256)S(1)} %log_add_fusion.10) | copy-start | bytes 3076
  487.0 23.7 %copy-start.17 = (f32[256,1024]{1,0:T(8,128)}, f32[256,1024]{1,0:T(8,128)S(1)}, u32[]{:S(2)}) copy-start(f32[256,1024]{1,0:T(8,128)S(1)} %get-tuple-element.553) | copy-start | bytes 3145732
  487.4 23.4 %copy-start.143 = (f32[256]{0:T(256)}, f32[256]{0:T(256)S(1)}, u32[]{:S(2)}) copy-start(f32[256]{0:T(256)S(1)} %log_add_fusion.11) | copy-start | bytes 3076
  489.2 15.6 copy-start.18
  489.6 15.2 copy-start.145
  515.8 49.3 %reduce-scatter.7.cloned.1.call-start = ((), (), s32[]{:S(2)}) async-start(), calls=%async_computation.8 | async-start | bytes 983040 | tf_op jit(solution)/shard_map/reduce_scatter | solution.py:317
  535.4 97.8 %reduce-scatter.9.cloned.1.call-start = ((), (), s32[]{:S(2)}) async-start(), calls=%async_computation.9 | async-start | bytes 983040 | tf_op jit(solution)/shard_map/reduce_scatter | solution.py:314
  535.4 8.4 copy-start.58
  541.7 25.1 %copy-start.108 = (f32[384]{0:T(512)S(1)}, f32[384]{0:T(512)}, u32[]{:S(2)}) copy-start(f32[384]{0:T(512)} %get-tuple-element.524) | copy-start | bytes 4612
  541.7 25.1 %copy-start.110 = (f32[256]{0:T(256)S(1)}, f32[256]{0:T(256)}, u32[]{:S(2)}) copy-start(f32[256]{0:T(256)} %copy-done.109) | copy-start | bytes 3076
  575.3 15.4 copy-start.41
  587.2 8.9 copy-start.49
  597.1 51.1 %reduce-scatter.11.cloned.1.call-start = ((), (), s32[]{:S(2)}) async-start(), calls=%async_computation.10 | async-start | bytes 983040 | tf_op jit(solution)/shard_map/reduce_scatter | solution.py:317
  624.8 891.1 %all-reduce.3.cloned.1.call-start = ((), (), s32[]{:S(2)}) async-start(), calls=%async_computation.12 | async-start | bytes 47185920
  630.2 19.7 %copy-start.104 = (f32[384]{0:T(512)S(1)}, f32[384]{0:T(512)}, u32[]{:S(2)}) copy-start(f32[384]{0:T(512)} %copy-done.103) | copy-start | bytes 4612
  630.2 19.7 %copy-start.113 = (f32[256]{0:T(256)S(1)}, f32[256]{0:T(256)}, u32[]{:S(2)}) copy-start(f32[256]{0:T(256)} %copy-done.112) | copy-start | bytes 3076
  630.2 19.7 %copy-start.148 = (f32[256]{0:T(256)S(1)}, f32[256]{0:T(256)}, u32[]{:S(2)}) copy-start(f32[256]{0:T(256)} %copy-done.147) | copy-start | bytes 3076
  633.2 19.4 %copy-start.36 = (f32[256,384]{1,0:T(8,128)S(1)}, f32[256,384]{1,0:T(8,128)}, u32[]{:S(2)}) copy-start(f32[256,384]{1,0:T(8,128)} %copy-done.35) | copy-start | bytes 1179652
  945.5 35.1 %copy-start.167 = (f32[384]{0:T(512)S(1)}, f32[384]{0:T(512)}, u32[]{:S(2)}) copy-start(f32[384]{0:T(512)} %get-tuple-element.400) | copy-start | bytes 4612
  1045.6 32.2 %copy-start.164 = (f32[384]{0:T(512)S(1)}, f32[384]{0:T(512)}, u32[]{:S(2)}) copy-start(f32[384]{0:T(512)} %get-tuple-element.484) | copy-start | bytes 4612
  1045.6 33.5 %copy-start.162 = (f32[384]{0:T(512)S(1)}, f32[384]{0:T(512)}, u32[]{:S(2)}) copy-start(f32[384]{0:T(512)} %get-tuple-element.398) | copy-start | bytes 4612
  1045.6 34.8 %copy-start.161 = (f32[384]{0:T(512)S(1)}, f32[384]{0:T(512)}, u32[]{:S(2)}) copy-start(f32[384]{0:T(512)} %get-tuple-element.386) | copy-start | bytes 4612
  1045.6 36.1 %copy-start.163 = (f32[384]{0:T(512)S(1)}, f32[384]{0:T(512)}, u32[]{:S(2)}) copy-start(f32[384]{0:T(512)} %get-tuple-element.518) | copy-start | bytes 4612
  1083.0 16.3 %copy-start.74 = (f32[147456]{0:T(1024)S(1)}, f32[147456]{0:T(1024)}, u32[]{:S(2)}) copy-start(f32[147456]{0:T(1024)} %reshape.458) | copy-start | bytes 1769476
  1101.2 21.4 %copy-start.29 = (f32[589824]{0:T(1024)S(1)}, f32[589824]{0:T(1024)}, u32[]{:S(2)}) copy-start(f32[589824]{0:T(1024)} %reshape.460) | copy-start | bytes 7077892
  1144.3 373.4 %copy-start.99 = (f32[18,4,1024]{2,1,0:T(4,128)S(1)}, f32[18,4,1024]{2,1,0:T(4,128)}, u32[]{:S(2)}) copy-start(f32[18,4,1024]{2,1,0:T(4,128)} %get-tuple-element.204) | copy-start | bytes 884740
  1144.3 414.6 %copy-start.96 = (f32[184320]{0:T(1024)S(1)}, f32[184320]{0:T(1024)}, u32[]{:S(2)}) copy-start(f32[184320]{0:T(1024)} %param.22) | copy-start | bytes 2211844
  1144.3 414.6 %copy-start.97 = (f32[184320]{0:T(1024)S(1)}, f32[184320]{0:T(1024)}, u32[]{:S(2)}) copy-start(f32[184320]{0:T(1024)} %param.23) | copy-start | bytes 2211844
  1144.4 414.6 %copy-start.68 = (f32[184320]{0:T(1024)S(1)}, f32[184320]{0:T(1024)}, u32[]{:S(2)}) copy-start(f32[184320]{0:T(1024)} %param.21) | copy-start | bytes 2211844
  (212 other events, 508.4 us)
Sparse Core Ops, SparseCore 0:
  11.5 95.0 all-gather.7
  338.9 44.7 all-gather.13
  417.3 19.6 all-gather.9
  458.7 19.6 all-gather.11
  516.0 23.2 reduce-scatter.4
  541.8 23.2 reduce-scatter.6
  597.2 23.2 reduce-scatter.8
  624.9 23.3 reduce-scatter.10
  1144.5 371.3 all-reduce.2
where the time goes:
time: 1600 us; the launch traced here: 1570 us
  waiting for transfers between devices  533 us (33%)
  local copies, waits for them, and re-layouts  499 us (31%)
  matrix products  332 us (21%)
  other arithmetic  124 us (8%)
  blocking collectives  58.6 us (4%)
  between operations  18.6 us (1%)
    unnamed x10, waiting for transfers between devices  372 us
    unnamed x395, local copies, waits for them, and re-layouts  237 us
    dot_general x69, matrix products, contract_rows(): lax.dot_general(left_mat, right_mat, (((0,), (0,)), ((), ())), preferred_...  124 us
    dot_general x89, matrix products, matmul(): return jnp.dot(left_mat, right_mat, preferred_element_type=jnp.float32)  104 us
    dot_general x69, matrix products, matmul_nt(): lax.dot_general(left_mat, right_mat, (((1,), (1,)), ((), ())), preferred_...  104 us
    all_gather x1, waiting for transfers between devices, local(): lax.all_gather(master.astype(jnp.bfloat16), ('var', 'dp'), axis=0, tiled=...  96 us
    squeeze x54, local copies, waits for them, and re-layouts, local(): lax.scan(accumulate, jnp.zeros((seq_len, D), jnp.float32), (local_weights...  55.2 us
    dynamic_update_slice x36, local copies, waits for them, and re-layouts, local(): lax.scan(embed_one, 0, (patches, embed_weight_local))  54.1 us
  transfers between devices with their start and end apart: 9, of which 7 were waited for; matrix products, arithmetic and copies ran while one was open for 7% of the time, Pallas kernels for 0%

commit v1 on v0

v1 whole, which is shorter than its diff:
```python
import functools
import math

import jax
import jax.numpy as jnp
from jax import lax
from jax.experimental import pallas as pl
from jax.experimental.pallas import tpu as pltpu
from jax.sharding import PartitionSpec as P

D = 384
HEADS = 6
HEAD_DIM = D // HEADS
FF = 1536
VARS = 72
PIX = 4
LAYERS = 2
STEP = 3
PARAMS = 5866368

NEG_BIG = -1e30
NORM_EPS = 1e-06
CLIP_COEF = 0.005
LEARN_RATE = 0.06
WEIGHT_DECAY = 0.1
ADAM_EPS = 1e-08
BETA_ONE = 0.5
BETA_TWO = 0.5
SCORE_SCALE = HEAD_DIM ** (-0.5)

LANES = 128
DB = D // LANES
VP = VARS * PIX
ADA_LINES = 6 * D * D // LANES
BIAS_LINES = 6 * DB
QKV_LINES = 3 * D * D // LANES
PROJ_LINES = D * D // LANES
FF_LINES = D * FF // LANES
EMBED_LINES = VP * DB
KV_LINES = 2 * D * D // LANES
HEAD_LINES = EMBED_LINES + DB + KV_LINES + PROJ_LINES
LAYER_LINES = ADA_LINES + BIAS_LINES + QKV_LINES + PROJ_LINES + 2 * FF_LINES

bf16 = jnp.bfloat16
f32 = jnp.float32


def down16(value):
    return value // 16 * 16


def up16(value):
    return (value + 15) // 16 * 16


def nn(left, right):
    return lax.dot_general(left, right, (((1,), (0,)), ((), ())), preferred_element_type=f32)


def nt(left, right):
    return lax.dot_general(left, right, (((1,), (1,)), ((), ())), preferred_element_type=f32)


def tn(left, right):
    return lax.dot_general(left, right, (((0,), (0,)), ((), ())), preferred_element_type=f32)


def nn_f32(left, right, dims):
    return lax.dot_general(
        left,
        right,
        (dims, ((), ())),
        preferred_element_type=f32,
        precision=lax.Precision.HIGHEST,
    )


VM = pl.BlockSpec(memory_space=pltpu.VMEM)
SM = pl.BlockSpec(memory_space=pltpu.SMEM)
ANY = pl.BlockSpec(memory_space=pl.ANY)


def run(kernel, name, outs, ins, in_specs=None, scratch=(), flops=0, out_specs=None, vmem=32):
    if in_specs is None:
        in_specs = [VM] * len(ins)
    nbytes = sum(math.prod(o.shape) * o.dtype.itemsize for o in outs)
    nbytes += sum(math.prod(i.shape) * i.dtype.itemsize for i in ins)
    return pl.pallas_call(
        kernel,
        name=name,
        out_shape=outs,
        in_specs=in_specs,
        out_specs=out_specs or [VM] * len(outs),
        scratch_shapes=list(scratch),
        cost_estimate=pl.CostEstimate(flops=flops, bytes_accessed=nbytes, transcendentals=0),
        compiler_params=pltpu.CompilerParams(vmem_limit_bytes=vmem * 2**20),
    )(*ins)


def shape(dims, dtype):
    return jax.ShapeDtypeStruct(dims, dtype)


def mod_row(ref, index):
    return jnp.concatenate(
        [ref[DB * index + c : DB * index + c + 1, :] for c in range(DB)], axis=1
    )


def norm_stats(values):
    centered = values - jnp.mean(values, axis=-1, keepdims=True)
    inverse = lax.rsqrt(jnp.mean(centered * centered, axis=-1, keepdims=True) + NORM_EPS)
    return centered * inverse, inverse


def norm_back(grad_normed, normed, inverse):
    mean_grad = jnp.mean(grad_normed, axis=-1, keepdims=True)
    mean_cross = jnp.mean(grad_normed * normed, axis=-1, keepdims=True)
    return inverse * (grad_normed - mean_grad - normed * mean_cross)


def lane_half(shape_):
    return lax.broadcasted_iota(jnp.int32, shape_, 1) < HEAD_DIM


def half_of(pair, half):
    first = lane_half(pair.shape)
    keep = first if half == 0 else jnp.logical_not(first)
    return jnp.where(keep, pair, jnp.zeros_like(pair))


def put_row(ref, index, row):
    for c in range(DB):
        ref[DB * index + c : DB * index + c + 1, :] = row[:, c * LANES : (c + 1) * LANES]


def narrow_lines(src, count, dst):
    step = 512
    whole = count // step

    def body(i, carry):
        row = pl.multiple_of(i * step, step)
        dst[pl.ds(row, step), :] = src[pl.ds(row, step), :].astype(bf16)
        return carry

    if whole:
        lax.fori_loop(0, whole, body, 0)
    rest = count - whole * step
    if rest:
        dst[whole * step : count, :] = src[whole * step : count, :].astype(bf16)


def unpack(lines, start, rows, blocks, out):
    for c in range(blocks):
        out[:, c * LANES : (c + 1) * LANES] = lines[
            pl.ds(start + c, rows, stride=blocks), :
        ].astype(bf16)


class Source:
    def __init__(self, arrays, specs, planned):
        self.arrays = arrays
        self.specs = specs
        self.planned = planned

    def span(self, start, end):
        if not self.planned:
            return down16(start), up16(end)
        return start // HALF * HALF, -(-end // HALF) * HALF

    def load(self, refs, base, lines):
        if not self.planned:
            lines[...] = refs[0][base : base + lines.shape[0], :].astype(f32)
            return
        table = refs[0]
        starts = [o * 2 * HALF + h * HALF for o, h in ENTRIES]
        first = starts.index(base)
        count = lines.shape[0] // HALF
        assert starts[first : first + count] == [base + i * HALF for i in range(count)]

        def body(index, carry):
            code = table[first + index]
            place = code % 4
            at = pl.multiple_of(index * HALF, 16)
            for k in range(12):

                @pl.when(code // 4 == k)
                def copy_block(k=k):
                    lines[pl.ds(at, HALF), :] = refs[1 + k][place].astype(f32)

            return carry

        lax.fori_loop(0, count, body, 0)


def ada_kernel(shard_lines, place, shard, cond_all, spread, column, table, partial, hot):
    line = place[0] * shard_lines + lax.broadcasted_iota(jnp.int32, (shard_lines, 1), 0)
    feature = lax.broadcasted_iota(jnp.int32, (1, D), 1)
    target = jnp.full((shard_lines, 1), -1, jnp.int32)
    is_bias = jnp.zeros((shard_lines, 1), jnp.int32)
    rank = jnp.full((shard_lines, 1), -1, jnp.int32)
    for layer in range(LAYERS):
        begin = HEAD_LINES + layer * LAYER_LINES
        here = jnp.logical_and(line >= begin, line < begin + ADA_LINES)
        rank = jnp.where(here, line - begin, rank)
        target = jnp.where(here, layer * BIAS_LINES, target)
        bias = jnp.logical_and(
            line >= begin + ADA_LINES, line < begin + ADA_LINES + BIAS_LINES
        )
        target = jnp.where(bias, layer * BIAS_LINES + line - begin - ADA_LINES, target)
        is_bias = jnp.where(bias, 1, is_bias)
    passed = rank >= (feature + 1) * BIAS_LINES
    row = jnp.sum(passed.astype(f32), axis=1, keepdims=True).astype(jnp.int32)
    hot[...] = jnp.where(
        jnp.logical_and(rank >= 0, row == feature), 1.0, 0.0
    ).astype(bf16)
    target = jnp.where(rank >= 0, target + rank - row * BIAS_LINES, target)
    factors = nt(hot[...], cond_all[...])
    factors = nn(factors.astype(bf16), spread[...])
    factors = jnp.where(is_bias > 0, 1.0, factors)
    table[...] = jnp.where(target == column[...], factors, 0.0).astype(bf16)
    partial[...] = tn(table[...], shard[...])


def copy_lines(src, start, count, dst, at):
    step = 512
    whole = count // step

    def body(i, carry):
        row = pl.multiple_of(i * step, step)
        dst[pl.ds(at + row, step), :] = src[pl.ds(start + row, step), :]
        return carry

    if whole:
        lax.fori_loop(0, whole, body, 0)
    rest = count - whole * step
    if rest:
        dst[at + whole * step : at + count, :] = src[start + whole * step : start + count, :]


def pack_kernel(meta, table, *refs):
    sections = refs[: len(meta)]
    targets = refs[len(meta) : len(meta) + 6]
    lines = refs[len(meta) + 6]
    end = 0
    tile = None
    for i, (base, size) in enumerate(meta):
        if base > end:
            lines[end:base, :] = jnp.zeros((base - end, LANES), bf16)
        copy_lines(sections[i], 0, size, lines, base)
        if base < end:
            lines[base:end, :] = lines[base:end, :] + tile
        tile = sections[i][size - 16 : size, :]
        end = base + size
    lines[end:, :] = jnp.zeros((lines.shape[0] - end, LANES), bf16)

    def first_line(index):
        number = jnp.where(index < 7, index, jnp.where(index < 28, index + 8, index + 16))
        return number * HALF

    def body(index, carry):
        code = table[index]
        at = pl.multiple_of(first_line(index), 16)
        for k, target in enumerate(targets):

            @pl.when(code // 8 == k)
            def copy_block(target=target):
                target[code % 8] = lines[pl.ds(at, HALF), :]

        return carry

    lax.fori_loop(0, len(ENTRIES), body, 0)


def agg_fwd_kernel(source, *refs):
    pieces = refs[: len(source.arrays)]
    (
        planes, mod,
        res, hid, agg_low, probs, w, u, e, kvw, aggw, query, pix,
        lines, e32, mask,
    ) = refs[len(source.arrays) :]
    source.load(pieces, 0, lines)
    for p in range(PIX):
        for c in range(DB):
            e32[p * VARS : (p + 1) * VARS, c * LANES : (c + 1) * LANES] = lines[
                pl.ds(p * DB + c, VARS, stride=PIX * DB), :
            ]
    e[...] = e32[...].astype(bf16)
    query[...] = jnp.concatenate(
        [lines[EMBED_LINES + c : EMBED_LINES + c + 1, :] for c in range(DB)], axis=1
    )
    unpack(lines, EMBED_LINES + DB, D, 2 * DB, kvw)
    unpack(lines, EMBED_LINES + DB + KV_LINES, D, DB, aggw)
    w[...] = nn(e[...], kvw[...])
    lane = lax.broadcasted_iota(jnp.int32, (VP, LANES), 1)
    table = jnp.zeros((VP, LANES), f32)
    for h in range(HEADS):
        at = h // 2 * LANES
        prod = w[:, at : at + LANES] * query[:, at : at + LANES]
        total = jnp.sum(half_of(prod, h % 2), axis=1, keepdims=True) * SCORE_SCALE
        table = jnp.where(lane == h, total, table)
    u[...] = table
    count = planes.shape[2]
    for b in range(planes.shape[0]):
        for p in range(PIX):
            pix[p, b * count : (b + 1) * count, :] = planes[b, p].astype(f32)
        mask[b * count : (b + 1) * count, :] = planes[b, PIX, :, :LANES].astype(f32)
    live = mask[:, :1] > 0.0
    rows = pix.shape[2]
    for pair in range(HEADS // 2):
        pieces = []
        at = pair * LANES
        for half in range(2):
            h = pair * 2 + half
            scores = jnp.zeros((VARS, rows), f32)
            for p in range(PIX):
                scores += pix[p] * u[p * VARS : (p + 1) * VARS, h : h + 1]
            scores = jnp.where(live, scores, NEG_BIG)
            highest = jnp.max(scores, axis=0, keepdims=True)
            exponent = jnp.where(live, jnp.exp(scores - highest), 0.0)
            prob = exponent / jnp.sum(exponent, axis=0, keepdims=True)
            probs[h] = prob
            weighted = jnp.concatenate([pix[p] * prob for p in range(PIX)], axis=0)
            pieces.append(nn_f32(weighted, w[:, D + at : D + at + LANES], ((0,), (0,))))
        both = jnp.where(lane_half(pieces[0].shape), pieces[0], pieces[1])
        agg_low[:, at : at + LANES] = both.astype(bf16)
    residual = nn(agg_low[...], aggw[...])
    res[...] = residual
    normed, unused = norm_stats(residual)
    hid[...] = (normed * (1.0 + mod_row(mod, 1)) + mod_row(mod, 0)).astype(bf16)


def agg_bwd_kernel(
    go, agg_low, probs, w, u, e, kvw, aggw, query, pix,
    planes, sec,
    sec32, gv, gk, pixg,
):
    rows = pix.shape[2]
    grad_res = go[...].astype(bf16)
    agg_grad = tn(agg_low[...], grad_res)
    start = EMBED_LINES + DB + KV_LINES
    for c in range(DB):
        sec32[pl.ds(start + c, D, stride=DB), :] = agg_grad[:, c * LANES : (c + 1) * LANES]
    grad_agg = nt(grad_res, aggw[...]).astype(bf16)
    first = lane_half((VP, LANES))
    pixel_sum = [jnp.zeros((VARS, rows), f32) for p in range(PIX)]
    for p in range(PIX):
        pixg[p] = pixel_sum[p]
    for pair in range(HEADS // 2):
        at = pair * LANES
        ga_pair = grad_agg[:, at : at + LANES]
        w_pair = w[:, D + at : D + at + LANES]
        value_parts = []
        key_parts = []
        for half in range(2):
            h = pair * 2 + half
            prob = probs[h]
            ga_half = half_of(ga_pair, half)
            back = nn_f32(w_pair, ga_half.astype(f32), ((1,), (1,)))
            grad_probs = jnp.zeros((VARS, rows), f32)
            for p in range(PIX):
                grad_probs += pix[p] * back[p * VARS : (p + 1) * VARS, :]
            inner = jnp.sum(prob * grad_probs, axis=0, keepdims=True)
            grad_scores = prob * (grad_probs - inner)
            sums = []
            for p in range(PIX):
                here = slice(p * VARS, (p + 1) * VARS)
                pixg[p] += grad_scores * u[here, h : h + 1] + prob * back[here, :]
                sums.append(jnp.sum(pix[p] * grad_scores, axis=1, keepdims=True))
            key_parts.append(jnp.concatenate(sums, axis=0) * SCORE_SCALE)
            weighted = jnp.concatenate([pix[p] * prob for p in range(PIX)], axis=0)
            value_parts.append(nn(weighted.astype(bf16), ga_half))
        gv[:, at : at + LANES] = jnp.where(first, value_parts[0], value_parts[1])
        gk[:, at : at + LANES] = jnp.where(first, key_parts[0], key_parts[1])
    count = planes.shape[2]
    for b in range(planes.shape[0]):
        for p in range(PIX):
            planes[b, p] = pixg[p, b * count : (b + 1) * count, :]
    query_grad = jnp.sum(gk[...] * w[:, :D], axis=0, keepdims=True)
    for c in range(DB):
        sec32[EMBED_LINES + c : EMBED_LINES + c + 1, :] = query_grad[:, c * LANES : (c + 1) * LANES]
    grad_kv = jnp.concatenate([gk[...] * query[...], gv[...]], axis=1).astype(bf16)
    kv_grad = tn(e[...], grad_kv)
    start = EMBED_LINES + DB
    for c in range(2 * DB):
        sec32[pl.ds(start + c, D, stride=2 * DB), :] = kv_grad[:, c * LANES : (c + 1) * LANES]
    embed_grad = nt(grad_kv, kvw[...])
    for p in range(PIX):
        for c in range(DB):
            sec32[pl.ds(p * DB + c, VARS, stride=PIX * DB), :] = embed_grad[
                p * VARS : (p + 1) * VARS, c * LANES : (c + 1) * LANES
            ]
    tail = up16(HEAD_LINES) - HEAD_LINES
    sec32[HEAD_LINES:, :] = jnp.zeros((tail, LANES), f32)
    narrow_lines(sec32, up16(HEAD_LINES), sec)


def unpack_kernel(source, base, start, *refs):
    pieces = refs[: len(source.arrays)]
    qkvw, projw, upw, downw, lines = refs[len(source.arrays) :]
    source.load(pieces, base, lines)
    start = start - base
    unpack(lines, start, D, 3 * DB, qkvw)
    start += QKV_LINES
    unpack(lines, start, D, DB, projw)
    start += PROJ_LINES
    unpack(lines, start, D, FF // LANES, upw)
    start += FF_LINES
    unpack(lines, start, FF, DB, downw)


def gelu_parts(value):
    scale = math.sqrt(2.0 / math.pi)
    square = value * value
    tanh = jnp.tanh(scale * (value + 0.044715 * value * square))
    half = 0.5 * (1.0 + tanh)
    slope = half + 0.5 * value * (1.0 - tanh * tanh) * scale * (1.0 + 3.0 * 0.044715 * square)
    return value * half, slope


def layer_fwd_kernel(
    block_count, limits, *refs
):
    hidden = refs[:block_count]
    (res, mod, mod_next, qkvw, projw, upw, downw) = refs[block_count : block_count + 7]
    (qkv, att, lse, b1, mid, pre, b2, res_next, hid_next, h_low, a_low) = refs[block_count + 7 :]
    length = limits[0]
    mine = limits[1]
    rows = res.shape[0]
    seq_len = block_count * rows
    for rel in range(block_count):
        at = pl.multiple_of((mine ^ rel) * rows, rows)
        qkv[pl.ds(at, rows), :] = nn(hidden[rel][...], qkvw[...]).astype(bf16)
    position = lax.broadcasted_iota(jnp.int32, (1, seq_len), 1)
    bias = jnp.where(position < length, 0.0, NEG_BIG)
    own = pl.ds(pl.multiple_of(mine * rows, rows), rows)
    first = lane_half((rows, LANES))
    lane = lax.broadcasted_iota(jnp.int32, (rows, LANES), 1)
    lse[...] = jnp.zeros((rows, LANES), f32)

    def attend(pair, carry):
        at, k_at, v_at = (pl.ds(pl.multiple_of(pair * LANES + i * D, LANES), LANES) for i in range(3))
        query = qkv[own, at] * SCORE_SCALE
        keys = qkv[:, k_at]
        values = qkv[:, v_at]
        parts = []
        for half in range(2):
            scores = nt(half_of(query, half), keys) + bias
            highest = jnp.max(scores, axis=1, keepdims=True)
            exponent = jnp.exp(scores - highest)
            total = jnp.sum(exponent, axis=1, keepdims=True)
            prob = (exponent * (1.0 / total)).astype(bf16)
            parts.append(nn(prob, values))
            lse[...] = jnp.where(lane == pair * 2 + half, highest + jnp.log(total), lse[...])
        att[:, at] = jnp.where(first, parts[0], parts[1])
        return carry

    lax.fori_loop(0, HEADS // 2, attend, 0)
    branch_one = nn(att[...].astype(bf16), projw[...])
    b1[...] = branch_one
    middle = res[...] + mod_row(mod, 2) * branch_one
    mid[...] = middle
    normed, unused = norm_stats(middle)
    h_low[...] = (normed * (1.0 + mod_row(mod, 4)) + mod_row(mod, 3)).astype(bf16)
    pre[...] = nn(h_low[...], upw[...])
    a_low[...] = gelu_parts(pre[...])[0].astype(bf16)
    branch_two = nn(a_low[...], downw[...])
    b2[...] = branch_two
    result = mid[...] + mod_row(mod, 5) * branch_two
    res_next[...] = result
    normed, unused = norm_stats(result)
    hid_next[...] = (normed * (1.0 + mod_row(mod_next, 1)) + mod_row(mod_next, 0)).astype(bf16)


def mlp_bwd_kernel(
    go, mod, pre, mid, b1, b2, att, lse, upw, downw, projw,
    gmid, ga_ext, delta, sums, act_low, gb2_low, h2_low, gp_low, gb1_low,
):
    rows = go.shape[0]
    grad_out = go[...]
    sums[...] = jnp.zeros(sums.shape, f32)
    put_row(sums, 5, jnp.sum(grad_out * b2[...], axis=0, keepdims=True))
    gb2_low[...] = (mod_row(mod, 5) * grad_out).astype(bf16)
    grad_act = nt(gb2_low[...], downw[...])
    act, slope = gelu_parts(pre[...])
    act_low[...] = act.astype(bf16)
    gp_low[...] = (grad_act * slope).astype(bf16)
    grad_hidden = nt(gp_low[...], upw[...])
    normed, inverse = norm_stats(mid[...])
    scale = 1.0 + mod_row(mod, 4)
    h2_low[...] = (normed * scale + mod_row(mod, 3)).astype(bf16)
    put_row(sums, 3, jnp.sum(grad_hidden, axis=0, keepdims=True))
    put_row(sums, 4, jnp.sum(grad_hidden * normed, axis=0, keepdims=True))
    grad_mid = grad_out + norm_back(grad_hidden * scale, normed, inverse)
    gmid[...] = grad_mid
    put_row(sums, 2, jnp.sum(grad_mid * b1[...], axis=0, keepdims=True))
    gb1_low[...] = (mod_row(mod, 2) * grad_mid).astype(bf16)
    grad_att = nt(gb1_low[...], projw[...]).astype(bf16)
    ga_ext[:rows, :] = grad_att
    lane = lax.broadcasted_iota(jnp.int32, (rows, LANES), 1)
    table = jnp.zeros((rows, LANES), f32)
    for h in range(HEADS):
        at = h // 2 * LANES
        prod = grad_att[:, at : at + LANES].astype(f32) * att[:, at : at + LANES]
        total = jnp.sum(half_of(prod, h % 2), axis=1, keepdims=True)
        table = jnp.where(lane == h, total, table)
    delta[...] = table
    both = jnp.where(lane < 8, lse[...], pltpu.roll(table, 8, 1))
    stats = jnp.transpose(both)[:16, :]
    high = stats.astype(bf16)
    low = (stats - high.astype(f32)).astype(bf16)
    ga_ext[rows:, :] = jnp.zeros((32, D), bf16)
    ga_ext[rows : rows + 16, :rows] = high
    ga_ext[rows + 16 : rows + 32, :rows] = low


def mlp_grads_kernel(shift, act_low, gb2_low, h2_low, gp_low, att, gb1_low, sec, sec32):
    lead = jnp.zeros((16, LANES), f32)
    sec32[0:16, :] = lead
    sec32[sec32.shape[0] - 16 :, :] = lead
    start = shift
    proj = tn(att[...].astype(bf16), gb1_low[...])
    for c in range(DB):
        sec32[pl.ds(start + c, D, stride=DB), :] = proj[:, c * LANES : (c + 1) * LANES]
    start += PROJ_LINES
    width = FF // LANES
    for c in range(0, width, 2):
        part = tn(h2_low[...], gp_low[:, c * LANES : (c + 2) * LANES])
        for k in range(2):
            sec32[pl.ds(start + c + k, D, stride=width), :] = part[
                :, k * LANES : (k + 1) * LANES
            ]
    start += FF_LINES
    for r in range(0, FF, D):
        part = tn(act_low[:, r : r + D], gb2_low[...])
        for c in range(DB):
            sec32[pl.ds(start + r * DB + c, D, stride=DB), :] = part[
                :, c * LANES : (c + 1) * LANES
            ]
    narrow_lines(sec32, sec32.shape[0], sec)


def query_bwd_kernel(limits, qkv, ga_ext, lse, delta, gq):
    length = limits[0]
    mine = limits[1]
    rows = lse.shape[0]
    seq_len = qkv.shape[0]
    position = lax.broadcasted_iota(jnp.int32, (1, seq_len), 1)
    bias = jnp.where(position < length, 0.0, NEG_BIG)
    own = pl.ds(pl.multiple_of(mine * rows, rows), rows)
    first = lane_half((rows, LANES))
    lane = lax.broadcasted_iota(jnp.int32, (rows, LANES), 1)

    def column(ref, index):
        return jnp.sum(jnp.where(lane == index, ref[...], 0.0), axis=1, keepdims=True)

    def one_pair(pair, carry):
        at, k_at, v_at = (pl.ds(pl.multiple_of(pair * LANES + i * D, LANES), LANES) for i in range(3))
        query = qkv[own, at] * SCORE_SCALE
        keys = qkv[:, k_at]
        values = qkv[:, v_at]
        grad_pair = ga_ext[:rows, at]
        parts = []
        for half in range(2):
            h = pair * 2 + half
            scores = nt(half_of(query, half), keys) + bias
            prob = jnp.exp(scores - column(lse, h))
            grad_prob = nt(half_of(grad_pair, half), values)
            grad_score = (prob * (grad_prob - column(delta, h))).astype(bf16)
            parts.append(nn(grad_score, keys) * SCORE_SCALE)
        gq[:, at] = jnp.where(first, parts[0], parts[1]).astype(bf16)
        return carry

    lax.fori_loop(0, HEADS // 2, one_pair, 0)


def keys_bwd_kernel(block_count, limits, *refs):
    pieces = refs[:block_count]
    (qkv, gq, res, mod, qkvw, gmid) = refs[block_count : block_count + 6]
    (gqkv, go_prev, sums, stats) = refs[block_count + 6 :]
    length = limits[0]
    mine = limits[1]
    rows = res.shape[0]
    own = pl.ds(pl.multiple_of(mine * rows, rows), rows)
    position = mine * rows + lax.broadcasted_iota(jnp.int32, (rows, 1), 0)
    bias = jnp.where(position < length, 0.0, NEG_BIG)
    first = lane_half((rows, LANES))
    for rel in range(block_count):
        both = pieces[rel][rows : rows + 32, :rows].astype(f32)
        stats[rel] = both[:16, :] + both[16:, :]
    gqkv[:, :D] = gq[...]

    def one_pair(pair, carry):
        at, k_at, v_at = (pl.ds(pl.multiple_of(pair * LANES + i * D, LANES), LANES) for i in range(3))
        keys = qkv[own, k_at] * SCORE_SCALE
        values = qkv[own, v_at]
        key_parts = []
        value_parts = []
        for half in range(2):
            h = pair * 2 + half
            key_half = half_of(keys, half)
            value_half = half_of(values, half)
            key_sum = jnp.zeros((rows, LANES), f32)
            value_sum = jnp.zeros((rows, LANES), f32)
            for rel in range(block_count):
                there = pl.ds(pl.multiple_of((mine ^ rel) * rows, rows), rows)
                query = qkv[there, at]
                grad_pair = pieces[rel][:rows, at]
                scores = nt(key_half, query) + bias
                prob = jnp.exp(scores - stats[rel, pl.ds(h, 1), :])
                grad_prob = nt(value_half, grad_pair)
                grad_score = (prob * (grad_prob - stats[rel, pl.ds(8 + h, 1), :])).astype(bf16)
                key_sum += nn(grad_score, query)
                value_sum += nn(prob.astype(bf16), grad_pair)
            key_parts.append(key_sum * SCORE_SCALE)
            value_parts.append(value_sum)
        gqkv[:, k_at] = jnp.where(first, key_parts[0], key_parts[1]).astype(bf16)
        gqkv[:, v_at] = jnp.where(first, value_parts[0], value_parts[1]).astype(bf16)
        return carry

    lax.fori_loop(0, HEADS // 2, one_pair, 0)
    grad_hidden = nt(gqkv[...], qkvw[...])
    normed, inverse = norm_stats(res[...])
    sums[...] = jnp.zeros(sums.shape, f32)
    put_row(sums, 0, jnp.sum(grad_hidden, axis=0, keepdims=True))
    put_row(sums, 1, jnp.sum(grad_hidden * normed, axis=0, keepdims=True))
    scale = 1.0 + mod_row(mod, 1)
    go_prev[...] = gmid[...] + norm_back(grad_hidden * scale, normed, inverse)


def qkv_grads_kernel(shift, hidden, gqkv, sec, sec32):
    sec32[0:16, :] = jnp.zeros((16, LANES), f32)
    sec32[sec32.shape[0] - 16 :, :] = jnp.zeros((16, LANES), f32)
    width = 3 * DB
    for c in range(0, width, DB):
        part = tn(hidden[...], gqkv[:, c * LANES : (c + DB) * LANES])
        for k in range(DB):
            sec32[pl.ds(shift + c + k, D, stride=width), :] = part[:, k * LANES : (k + 1) * LANES]
    narrow_lines(sec32, sec32.shape[0], sec)


def axis_dims(axis, count):
    dims = []
    for bit in range((count - 1).bit_length()):
        dims.append((axis, [i ^ (1 << bit) for i in range(count)], [i >> bit & 1 for i in range(count)]))
    return dims


def together(values):
    return lax.optimization_barrier(values)


def total_of(parts, begin, end):
    return sum(part[begin:end].astype(f32) for part in parts)


class Cube:
    def __init__(self, var_count, dp_count):
        self.dp_count = dp_count
        self.owners = var_count * dp_count
        var_dims = axis_dims("var", var_count)
        self.core = var_dims[0]
        self.dims = var_dims[1:] + axis_dims("dp", dp_count)

    def partner(self, owner, dim):
        axis, partner, unused = dim
        v, d = divmod(owner, self.dp_count)
        if axis == "var":
            return partner[v] * self.dp_count + d
        return v * self.dp_count + partner[d]

    def bit(self, owner, dim):
        axis, unused, bits = dim
        v, d = divmod(owner, self.dp_count)
        return bits[v] if axis == "var" else bits[d]

    def hop(self, value, *dims, core=None):
        pairs = []
        for owner in range(self.owners):
            other = owner
            for dim in dims:
                other = self.partner(other, dim)
            if core is None or self.bit(owner, self.core) == core:
                pairs.append((owner, other))
        return self.send(value, pairs)

    def send(self, value, pairs):
        return lax.ppermute(value, ("var", "dp"), pairs)

    def mine(self):
        return lax.axis_index("var") * self.dp_count + lax.axis_index("dp")

    def exchange_sum(self, value, groups):
        for group in groups:
            terms = [value]
            for mask in range(1, 2 ** len(group)):
                terms.append(self.hop(value, *[d for i, d in enumerate(group) if mask >> i & 1]))
            while len(terms) > 1:
                terms = [terms[i] + terms[i + 1] for i in range(0, len(terms), 2)]
            value = terms[0]
        return value


PLAN_SHAPE = (4, 8, 1440)
HALF = 720
NEEDED_ZERO = {0: 3, 1: 3, 2: 3, 3: 1, 7: 2, 16: 3, 17: 3, 22: 3, 23: 3}
ENTRIES = (
    [(o, h) for o in (0, 1, 2) for h in (0, 1)]
    + [(3, 0), (7, 1)]
    + [(o, h) for o in range(8, 18) for h in (0, 1)]
    + [(o, h) for o in range(22, 32) for h in (0, 1)]
)


class Plan:
    def __init__(self, cube):
        self.cube = cube
        x, y, step, pair = cube.dims
        self.pair = pair
        self.orders = ((x, y, step), (y, step, x), (step, x, y))
        rows = [self.codes(o) + self.flags(o) for o in range(cube.owners)]
        row = jnp.asarray(rows, jnp.int32)[cube.mine()]
        self.table = row[: len(ENTRIES)]
        self.flag = [row[len(ENTRIES) + i] == 1 for i in range(3)]
        ones = [o for o in range(cube.owners) if cube.bit(o, cube.core)]
        self.ones_pairs = [(o, cube.partner(o, pair)) for o in ones]
        self.zero_pairs = [(o, cube.partner(o, pair)) for o in NEEDED_ZERO]

    def flags(self, device):
        needed = NEEDED_ZERO.get(device, 0)
        return [self.cube.bit(device, self.cube.core), needed & 1, needed >> 1]

    def codes(self, device):
        cube = self.cube
        codes = []
        for owner, half in ENTRIES:
            chunk = 1 + half
            stream = cube.bit(owner, cube.core)
            if stream == 1 and cube.bit(owner, self.pair) == cube.bit(device, self.pair):
                chunk = 0
                stream = 1 - half
            place = 0
            for s, dim in enumerate(self.orders[chunk]):
                place += (cube.bit(owner, dim) ^ cube.bit(device, dim)) << s
            codes.append(chunk * 16 + (stream ^ cube.bit(device, cube.core)) * 8 + place)
        return codes

    def gather(self, shard, shard_zero, early, first_work, late, last_work):
        cube = self.cube
        is_one, own_first, own_second = self.flag
        lower = cube.hop(shard[HALF:], cube.core)
        from_one = cube.send(shard, self.ones_pairs)
        from_zero = cube.send(shard_zero, self.zero_pairs)
        from_one, from_zero, early = together((from_one, from_zero, early))
        first = jnp.where(own_first, shard[:HALF], from_zero[:HALF])
        second = jnp.where(own_second, shard[HALF:], from_zero[HALF:])
        current = [
            jnp.where(is_one, shard[:HALF], lower)[None],
            jnp.where(is_one, from_one[:HALF], first)[None],
            jnp.where(is_one, from_one[HALF:], second)[None],
        ]
        early = first_work(early)
        for step in range(2):
            got = [cube.hop(current[q], self.orders[q][step]) for q in range(3)]
            current = [jnp.concatenate([a, b], axis=0) for a, b in zip(current, got)]
        current, early, late = together((current, early, late))
        last = [cube.hop(current[q], self.orders[q][2]) for q in range(3)]
        other = [cube.hop(value, cube.core) for value in current]
        last, late = together((last, last_work(late)))
        other_last = [cube.hop(value, cube.core) for value in last]
        pieces = [entry for group in zip(current, last, other, other_last) for entry in group]
        return pieces, early, late

    def scatter(self, keep, send, late, work):
        cube = self.cube
        is_one, own_first, own_second = self.flag
        parts = [[a, cube.hop(b, cube.core)] for a, b in zip(keep, send)]
        half = 4
        for step in range(3):
            outs = [total_of(part, half, 2 * half).astype(bf16) for part in parts]
            for q in range(3):
                got = cube.hop(outs[q], self.orders[q][2 - step])
                parts[q] = [part[:half] for part in parts[q]] + [got]
            half //= 2
        first, second, third = (total_of(part, 0, 1)[0] for part in parts)
        both = jnp.concatenate([second, third], axis=0)
        back = [(b, a) for a, b in self.ones_pairs + self.zero_pairs]
        partner = cube.send(both.astype(bf16), back).astype(f32)
        lower = cube.hop(first.astype(bf16), cube.core).astype(f32)
        lower, late = together((lower, late))
        partner, late = together((partner, work(late)))
        one = jnp.concatenate([first, lower], axis=0)
        return jnp.where(is_one, one, both) + partner, late


def flip(value, axis, bit):
    count = lax.axis_size(axis)
    return lax.ppermute(value, axis, [(i, i ^ bit) for i in range(count)])


def gather_blocks(value, extra):
    count = lax.axis_size("var")
    pieces = {0: value}
    bit = count // 2
    while bit:
        got = {r ^ bit: flip(piece, "var", bit) for r, piece in pieces.items()}
        if bit == 2:
            got, extra = together((got, extra))
        pieces.update(got)
        bit //= 2
    return [pieces[r] for r in range(count)], extra


def local(pixels, var_mask, lengths, condition, cotangent, master, moment_one, moment_two):
    var_count = lax.axis_size("var")
    dp_count = lax.axis_size("dp")
    var_index = lax.axis_index("var")
    rows = cotangent.shape[1]
    seq_len = rows * var_count
    local_vars = pixels.shape[0]
    shard_lines = master.shape[0] // LANES
    total_lines = shard_lines * var_count * dp_count

    shard = master.astype(bf16).reshape(shard_lines, LANES)
    present = jnp.where(var_mask == 1, 1.0, 0.0).astype(bf16)
    planes = jnp.concatenate(
        [pixels[:, :, 0, :], jnp.broadcast_to(present[:, None, None], (local_vars, 1, seq_len))],
        axis=1,
    )
    planes = planes.reshape(local_vars, PIX + 1, var_count, rows).transpose(2, 1, 0, 3)

    def spread(values):
        return lax.all_to_all(values, "var", 0, 0, tiled=True)

    cube = Cube(var_count, dp_count)
    planned = (var_count, dp_count, shard_lines) == PLAN_SHAPE
    cond_low = jax.nn.silu(condition.astype(f32)).astype(bf16)
    limits = jnp.stack([lengths[0], var_index.astype(jnp.int32)])
    if planned:
        plan = Plan(cube)
        dp_index = lax.axis_index("dp")
        slots = LAYERS * BIAS_LINES
        x, y, *zs = cube.dims
        every = [[cube.core], [x, y], zs]

        def to_all(value):
            copies = jnp.broadcast_to(value[None], (dp_count,) + value.shape)
            return lax.all_to_all(copies, "dp", 0, 0, tiled=True)

        conds = to_all(cond_low[0].reshape(DB, LANES)).reshape(dp_count, D)
        shard_zero, conds = together((shard, conds))
        of_slot = jnp.arange(dp_count * slots) // slots
        ada_table, partial = run(
            functools.partial(ada_kernel, shard_lines),
            "ada",
            [shape((shard_lines, dp_count * slots), bf16), shape((dp_count * slots, LANES), f32)],
            [
                cube.mine()[None].astype(jnp.int32), shard, conds,
                (jnp.arange(dp_count)[:, None] == of_slot[None, :]).astype(bf16),
                (jnp.arange(dp_count * slots) % slots)[None, :].astype(jnp.int32),
            ],
            [SM] + [VM] * 4,
            [pltpu.VMEM((shard_lines, D), bf16)],
            flops=10**9,
        )
        partial = lax.all_to_all(
            partial.reshape(dp_count, slots, LANES), "dp", 0, 0, tiled=True
        )

        def beside(sums):
            return cube.exchange_sum(sums, [[cube.core], [x]])

        pieces, own, planes = plan.gather(
            shard, shard_zero, jnp.sum(partial, axis=0), beside, planes, spread
        )
        arrays = [plan.table, *pieces]
        specs = [SM] + [VM] * len(pieces)
        mods = [own[layer * BIAS_LINES : (layer + 1) * BIAS_LINES] for layer in range(LAYERS)]
    else:
        planes = spread(planes)
        arrays = [lax.all_gather(shard, ("var", "dp"), axis=0, tiled=True)]
        specs = [VM]
        mods = []
        for layer in range(LAYERS):
            start = HEAD_LINES + layer * LAYER_LINES
            ada = arrays[0][start : start + ADA_LINES].reshape(D, 6 * D)
            bias = arrays[0][start + ADA_LINES : start + ADA_LINES + BIAS_LINES]
            mods.append(
                jnp.dot(cond_low, ada, preferred_element_type=f32).reshape(BIAS_LINES, LANES)
                + bias.astype(f32)
            )
    mods = [jnp.pad(mod, ((0, 24 - BIAS_LINES), (0, 0))) for mod in mods]
    source = Source(arrays, specs, planned)

    begin, end = source.span(0, HEAD_LINES)
    (residual, hidden, agg_low, probs, w, u, e, kvw, aggw, query, pix) = run(
        functools.partial(agg_fwd_kernel, source),
        "agg_fwd",
        [
            shape((rows, D), f32), shape((rows, D), bf16), shape((rows, D), bf16),
            shape((HEADS, VARS, rows), f32), shape((VP, 2 * D), f32), shape((VP, LANES), f32),
            shape((VP, D), bf16), shape((D, 2 * D), bf16), shape((D, D), bf16),
            shape((1, D), f32), shape((PIX, VARS, rows), f32),
        ],
        [*arrays, planes, mods[0]],
        [*specs, VM, VM],
        [
            pltpu.VMEM((end - begin, LANES), f32), pltpu.VMEM((VP, D), f32),
            pltpu.VMEM((VARS, LANES), f32),
        ],
        flops=10**9,
    )

    def unpack_layer(layer):
        start = HEAD_LINES + layer * LAYER_LINES + ADA_LINES + BIAS_LINES
        begin, end = source.span(start, HEAD_LINES + (layer + 1) * LAYER_LINES)
        return run(
            functools.partial(unpack_kernel, source, begin, start),
            f"unpack_{layer}",
            [
                shape((D, 3 * D), bf16), shape((D, D), bf16), shape((D, FF), bf16),
                shape((FF, D), bf16),
            ],
            arrays,
            specs,
            [pltpu.VMEM((end - begin, LANES), f32)],
            flops=10**9,
            vmem=24,
        )

    weights = [None] * LAYERS
    hidden_blocks, weights[0] = gather_blocks(hidden, unpack_layer(0))

    stored = []
    for layer in range(LAYERS):
        qkvw, projw, upw, downw = weights[layer]
        mod = mods[layer]
        mod_next = mods[min(layer + 1, LAYERS - 1)]
        blocks = hidden_blocks
        outs = [
            shape((seq_len, 3 * D), bf16), shape((rows, D), f32), shape((rows, LANES), f32),
            shape((rows, D), f32), shape((rows, D), f32), shape((rows, FF), f32),
            shape((rows, D), f32), shape((rows, D), f32), shape((rows, D), bf16),
        ]
        qkv, att, lse, b1, mid, pre, b2, next_residual, next_hidden = run(
            functools.partial(layer_fwd_kernel, var_count),
            f"layer_fwd_{layer}",
            outs,
            [limits, *blocks, residual, mod, mod_next, qkvw, projw, upw, downw],
            [SM] + [VM] * (var_count + 7),
            [pltpu.VMEM((rows, D), bf16), pltpu.VMEM((rows, FF), bf16)],
            flops=4 * 10**9,
        )
        stored.append((hidden, residual, qkv, att, lse, b1, mid, pre, b2))
        residual, hidden = next_residual, next_hidden
        if layer + 1 < LAYERS:
            hidden_blocks, weights[layer + 1] = gather_blocks(hidden, unpack_layer(layer + 1))
    output = residual

    grad_out = cotangent[0]
    sections = []
    ada_sums = [None] * LAYERS
    for layer in reversed(range(LAYERS)):
        qkvw, projw, upw, downw = weights[layer]
        mod = mods[layer]
        hidden, residual, qkv, att, lse, b1, mid, pre, b2 = stored[layer]
        first_line = HEAD_LINES + layer * LAYER_LINES
        outs = [
            shape((rows, D), f32), shape((rows + 32, D), bf16), shape((rows, LANES), f32),
            shape((24, LANES), f32), shape((rows, FF), bf16), shape((rows, D), bf16),
            shape((rows, D), bf16), shape((rows, FF), bf16), shape((rows, D), bf16),
        ]
        gmid, ga_ext, delta, sums_a, act_low, gb2_low, h2_low, gp_low, gb1_low = run(
            mlp_bwd_kernel,
            f"mlp_bwd_{layer}",
            outs,
            [grad_out, mod, pre, mid, b1, b2, att, lse, upw, downw, projw],
            flops=2 * 10**9,
        )
        (gq,) = run(
            query_bwd_kernel,
            f"query_bwd_{layer}",
            [shape((rows, D), bf16)],
            [limits, qkv, ga_ext, lse, delta],
            [SM] + [VM] * 4,
            flops=4 * 10**9,
        )
        blocks, gq = gather_blocks(ga_ext, gq)
        start = first_line + ADA_LINES + BIAS_LINES + QKV_LINES
        count = up16(start + PROJ_LINES + 2 * FF_LINES) - down16(start)
        (section,) = run(
            functools.partial(mlp_grads_kernel, start - down16(start)),
            f"mlp_grads_{layer}",
            [shape((count, LANES), bf16)],
            [act_low, gb2_low, h2_low, gp_low, att, gb1_low],
            scratch=[pltpu.VMEM((count, LANES), f32)],
            flops=2 * 10**9,
        )
        sections.append((start, PROJ_LINES + 2 * FF_LINES, section))
        gqkv, grad_out, sums_b = run(
            functools.partial(keys_bwd_kernel, var_count),
            f"keys_bwd_{layer}",
            [shape((rows, 3 * D), bf16), shape((rows, D), f32), shape((24, LANES), f32)],
            [limits, *blocks, qkv, gq, residual, mod, qkvw, gmid],
            [SM] + [VM] * (var_count + 6),
            [pltpu.VMEM((var_count, 16, rows), f32)],
            flops=5 * 10**9,
        )
        start = first_line + ADA_LINES + BIAS_LINES
        count = up16(start + QKV_LINES) - down16(start)
        (section,) = run(
            functools.partial(qkv_grads_kernel, start - down16(start)),
            f"qkv_grads_{layer}",
            [shape((count, LANES), bf16)],
            [hidden, gqkv],
            scratch=[pltpu.VMEM((count, LANES), f32)],
            flops=10**9,
        )
        sections.append((start, QKV_LINES, section))
        ada_sums[layer] = (sums_a + sums_b)[:BIAS_LINES]

    pixel_grad, section = run(
        agg_bwd_kernel,
        "agg_bwd",
        [
            shape((var_count, PIX, local_vars, rows), f32),
            shape((up16(HEAD_LINES), LANES), bf16),
        ],
        [grad_out, agg_low, probs, w, u, e, kvw, aggw, query, pix],
        scratch=[
            pltpu.VMEM((up16(HEAD_LINES), LANES), f32), pltpu.VMEM((VP, D), f32),
            pltpu.VMEM((VP, D), f32), pltpu.VMEM((PIX, VARS, rows), f32),
        ],
        flops=10**9,
    )
    sections.append((0, HEAD_LINES, section))
    def unspread(values):
        values = lax.all_to_all(values, "var", 0, 0, tiled=True)
        return values.transpose(2, 1, 0, 3).reshape(local_vars, PIX, seq_len)

    if planned:
        sections.sort(key=lambda entry: entry[0])
        meta = [(down16(start), part.shape[0]) for start, count, part in sections]
        own = cube.exchange_sum(jnp.concatenate(ada_sums, axis=0), [[cube.core], [x]])
        parts, own = together(([s[2] for s in sections], own))
        packed = run(
            functools.partial(pack_kernel, meta),
            "pack",
            [shape((8, HALF, LANES), bf16)] * 6,
            [
                plan.table,
                *parts,
            ],
            [SM] + [VM] * len(sections),
            [pltpu.VMEM((total_lines, LANES), bf16)],
            vmem=16,
        )

        def beside_scatter(values):
            grads, own = values
            return unspread(grads), to_all(own)

        grad_lines, (patch_grads, sums) = plan.scatter(
            packed[::2], packed[1::2], (pixel_grad, own), beside_scatter
        )
        sums = sums.reshape(dp_count * slots, LANES)
        high = sums.astype(bf16)
        low = (sums - high.astype(f32)).astype(bf16)
        ada_lines = nn(ada_table, high) + nn(ada_table, low)
        line = cube.mine() * shard_lines + lax.broadcasted_iota(jnp.int32, (shard_lines, 1), 0)
        for layer in range(LAYERS):
            start = HEAD_LINES + layer * LAYER_LINES
            inside = jnp.logical_and(line >= start, line < start + ADA_LINES + BIAS_LINES)
            grad_lines = jnp.where(inside, ada_lines, grad_lines)
    else:
        patch_grads = unspread(pixel_grad)
        for layer in range(LAYERS):
            start = HEAD_LINES + layer * LAYER_LINES
            outer = cond_low[0].astype(f32)[:, None, None] * ada_sums[layer][None]
            outer = outer.reshape(ADA_LINES, LANES).astype(bf16)
            shift = start - down16(start)
            outer = jnp.concatenate(
                [jnp.zeros((shift, LANES), bf16), outer, ada_sums[layer].astype(bf16)], axis=0
            )
            sections.append((start, ADA_LINES + BIAS_LINES, outer))
        sections.sort(key=lambda entry: entry[0])
        parts = [
            part[start - down16(start) : start - down16(start) + count]
            for start, count, part in sections
        ]
        used = sections[-1][0] + sections[-1][1]
        parts.append(jnp.zeros((total_lines - used, LANES), bf16))
        whole = jnp.concatenate(parts, axis=0)
        grad_lines = lax.psum_scatter(
            whole, ("var", "dp"), scatter_dimension=0, tiled=True
        ).astype(f32)
    grad_shard = grad_lines.reshape(-1)
    squares = jnp.sum(grad_shard * grad_shard)
    if planned:
        squares = cube.exchange_sum(jnp.broadcast_to(squares, (8, LANES)), every)[0, 0]
    else:
        squares = lax.psum(squares, ("var", "dp"))
    grad_norm = jnp.sqrt(squares)
    clip_limit = CLIP_COEF * math.sqrt(PARAMS * seq_len * dp_count)
    clipped = grad_shard * (clip_limit / jnp.maximum(grad_norm, clip_limit))
    new_one = BETA_ONE * moment_one + (1.0 - BETA_ONE) * clipped
    new_two = BETA_TWO * moment_two + (1.0 - BETA_TWO) * clipped * clipped
    ratio = (
        new_one / (1.0 - BETA_ONE**STEP) / (jnp.sqrt(new_two / (1.0 - BETA_TWO**STEP)) + ADAM_EPS)
    )
    new_master = master - LEARN_RATE * (ratio + WEIGHT_DECAY * master)
    return (
        output[None],
        patch_grads[:, :, None, :],
        grad_norm,
        new_master,
        new_one,
        new_two,
        new_master.astype(bf16),
    )


def solution(mesh):
    in_specs = (
        P("var", None, "dp", None),
        P("var"),
        P("dp"),
        P("dp", None),
        P("dp", "var", None),
        P(("var", "dp")),
        P(("var", "dp")),
        P(("var", "dp")),
    )
    out_specs = (
        P("dp", "var", None),
        P("var", None, "dp", None),
        P(),
        P(("var", "dp")),
        P(("var", "dp")),
        P(("var", "dp")),
        P(("var", "dp")),
    )
    return jax.shard_map(local, mesh=mesh, in_specs=in_specs, out_specs=out_specs, check_vma=False)
```

time: 1600 us -> 270 us (0.17); the launches traced: 1570 us -> 265 us
  local copies, waits for them, and re-layouts: 499 us -> 8.89 us
  waiting for transfers between devices: 533 us -> 93.5 us
  matrix products: 332 us -> 0.91 us
  other arithmetic: 124 us -> 13.1 us
  Pallas kernels: 0 us -> 72.5 us
  starting transfers between devices: 1.16 us -> 70.6 us
  blocking collectives: 58.6 us -> 0 us
    unnamed x10 -> x0, waiting for transfers between devices: 372 us -> none
    dot_general x227 -> x2, matrix products: 332 us -> 0.91 us  [nn(): lax.dot_general(left, right, (((1,), (0,)), ((), ())), preferred_element_...]
    unnamed x395 -> x24, local copies, waits for them, and re-layouts: 237 us -> 2.68 us
    all_gather x4 -> x0, waiting for transfers between devices: 131 us -> none  [the longest x1 96 us: local(): lax.all_gather(master.astype(jnp.bfloat16), ('var', 'dp'), axis=0, tiled=...]
    ppermute x0 -> x55, waiting for transfers between devices: none -> 79.6 us  [the longest x43 73.4 us: send(): return lax.ppermute(value, ('var', 'dp'), pairs)]
    pallas_call x0 -> x18, Pallas kernels: none -> 72.5 us  [run(): pl.pallas_call(kernel, name=name, out_shape=outs, in_specs=in_specs, out_...]
    squeeze x54 -> x0, local copies, waits for them, and re-layouts: 55.2 us -> none  [local(): lax.scan(accumulate, jnp.zeros((seq_len, D), jnp.float32), (local_weights...]
    dynamic_update_slice x37 -> x0, local copies, waits for them, and re-layouts: 54.2 us -> none  [the longest x36 54.1 us: local(): lax.scan(embed_one, 0, (patches, embed_weight_local))]
  transfers between devices with their start and end apart: 9 -> 60, of which waited for: 7 -> 39; matrix products, arithmetic and copies ran while one was open for 7% -> 4% of each run, Pallas kernels for 0% -> 10%
where the time goes in v1:
time: 270 us; the launch traced here: 265 us
  waiting for transfers between devices  93.5 us (35%)
  Pallas kernels  72.5 us (27%)
  starting transfers between devices  70.6 us (26%)
  other arithmetic  13.1 us (5%)
  local copies, waits for them, and re-layouts  8.89 us (3%)
  between operations  5.95 us (2%)
    ppermute x43, waiting for transfers between devices, send(): return lax.ppermute(value, ('var', 'dp'), pairs)  73.4 us
    pallas_call x18, Pallas kernels, run(): pl.pallas_call(kernel, name=name, out_shape=outs, in_specs=in_specs, out_...  72.5 us
    ppermute x43, starting transfers between devices, send(): return lax.ppermute(value, ('var', 'dp'), pairs)  39.5 us
    all_to_all x2, starting transfers between devices, to_all(): return lax.all_to_all(copies, 'dp', 0, 0, tiled=True)  12.7 us
    ppermute x12, starting transfers between devices, flip(): return lax.ppermute(value, axis, [(i, i ^ bit) for i in range(count)])  7.88 us
    ppermute x12, waiting for transfers between devices, flip(): return lax.ppermute(value, axis, [(i, i ^ bit) for i in range(count)])  6.28 us
    all_to_all x2, waiting for transfers between devices, to_all(): return lax.all_to_all(copies, 'dp', 0, 0, tiled=True)  5.51 us
  transfers between devices with their start and end apart: 60, of which 39 were waited for; matrix products, arithmetic and copies ran while one was open for 4% of the time, Pallas kernels for 10%

profile of v1, /device:TPU:0, one launch (start us, length us, event | category | flops | bytes accessed | tf_op | source)
XLA Modules:
  0.0 265.4 jit_solution(16759455954906023581)
XLA Ops:
  2.0 7.3 %all-to-all-start = ((bf16[8,3,128]{2,1,0:T(4,128)(2,1)}), bf16[8,3,128]{2,1,0:T(4,128)(2,1)S(1)}, u32[]{:S(2)}, u32[]{:S(2)}) async-start(bf16[8,3,128]{2,1,0:T(4,128)(2,1)} %broadcast_in_dim.66), calls=%async_computation | async-start | bytes 16384 | tf_op jit(solution)/shard_map/all_to_all | solution.py:848
  11.3 4.6 %all-to-all-done = bf16[8,3,128]{2,1,0:T(4,128)(2,1)S(1)} async-done(((bf16[8,3,128]{2,1,0:T(4,128)(2,1)}), bf16[8,3,128]{2,1,0:T(4,128)(2,1)S(1)}, u32[]{:S(2)}, u32[]{:S(2)}) %all-to-all-start) | async-done | bytes 6176 | tf_op jit(solution)/shard_map/all_to_all | solution.py:848
  15.8 2.4 ada.1
  19.9 3.4 %all-to-all-start.1 = ((f32[8,36,128]{2,1,0:T(8,128)}), f32[8,36,128]{2,1,0:T(8,128)S(1)}, u32[]{:S(2)}, u32[]{:S(2)}) async-start(f32[8,36,128]{2,1,0:T(8,128)} %reshape.125), calls=%async_computation.1 | async-start | bytes 327680 | tf_op jit(solution)/shard_map/all_to_all | solution.py:866
  23.3 4.8 %collective-permute-start.4 = (bf16[1440,128]{1,0:T(8,128)(2,1)S(1)}, bf16[1440,128]{1,0:T(8,128)(2,1)S(1)}, u32[]{:S(2)}, u32[]{:S(2)}) collective-permute-start(bf16[1440,128]{1,0:T(8,128)(2,1)S(1)} %convert_bitcast_fusion.shard), channel_id=1, source_target_pairs={{0,4},{1,5},{2,6},{3,7},{7,3},{16,20},{17,21},{22,18},{23,19}} | collective-permute-start | bytes 1105928 | tf_op jit(solution)/shard_map/ppermute | solution.py:688
  33.2 5.4 %collective-permute-start.7 = (bf16[1,720,128]{2,1,0:T(8,128)(2,1)S(1)}, bf16[1,720,128]{2,1,0:T(8,128)(2,1)S(1)}, u32[]{:S(2)}, u32[]{:S(2)}) collective-permute-start(bf16[1,720,128]{2,1,0:T(8,128)(2,1)S(1)} %get-tuple-element.256), channel_id=1, source_target_pairs={{0,2},{1,3},{2,0},{3,1},{4,6},{5,7},{6,4},{7,5},{8,10},{9,11},{10,... | collective-permute-start | bytes 552968 | tf_op jit(solution)/shard_map/ppermute | solution.py:688
  40.2 2.0 collective-permute-done.7
  42.5 2.1 collective-permute-start.10
  44.6 2.1 collective-permute-start.6
  49.1 4.9 %collective-permute-done.10 = f32[36,128]{1,0:T(8,128)S(1)} collective-permute-done((f32[36,128]{1,0:T(8,128)S(1)}, f32[36,128]{1,0:T(8,128)S(1)}, u32[]{:S(2)}, u32[]{:S(2)}) %collective-permute-start.10) | collective-permute-done | bytes 18464 | tf_op jit(solution)/shard_map/ppermute | solution.py:688
  57.6 3.6 %all-to-all-start.2 = ((bf16[4,5,18,256]{3,2,1,0:T(8,128)(2,1)}), bf16[4,5,18,256]{3,2,1,0:T(8,128)(2,1)S(1)}, u32[]{:S(2)}, u32[]{:S(2)}) async-start(bf16[4,5,18,256]{3,2,1,0:T(8,128)(2,1)} %maximum_bitcast_fusion), calls=%async_computation.2 | async-start | bytes 491520 | tf_op jit(solution)/shard_map/all_to_all | solution.py:833
  61.8 9.1 %collective-permute-done.11.refs_2_ = bf16[4,720,128]{2,1,0:T(8,128)(2,1)S(1)} collective-permute-done((bf16[4,720,128]{2,1,0:T(8,128)(2,1)S(1)}, bf16[4,720,128]{2,1,0:T(8,128)(2,1)S(1)}, u32[]{:S(2)}, u32[]{:S(2)}) %collective-permute-start.11) | collective-permute-done | bytes 737312 | tf_op jit(solution)/shard_map/ppermute | solution.py:688
  70.8 3.4 %all-to-all-done.2.refs_13_ = bf16[4,5,18,256]{3,2,1,0:T(8,128)(2,1)S(1)} async-done(((bf16[4,5,18,256]{3,2,1,0:T(8,128)(2,1)}), bf16[4,5,18,256]{3,2,1,0:T(8,128)(2,1)S(1)}, u32[]{:S(2)}, u32[]{:S(2)}) %all-to-all-start.2) | async-done | bytes 184352 | tf_op jit(solution)/shard_map/all_to_all | solution.py:833
  75.0 1.9 collective-permute-done.15.refs_4_
  78.8 6.5 %agg_fwd.1 = (f32[256,384]{1,0:T(8,128)S(1)}, bf16[256,384]{1,0:T(8,128)(2,1)S(1)}, bf16[256,384]{1,0:T(8,128)(2,1)S(1)}, f32[6,72,256]{2,1,0:T(8,128)S(1)}, f32...) custom-call(s32[48]{0:T(128)S(1)} %slice_bitcast_fusion.2.refs_0_.ta, ...), custom_call_target="tpu_custom_call" | custom-call | flops 1000000000 | bytes 12707520 | tf_op jit(solution)/shard_map/agg_fwd/pallas_call | solution.py:88
  85.3 1.8 collective-permute-start.21
  87.1 4.7 %unpack_0.1 = (bf16[384,1152]{1,0:T(8,128)(2,1)S(1)}, bf16[384,384]{1,0:T(8,128)(2,1)S(1)}, bf16[384,1536]{1,0:T(8,128)(2,1)S(1)}, bf16[1536,384]{1,0:T(8,128)(2,1)S(1)}) custom-call(s32[48]{0:T(128)S(1)} %slice_bitcast_fusion.2.refs_0_.table, bf16[4,720,128]{2,1,0:T(8,128)(2,1)S(1)} %pad_maximum_fusion.refs_1_, ...), custom_call_target="tpu_custom_call" | custom-call | flops 1000000000 | bytes 12386496 | tf_op jit(solution)/shard_map/unpack_0/pallas_call | solution.py:88
  93.7 7.8 %layer_fwd_0.1 = (bf16[1024,1152]{1,0:T(8,128)(2,1)S(1)}, f32[256,384]{1,0:T(8,128)S(1)}, f32[256,128]{1,0:T(8,128)S(1)}, f32[256,384]{1,0:T(8,128)S(1)}, f32[25...) custom-call(s32[2]{0:T(128)S(1)} %pad_add_fusion.limits, ...), custom_call_target="tpu_custom_call" | custom-call | flops 4000000000 | bytes 10969096 | tf_op jit(solution)/shard_map/layer_fwd_0/pallas_call | solution.py:88
  101.6 1.8 collective-permute-start.24
  103.4 4.7 %unpack_1.1 = (bf16[384,1152]{1,0:T(8,128)(2,1)S(1)}, bf16[384,384]{1,0:T(8,128)(2,1)S(1)}, bf16[384,1536]{1,0:T(8,128)(2,1)S(1)}, bf16[1536,384]{1,0:T(8,128)(2,1)S(1)}) custom-call(s32[48]{0:T(128)S(1)} %slice_bitcast_fusion.2.refs_0_.table, bf16[4,720,128]{2,1,0:T(8,128)(2,1)S(1)} %pad_maximum_fusion.refs_1_, ...), custom_call_target="tpu_custom_call" | custom-call | flops 1000000000 | bytes 12386496 | tf_op jit(solution)/shard_map/unpack_1/pallas_call | solution.py:88
  110.0 8.8 %layer_fwd_1.1 = (bf16[1024,1152]{1,0:T(8,128)(2,1)S(1)}, f32[256,384]{1,0:T(8,128)S(1)}, f32[256,128]{1,0:T(8,128)S(1)}, f32[256,384]{1,0:T(8,128)S(1)}, f32[25...) custom-call(s32[2]{0:T(128)S(1)} %pad_add_fusion.limits, ...), custom_call_target="tpu_custom_call" | custom-call | flops 4000000000 | bytes 10969096 | tf_op jit(solution)/shard_map/layer_fwd_1/pallas_call | solution.py:88
  118.8 2.3 mlp_bwd_1.1
  121.1 1.8 collective-permute-start.27
  122.9 3.7 %query_bwd_1.1.refs_5_ = bf16[256,384]{1,0:T(8,128)(2,1)S(1)} custom-call(s32[2]{0:T(128)S(1)} %pad_add_fusion.limits, bf16[1024,1152]{1,0:T(8,128)(2,1)S(1)} %get-tuple-element.162.qkv.refs_4_, bf16[288,384]{1,0:T(8,128)(2,1)S(1)} %get-tuple-element.161.ga_ext.refs_0_, f32[256,128]{1,0:T(8,128)S(1)} %get-tuple-element.160.lse, ...), custom_call_target="tpu_custom_call" | custom-call | flops 4000000000 | bytes 3039240 | tf_op jit(solution)/shard_map/query_bwd_1/pallas_call | solution.py:88
  126.6 2.0 collective-permute-done.27.refs_2_
  130.1 6.5 %keys_bwd_1.1 = (bf16[256,1152]{1,0:T(8,128)(2,1)S(1)}, f32[256,384]{1,0:T(8,128)S(1)}, f32[24,128]{1,0:T(8,128)S(1)}) custom-call(s32[2]{0:T(128)S(1)} %pad_add_fusion.limits, bf16[288,384]{1,0:T(8,128)(2,1)S(1)} %get-tuple-element.161.ga_ext.refs_0_, bf16[288,384]{1,0:T(8,128)(2,1)S(1)} %collective-permute-done.26.refs_1_, ...), custom_call_target="tpu_custom_call" | custom-call | flops 5000000000 | bytes 6119432 | tf_op jit(solution)/shard_map/keys_bwd_1/pallas_call | solution.py:88
  136.6 2.4 mlp_bwd_0.1
  139.0 1.8 collective-permute-start.30
  140.9 4.2 %query_bwd_0.1.refs_5_ = bf16[256,384]{1,0:T(8,128)(2,1)S(1)} custom-call(s32[2]{0:T(128)S(1)} %pad_add_fusion.limits, bf16[1024,1152]{1,0:T(8,128)(2,1)S(1)} %get-tuple-element.175.qkv.refs_4_, bf16[288,384]{1,0:T(8,128)(2,1)S(1)} %get-tuple-element.174.ga_ext.refs_0_, f32[256,128]{1,0:T(8,128)S(1)} %get-tuple-element.173.lse, ...), custom_call_target="tpu_custom_call" | custom-call | flops 4000000000 | bytes 3039240 | tf_op jit(solution)/shard_map/query_bwd_0/pallas_call | solution.py:88
  148.7 6.5 %keys_bwd_0.1 = (bf16[256,1152]{1,0:T(8,128)(2,1)S(1)}, f32[256,384]{1,0:T(8,128)S(1)}, f32[24,128]{1,0:T(8,128)S(1)}) custom-call(s32[2]{0:T(128)S(1)} %pad_add_fusion.limits, bf16[288,384]{1,0:T(8,128)(2,1)S(1)} %get-tuple-element.174.ga_ext.refs_0_, bf16[288,384]{1,0:T(8,128)(2,1)S(1)} %collective-permute-done.29.refs_1_, ...), custom_call_target="tpu_custom_call" | custom-call | flops 5000000000 | bytes 6119432 | tf_op jit(solution)/shard_map/keys_bwd_0/pallas_call | solution.py:88
  157.9 3.5 %agg_bwd.1 = (f32[4,4,18,256]{3,2,1,0:T(8,128)S(1)}, bf16[4336,128]{1,0:T(8,128)(2,1)S(1)}) custom-call(f32[256,384]{1,0:T(8,128)S(1)} %get-tuple-element.180.go, bf16[256,384]{1,0:T(8,128)(2,1)S(1)} %get-tuple-element.181.agg_low, f32[6,72,256]{2,1,0:T(8,128)S(1)} %get-tuple-element.182.probs, f32[288,768]{1,0:T(8,128)S(1)} %get-tuple-element.183.w, ...), custom_call_target="tpu_custom_call" | custom-call | flops 1000000000 | bytes 4871680 | tf_op jit(solution)/shard_map/agg_bwd/pallas_call | solution.py:88
  161.4 4.6 %pack.1 = (bf16[8,720,128]{2,1,0:T(8,128)(2,1)S(1)}, bf16[8,720,128]{2,1,0:T(8,128)(2,1)S(1)}, bf16[8,720,128]{2,1,0:T(8,128)(2,1)S(1)}, bf16[8,720,128]{2,1,0:T...) custom-call(s32[48]{0:T(128)S(1)} %slice_bitcast_fusion.2.refs_0_.table, ...), custom_call_target="tpu_custom_call" | custom-call | bytes 17051840 | tf_op jit(solution)/shard_map/pack/pallas_call | solution.py:88
  166.7 2.7 %collective-permute-done.43 = bf16[8,720,128]{2,1,0:T(8,128)(2,1)S(1)} collective-permute-done((bf16[8,720,128]{2,1,0:T(8,128)(2,1)S(1)}, bf16[8,720,128]{2,1,0:T(8,128)(2,1)S(1)}, u32[]{:S(2)}, u32[]{:S(2)}) %collective-permute-start.43) | collective-permute-done | bytes 1474592 | tf_op jit(solution)/shard_map/ppermute | solution.py:688
  173.9 14.2 %collective-permute-done.44 = bf16[4,720,128]{2,1,0:T(8,128)(2,1)S(1)} collective-permute-done((bf16[4,720,128]{2,1,0:T(8,128)(2,1)S(1)}, bf16[4,720,128]{2,1,0:T(8,128)(2,1)S(1)}, u32[]{:S(2)}, u32[]{:S(2)}) %collective-permute-start.44) | collective-permute-done | bytes 737312 | tf_op jit(solution)/shard_map/ppermute | solution.py:688
  188.5 1.8 collective-permute-done.35
  194.1 6.2 %collective-permute-done.45 = bf16[2,720,128]{2,1,0:T(8,128)(2,1)S(1)} collective-permute-done((bf16[2,720,128]{2,1,0:T(8,128)(2,1)S(1)}, bf16[2,720,128]{2,1,0:T(8,128)(2,1)S(1)}, u32[]{:S(2)}, u32[]{:S(2)}) %collective-permute-start.45) | collective-permute-done | bytes 368672 | tf_op jit(solution)/shard_map/ppermute | solution.py:688
  203.8 2.6 collective-permute-done.46
  210.2 3.6 %all-to-all-start.3 = ((f32[4,4,18,256]{3,1,2,0:T(4,128)}), f32[4,4,18,256]{3,1,2,0:T(4,128)S(1)}, u32[]{:S(2)}, u32[]{:S(2)}) async-start(f32[4,4,18,256]{3,1,2,0:T(4,128)} %copy.24), calls=%async_computation.3 | async-start | bytes 589824 | tf_op jit(solution)/shard_map/all_to_all | solution.py:1038
  215.4 4.9 %all-to-all-done.3 = f32[4,4,18,256]{3,1,2,0:T(4,128)S(1)} async-done(((f32[4,4,18,256]{3,1,2,0:T(4,128)}), f32[4,4,18,256]{3,1,2,0:T(4,128)S(1)}, u32[]{:S(2)}, u32[]{:S(2)}) %all-to-all-start.3) | async-done | bytes 294944 | tf_op jit(solution)/shard_map/all_to_all | solution.py:1038
  220.9 5.4 %all-to-all-start.4 = ((f32[8,36,128]{2,1,0:T(8,128)}), f32[8,36,128]{2,1,0:T(8,128)S(1)}, u32[]{:S(2)}, u32[]{:S(2)}) async-start(f32[8,36,128]{2,1,0:T(8,128)} %broadcast_in_dim.74), calls=%async_computation.4 | async-start | bytes 327680 | tf_op jit(solution)/shard_map/all_to_all | solution.py:848
  226.3 11.3 %collective-permute-done.42 = bf16[1440,128]{1,0:T(8,128)(2,1)S(1)} collective-permute-done((bf16[1440,128]{1,0:T(8,128)(2,1)S(1)}, bf16[1440,128]{1,0:T(8,128)(2,1)S(1)}, u32[]{:S(2)}, u32[]{:S(2)}) %collective-permute-start.42) | collective-permute-done | bytes 368672 | tf_op jit(solution)/shard_map/ppermute | solution.py:688
  241.0 1.9 multiply_reduce_fusion
  246.6 2.4 collective-permute-start.51
  249.2 1.9 collective-permute-done.51
  251.9 2.3 collective-permute-start.53
  254.1 2.1 collective-permute-start.54
  257.3 2.3 collective-permute-done.54
  260.8 3.2 %fusion.17 = (bf16[184320]{0:T(1024)(128)(2,1)}, f32[184320]{0:T(1024)}, f32[184320]{0:T(1024)}, f32[184320]{0:T(1024)}) fusion(f32[184320]{0:T(1024)S(1)} %copy-done.4, f32[1440,128]{1,0:T(8,128)S(1)} %get-tuple-element.253, f32[]{:T(128)S(6)} %div.28, f32[184320]{0:T(1024)} %param.15, f32[184320]{0:T(1024)} %param.16), kind=kLoop, calls=%fused_computation.71 | loop fusion | flops 2949120 | bytes 5529604 | tf_op jit(solution)/shard_map/convert_element_type | solution.py:1119
  (179 shorter events, 58.6 us)
Async XLA Ops:
  2.0 13.8 %all-to-all-start = ((bf16[8,3,128]{2,1,0:T(4,128)(2,1)}), bf16[8,3,128]{2,1,0:T(4,128)(2,1)S(1)}, u32[]{:S(2)}, u32[]{:S(2)}) async-start(bf16[8,3,128]{2,1,0:T(4,128)(2,1)} %broadcast_in_dim.66), calls=%async_computation | async-start | bytes 16384 | tf_op jit(solution)/shard_map/all_to_all | solution.py:848
  10.5 21.0 %collective-permute-start.3 = (bf16[1440,128]{1,0:T(8,128)(2,1)S(1)}, bf16[1440,128]{1,0:T(8,128)(2,1)S(1)}, u32[]{:S(2)}, u32[]{:S(2)}) collective-permute-start(bf16[1440,128]{1,0:T(8,128)(2,1)S(1)} %convert_bitcast_fusion.shard), channel_id=1, source_target_pairs={{8,12},{9,13},{10,14},{11,15},{12,8},{13,9},{14,10},{15,11},{24,28... | collective-permute-start | bytes 1105928 | tf_op jit(solution)/shard_map/ppermute | solution.py:688
  19.9 11.5 %all-to-all-start.1 = ((f32[8,36,128]{2,1,0:T(8,128)}), f32[8,36,128]{2,1,0:T(8,128)S(1)}, u32[]{:S(2)}, u32[]{:S(2)}) async-start(f32[8,36,128]{2,1,0:T(8,128)} %reshape.125), calls=%async_computation.1 | async-start | bytes 327680 | tf_op jit(solution)/shard_map/all_to_all | solution.py:866
  23.3 9.8 %collective-permute-start.4 = (bf16[1440,128]{1,0:T(8,128)(2,1)S(1)}, bf16[1440,128]{1,0:T(8,128)(2,1)S(1)}, u32[]{:S(2)}, u32[]{:S(2)}) collective-permute-start(bf16[1440,128]{1,0:T(8,128)(2,1)S(1)} %convert_bitcast_fusion.shard), channel_id=1, source_target_pairs={{0,4},{1,5},{2,6},{3,7},{7,3},{16,20},{17,21},{22,18},{23,19}} | collective-permute-start | bytes 1105928 | tf_op jit(solution)/shard_map/ppermute | solution.py:688
  28.1 5.0 %collective-permute-start = (bf16[720,128]{1,0:T(8,128)(2,1)S(1)}, bf16[720,128]{1,0:T(8,128)(2,1)S(1)}, u32[]{:S(2)}, u32[]{:S(2)}) collective-permute-start(bf16[720,128]{1,0:T(8,128)(2,1)S(1)} %slice_bitcast_fusion), channel_id=1, source_target_pairs={{0,8},{1,9},{2,10},{3,11},{4,12},{5,13},{6,14},{7,15},{8,0},{9,1},... | collective-permute-start | bytes 552968 | tf_op jit(solution)/shard_map/ppermute | solution.py:688
  33.2 9.0 %collective-permute-start.7 = (bf16[1,720,128]{2,1,0:T(8,128)(2,1)S(1)}, bf16[1,720,128]{2,1,0:T(8,128)(2,1)S(1)}, u32[]{:S(2)}, u32[]{:S(2)}) collective-permute-start(bf16[1,720,128]{2,1,0:T(8,128)(2,1)S(1)} %get-tuple-element.256), channel_id=1, source_target_pairs={{0,2},{1,3},{2,0},{3,1},{4,6},{5,7},{6,4},{7,5},{8,10},{9,11},{10,... | collective-permute-start | bytes 552968 | tf_op jit(solution)/shard_map/ppermute | solution.py:688
  38.7 5.9 %collective-permute-start.5 = (bf16[1,720,128]{2,1,0:T(8,128)(2,1)S(1)}, bf16[1,720,128]{2,1,0:T(8,128)(2,1)S(1)}, u32[]{:S(2)}, u32[]{:S(2)}) collective-permute-start(bf16[1,720,128]{2,1,0:T(8,128)(2,1)S(1)} %get-tuple-element.257), channel_id=1, source_target_pairs={{0,1},{1,0},{2,3},{3,2},{4,5},{5,4},{6,7},{7,6},{8,9},{9,8},{10,11... | collective-permute-start | bytes 552968 | tf_op jit(solution)/shard_map/ppermute | solution.py:688
  40.2 7.5 %collective-permute-start.1 = (bf16[1,720,128]{2,1,0:T(8,128)(2,1)S(1)}, bf16[1,720,128]{2,1,0:T(8,128)(2,1)S(1)}, u32[]{:S(2)}, u32[]{:S(2)}) collective-permute-start(bf16[1,720,128]{2,1,0:T(8,128)(2,1)S(1)} %get-tuple-element.258), channel_id=1, source_target_pairs={{0,16},{1,17},{2,18},{3,19},{4,20},{5,21},{6,22},{7,23},{8,24},{9,... | collective-permute-start | bytes 552968 | tf_op jit(solution)/shard_map/ppermute | solution.py:688
  42.2 11.8 %collective-permute-start.8 = (bf16[2,720,128]{2,1,0:T(8,128)(2,1)S(1)}, bf16[2,720,128]{2,1,0:T(8,128)(2,1)S(1)}, u32[]{:S(2)}, u32[]{:S(2)}) collective-permute-start(bf16[2,720,128]{2,1,0:T(8,128)(2,1)S(1)} %pad_maximum_fusion.6), channel_id=1, source_target_pairs={{0,16},{1,17},{2,18},{3,19},{4,20},{5,21},{6,22},{7,23},{8,24},{9,... | collective-permute-start | bytes 1105928 | tf_op jit(solution)/shard_map/ppermute | solution.py:688
  42.5 11.5 %collective-permute-start.10 = (f32[36,128]{1,0:T(8,128)S(1)}, f32[36,128]{1,0:T(8,128)S(1)}, u32[]{:S(2)}, u32[]{:S(2)}) collective-permute-start(f32[36,128]{1,0:T(8,128)S(1)} %add.200), channel_id=1, source_target_pairs={{0,16},{1,17},{2,18},{3,19},{4,20},{5,21},{6,22},{7,23},{8,24},{9,... | collective-permute-start | bytes 55304 | tf_op jit(solution)/shard_map/ppermute | solution.py:688
  44.6 9.5 %collective-permute-start.6 = (bf16[2,720,128]{2,1,0:T(8,128)(2,1)S(1)}, bf16[2,720,128]{2,1,0:T(8,128)(2,1)S(1)}, u32[]{:S(2)}, u32[]{:S(2)}) collective-permute-start(bf16[2,720,128]{2,1,0:T(8,128)(2,1)S(1)} %pad_maximum_fusion.5), channel_id=1, source_target_pairs={{0,2},{1,3},{2,0},{3,1},{4,6},{5,7},{6,4},{7,5},{8,10},{9,11},{10,... | collective-permute-start | bytes 1105928 | tf_op jit(solution)/shard_map/ppermute | solution.py:688
  47.7 7.6 %collective-permute-start.2 = (bf16[2,720,128]{2,1,0:T(8,128)(2,1)S(1)}, bf16[2,720,128]{2,1,0:T(8,128)(2,1)S(1)}, u32[]{:S(2)}, u32[]{:S(2)}) collective-permute-start(bf16[2,720,128]{2,1,0:T(8,128)(2,1)S(1)} %pad_maximum_fusion.4), channel_id=1, source_target_pairs={{0,1},{1,0},{2,3},{3,2},{4,5},{5,4},{6,7},{7,6},{8,9},{9,8},{10,11... | collective-permute-start | bytes 1105928 | tf_op jit(solution)/shard_map/ppermute | solution.py:688
  55.4 15.4 %collective-permute-start.11 = (bf16[4,720,128]{2,1,0:T(8,128)(2,1)S(1)}, bf16[4,720,128]{2,1,0:T(8,128)(2,1)S(1)}, u32[]{:S(2)}, u32[]{:S(2)}) collective-permute-start(bf16[4,720,128]{2,1,0:T(8,128)(2,1)S(1)} %pad_maximum_fusion.refs_1_), channel_id=1, source_target_pairs={{0,2},{1,3},{2,0},{3,1},{4,6},{5,7},{6,4},{7,5},{8,10},{9,11},{10,... | collective-permute-start | bytes 2211848 | tf_op jit(solution)/shard_map/ppermute | solution.py:688
  55.9 18.4 %collective-permute-start.12 = (bf16[4,720,128]{2,1,0:T(8,128)(2,1)S(1)}, bf16[4,720,128]{2,1,0:T(8,128)(2,1)}, u32[]{:S(2)}, u32[]{:S(2)}) collective-permute-start(bf16[4,720,128]{2,1,0:T(8,128)(2,1)S(1)} %pad_maximum_fusion.1.refs_5_), channel_id=1, source_target_pairs={{0,16},{1,17},{2,18},{3,19},{4,20},{5,21},{6,22},{7,23},{8,24},{9,... | collective-permute-start | bytes 2211848 | tf_op jit(solution)/shard_map/ppermute | solution.py:688
  57.1 17.1 %collective-permute-start.13 = (bf16[4,720,128]{2,1,0:T(8,128)(2,1)S(1)}, bf16[4,720,128]{2,1,0:T(8,128)(2,1)}, u32[]{:S(2)}, u32[]{:S(2)}) collective-permute-start(bf16[4,720,128]{2,1,0:T(8,128)(2,1)S(1)} %pad_maximum_fusion.2.refs_9_), channel_id=1, source_target_pairs={{0,1},{1,0},{2,3},{3,2},{4,5},{5,4},{6,7},{7,6},{8,9},{9,8},{10,11... | collective-permute-start | bytes 2211848 | tf_op jit(solution)/shard_map/ppermute | solution.py:688
  57.6 17.2 %collective-permute-start.14 = (bf16[4,720,128]{2,1,0:T(8,128)(2,1)S(1)}, bf16[4,720,128]{2,1,0:T(8,128)(2,1)}, u32[]{:S(2)}, u32[]{:S(2)}) collective-permute-start(bf16[4,720,128]{2,1,0:T(8,128)(2,1)S(1)} %pad_maximum_fusion.refs_1_), channel_id=1, source_target_pairs={{0,8},{1,9},{2,10},{3,11},{4,12},{5,13},{6,14},{7,15},{8,0},{9,1},... | collective-permute-start | bytes 2211848 | tf_op jit(solution)/shard_map/ppermute | solution.py:688
  57.6 16.6 %all-to-all-start.2 = ((bf16[4,5,18,256]{3,2,1,0:T(8,128)(2,1)}), bf16[4,5,18,256]{3,2,1,0:T(8,128)(2,1)S(1)}, u32[]{:S(2)}, u32[]{:S(2)}) async-start(bf16[4,5,18,256]{3,2,1,0:T(8,128)(2,1)} %maximum_bitcast_fusion), calls=%async_computation.2 | async-start | bytes 491520 | tf_op jit(solution)/shard_map/all_to_all | solution.py:833
  61.2 13.7 %collective-permute-start.16 = (bf16[4,720,128]{2,1,0:T(8,128)(2,1)S(1)}, bf16[4,720,128]{2,1,0:T(8,128)(2,1)}, u32[]{:S(2)}, u32[]{:S(2)}) collective-permute-start(bf16[4,720,128]{2,1,0:T(8,128)(2,1)S(1)} %pad_maximum_fusion.1.refs_5_), channel_id=1, source_target_pairs={{0,8},{1,9},{2,10},{3,11},{4,12},{5,13},{6,14},{7,15},{8,0},{9,1},... | collective-permute-start | bytes 2211848 | tf_op jit(solution)/shard_map/ppermute | solution.py:688
  70.8 4.1 %collective-permute-start.18 = (bf16[4,720,128]{2,1,0:T(8,128)(2,1)S(1)}, bf16[4,720,128]{2,1,0:T(8,128)(2,1)}, u32[]{:S(2)}, u32[]{:S(2)}) collective-permute-start(bf16[4,720,128]{2,1,0:T(8,128)(2,1)S(1)} %pad_maximum_fusion.2.refs_9_), channel_id=1, source_target_pairs={{0,8},{1,9},{2,10},{3,11},{4,12},{5,13},{6,14},{7,15},{8,0},{9,1},... | collective-permute-start | bytes 2211848 | tf_op jit(solution)/shard_map/ppermute | solution.py:688
  74.8 4.0 %collective-permute-start.19 = (bf16[4,720,128]{2,1,0:T(8,128)(2,1)}, bf16[4,720,128]{2,1,0:T(8,128)(2,1)S(1)}, u32[]{:S(2)}, u32[]{:S(2)}) collective-permute-start(bf16[4,720,128]{2,1,0:T(8,128)(2,1)} %collective-permute-done.13.refs_10_), channel_id=1, source_target_pairs={{0,8},{1,9},{2,10},{3,11},{4,12},{5,13},{6,14},{7,15},{8,0},{9,1},... | collective-permute-start | bytes 2211848 | tf_op jit(solution)/shard_map/ppermute | solution.py:688
  85.3 7.0 %collective-permute-start.21 = (bf16[256,384]{1,0:T(8,128)(2,1)S(1)}, bf16[256,384]{1,0:T(8,128)(2,1)S(1)}, u32[]{:S(2)}, u32[]{:S(2)}) collective-permute-start(bf16[256,384]{1,0:T(8,128)(2,1)S(1)} %get-tuple-element.132.refs_0_.hidden), channel_id=1, source_target_pairs={{0,16},{8,24},{16,0},{24,8},{1,17},{9,25},{17,1},{25,9},{2,18},{10... | collective-permute-start | bytes 589832 | tf_op jit(solution)/shard_map/ppermute | solution.py:798
  87.1 6.0 %collective-permute-start.20 = (bf16[256,384]{1,0:T(8,128)(2,1)S(1)}, bf16[256,384]{1,0:T(8,128)(2,1)S(1)}, u32[]{:S(2)}, u32[]{:S(2)}) collective-permute-start(bf16[256,384]{1,0:T(8,128)(2,1)S(1)} %get-tuple-element.132.refs_0_.hidden), channel_id=1, source_target_pairs={{0,8},{8,0},{16,24},{24,16},{1,9},{9,1},{17,25},{25,17},{2,10},{10... | collective-permute-start | bytes 589832 | tf_op jit(solution)/shard_map/ppermute | solution.py:798
  101.6 7.0 %collective-permute-start.24 = (bf16[256,384]{1,0:T(8,128)(2,1)S(1)}, bf16[256,384]{1,0:T(8,128)(2,1)S(1)}, u32[]{:S(2)}, u32[]{:S(2)}) collective-permute-start(bf16[256,384]{1,0:T(8,128)(2,1)S(1)} %get-tuple-element.143.refs_0_.hidden), channel_id=1, source_target_pairs={{0,16},{8,24},{16,0},{24,8},{1,17},{9,25},{17,1},{25,9},{2,18},{10... | collective-permute-start | bytes 589832 | tf_op jit(solution)/shard_map/ppermute | solution.py:798
  121.1 7.5 %collective-permute-start.27 = (bf16[288,384]{1,0:T(8,128)(2,1)S(1)}, bf16[288,384]{1,0:T(8,128)(2,1)S(1)}, u32[]{:S(2)}, u32[]{:S(2)}) collective-permute-start(bf16[288,384]{1,0:T(8,128)(2,1)S(1)} %get-tuple-element.161.ga_ext.refs_0_), channel_id=1, source_target_pairs={{0,16},{8,24},{16,0},{24,8},{1,17},{9,25},{17,1},{25,9},{2,18},{10... | collective-permute-start | bytes 663560 | tf_op jit(solution)/shard_map/ppermute | solution.py:798
  122.9 7.1 %collective-permute-start.26 = (bf16[288,384]{1,0:T(8,128)(2,1)S(1)}, bf16[288,384]{1,0:T(8,128)(2,1)S(1)}, u32[]{:S(2)}, u32[]{:S(2)}) collective-permute-start(bf16[288,384]{1,0:T(8,128)(2,1)S(1)} %get-tuple-element.161.ga_ext.refs_0_), channel_id=1, source_target_pairs={{0,8},{8,0},{16,24},{24,16},{1,9},{9,1},{17,25},{25,17},{2,10},{10... | collective-permute-start | bytes 663560 | tf_op jit(solution)/shard_map/ppermute | solution.py:798
  139.0 8.2 %collective-permute-start.30 = (bf16[288,384]{1,0:T(8,128)(2,1)S(1)}, bf16[288,384]{1,0:T(8,128)(2,1)S(1)}, u32[]{:S(2)}, u32[]{:S(2)}) collective-permute-start(bf16[288,384]{1,0:T(8,128)(2,1)S(1)} %get-tuple-element.174.ga_ext.refs_0_), channel_id=1, source_target_pairs={{0,16},{8,24},{16,0},{24,8},{1,17},{9,25},{17,1},{25,9},{2,18},{10... | collective-permute-start | bytes 663560 | tf_op jit(solution)/shard_map/ppermute | solution.py:798
  140.8 6.8 %collective-permute-start.29 = (bf16[288,384]{1,0:T(8,128)(2,1)S(1)}, bf16[288,384]{1,0:T(8,128)(2,1)S(1)}, u32[]{:S(2)}, u32[]{:S(2)}) collective-permute-start(bf16[288,384]{1,0:T(8,128)(2,1)S(1)} %get-tuple-element.174.ga_ext.refs_0_), channel_id=1, source_target_pairs={{0,8},{8,0},{16,24},{24,16},{1,9},{9,1},{17,25},{25,17},{2,10},{10... | collective-permute-start | bytes 663560 | tf_op jit(solution)/shard_map/ppermute | solution.py:798
  156.5 4.9 %collective-permute-start.33 = (f32[36,128]{1,0:T(8,128)S(1)}, f32[36,128]{1,0:T(8,128)S(1)}, u32[]{:S(2)}, u32[]{:S(2)}) collective-permute-start(f32[36,128]{1,0:T(8,128)S(1)} %fusion.23), channel_id=1, source_target_pairs={{0,16},{1,17},{2,18},{3,19},{4,20},{5,21},{6,22},{7,23},{8,24},{9,... | collective-permute-start | bytes 55304 | tf_op jit(solution)/shard_map/ppermute | solution.py:688
  166.1 5.4 %collective-permute-start.34 = (bf16[8,720,128]{2,1,0:T(8,128)(2,1)S(1)}, bf16[8,720,128]{2,1,0:T(8,128)(2,1)S(1)}, u32[]{:S(2)}, u32[]{:S(2)}) collective-permute-start(bf16[8,720,128]{2,1,0:T(8,128)(2,1)S(1)} %get-tuple-element.213), channel_id=1, source_target_pairs={{0,8},{1,9},{2,10},{3,11},{4,12},{5,13},{6,14},{7,15},{8,0},{9,1},... | collective-permute-start | bytes 4423688 | tf_op jit(solution)/shard_map/ppermute | solution.py:688
  166.6 7.0 %collective-permute-start.38 = (bf16[8,720,128]{2,1,0:T(8,128)(2,1)S(1)}, bf16[8,720,128]{2,1,0:T(8,128)(2,1)S(1)}, u32[]{:S(2)}, u32[]{:S(2)}) collective-permute-start(bf16[8,720,128]{2,1,0:T(8,128)(2,1)S(1)} %get-tuple-element.215), channel_id=1, source_target_pairs={{0,8},{1,9},{2,10},{3,11},{4,12},{5,13},{6,14},{7,15},{8,0},{9,1},... | collective-permute-start | bytes 4423688 | tf_op jit(solution)/shard_map/ppermute | solution.py:688
  169.6 18.6 %collective-permute-start.44 = (bf16[4,720,128]{2,1,0:T(8,128)(2,1)S(1)}, bf16[4,720,128]{2,1,0:T(8,128)(2,1)S(1)}, u32[]{:S(2)}, u32[]{:S(2)}) collective-permute-start(bf16[4,720,128]{2,1,0:T(8,128)(2,1)S(1)} %add_convert_fusion), channel_id=1, source_target_pairs={{0,2},{1,3},{2,0},{3,1},{4,6},{5,7},{6,4},{7,5},{8,10},{9,11},{10,... | collective-permute-start | bytes 2211848 | tf_op jit(solution)/shard_map/ppermute | solution.py:688
  171.7 18.6 %collective-permute-start.35 = (bf16[4,720,128]{2,1,0:T(8,128)(2,1)S(1)}, bf16[4,720,128]{2,1,0:T(8,128)(2,1)S(1)}, u32[]{:S(2)}, u32[]{:S(2)}) collective-permute-start(bf16[4,720,128]{2,1,0:T(8,128)(2,1)S(1)} %add_convert_fusion.2), channel_id=1, source_target_pairs={{0,16},{1,17},{2,18},{3,19},{4,20},{5,21},{6,22},{7,23},{8,24},{9,... | collective-permute-start | bytes 2211848 | tf_op jit(solution)/shard_map/ppermute | solution.py:688
  173.8 19.4 %collective-permute-start.39 = (bf16[4,720,128]{2,1,0:T(8,128)(2,1)S(1)}, bf16[4,720,128]{2,1,0:T(8,128)(2,1)S(1)}, u32[]{:S(2)}, u32[]{:S(2)}) collective-permute-start(bf16[4,720,128]{2,1,0:T(8,128)(2,1)S(1)} %add_convert_fusion.1), channel_id=1, source_target_pairs={{0,1},{1,0},{2,3},{3,2},{4,5},{5,4},{6,7},{7,6},{8,9},{9,8},{10,11... | collective-permute-start | bytes 2211848 | tf_op jit(solution)/shard_map/ppermute | solution.py:688
  188.3 12.0 %collective-permute-start.45 = (bf16[2,720,128]{2,1,0:T(8,128)(2,1)S(1)}, bf16[2,720,128]{2,1,0:T(8,128)(2,1)S(1)}, u32[]{:S(2)}, u32[]{:S(2)}) collective-permute-start(bf16[2,720,128]{2,1,0:T(8,128)(2,1)S(1)} %add_convert_fusion.3), channel_id=1, source_target_pairs={{0,1},{1,0},{2,3},{3,2},{4,5},{5,4},{6,7},{7,6},{8,9},{9,8},{10,11... | collective-permute-start | bytes 1105928 | tf_op jit(solution)/shard_map/ppermute | solution.py:688
  190.4 10.7 %collective-permute-start.36 = (bf16[2,720,128]{2,1,0:T(8,128)(2,1)S(1)}, bf16[2,720,128]{2,1,0:T(8,128)(2,1)S(1)}, u32[]{:S(2)}, u32[]{:S(2)}) collective-permute-start(bf16[2,720,128]{2,1,0:T(8,128)(2,1)S(1)} %add_convert_fusion.5), channel_id=1, source_target_pairs={{0,2},{1,3},{2,0},{3,1},{4,6},{5,7},{6,4},{7,5},{8,10},{9,11},{10,... | collective-permute-start | bytes 1105928 | tf_op jit(solution)/shard_map/ppermute | solution.py:688
  193.3 9.1 %collective-permute-start.40 = (bf16[2,720,128]{2,1,0:T(8,128)(2,1)S(1)}, bf16[2,720,128]{2,1,0:T(8,128)(2,1)S(1)}, u32[]{:S(2)}, u32[]{:S(2)}) collective-permute-start(bf16[2,720,128]{2,1,0:T(8,128)(2,1)S(1)} %add_convert_fusion.4), channel_id=1, source_target_pairs={{0,16},{1,17},{2,18},{3,19},{4,20},{5,21},{6,22},{7,23},{8,24},{9,... | collective-permute-start | bytes 1105928 | tf_op jit(solution)/shard_map/ppermute | solution.py:688
  200.4 6.0 %collective-permute-start.46 = (bf16[1,720,128]{2,1,0:T(8,128)(2,1)S(1)}, bf16[1,720,128]{2,1,0:T(8,128)(2,1)S(1)}, u32[]{:S(2)}, u32[]{:S(2)}) collective-permute-start(bf16[1,720,128]{2,1,0:T(8,128)(2,1)S(1)} %add_convert_fusion.6), channel_id=1, source_target_pairs={{0,16},{1,17},{2,18},{3,19},{4,20},{5,21},{6,22},{7,23},{8,24},{9,... | collective-permute-start | bytes 552968 | tf_op jit(solution)/shard_map/ppermute | solution.py:688
  201.2 6.0 %collective-permute-start.37 = (bf16[1,720,128]{2,1,0:T(8,128)(2,1)S(1)}, bf16[1,720,128]{2,1,0:T(8,128)(2,1)S(1)}, u32[]{:S(2)}, u32[]{:S(2)}) collective-permute-start(bf16[1,720,128]{2,1,0:T(8,128)(2,1)S(1)} %add_convert_fusion.8), channel_id=1, source_target_pairs={{0,1},{1,0},{2,3},{3,2},{4,5},{5,4},{6,7},{7,6},{8,9},{9,8},{10,11... | collective-permute-start | bytes 552968 | tf_op jit(solution)/shard_map/ppermute | solution.py:688
  202.5 5.6 %collective-permute-start.41 = (bf16[1,720,128]{2,1,0:T(8,128)(2,1)S(1)}, bf16[1,720,128]{2,1,0:T(8,128)(2,1)S(1)}, u32[]{:S(2)}, u32[]{:S(2)}) collective-permute-start(bf16[1,720,128]{2,1,0:T(8,128)(2,1)S(1)} %add_convert_fusion.7), channel_id=1, source_target_pairs={{0,2},{1,3},{2,0},{3,1},{4,6},{5,7},{6,4},{7,5},{8,10},{9,11},{10,... | collective-permute-start | bytes 552968 | tf_op jit(solution)/shard_map/ppermute | solution.py:688
  210.2 10.0 %all-to-all-start.3 = ((f32[4,4,18,256]{3,1,2,0:T(4,128)}), f32[4,4,18,256]{3,1,2,0:T(4,128)S(1)}, u32[]{:S(2)}, u32[]{:S(2)}) async-start(f32[4,4,18,256]{3,1,2,0:T(4,128)} %copy.24), calls=%async_computation.3 | async-start | bytes 589824 | tf_op jit(solution)/shard_map/all_to_all | solution.py:1038
  213.9 23.7 %collective-permute-start.42 = (bf16[1440,128]{1,0:T(8,128)(2,1)S(1)}, bf16[1440,128]{1,0:T(8,128)(2,1)S(1)}, u32[]{:S(2)}, u32[]{:S(2)}) collective-permute-start(bf16[1440,128]{1,0:T(8,128)(2,1)S(1)} %fusion.2), channel_id=1, source_target_pairs={{12,8},{13,9},{14,10},{15,11},{8,12},{9,13},{10,14},{11,15},{28,24... | collective-permute-start | bytes 1105928 | tf_op jit(solution)/shard_map/ppermute | solution.py:688
  220.9 18.5 %all-to-all-start.4 = ((f32[8,36,128]{2,1,0:T(8,128)}), f32[8,36,128]{2,1,0:T(8,128)S(1)}, u32[]{:S(2)}, u32[]{:S(2)}) async-start(f32[8,36,128]{2,1,0:T(8,128)} %broadcast_in_dim.74), calls=%async_computation.4 | async-start | bytes 327680 | tf_op jit(solution)/shard_map/all_to_all | solution.py:848
  245.4 3.7 %collective-permute-start.49 = (f32[8,128]{1,0:T(8,128)S(1)}, f32[8,128]{1,0:T(8,128)S(1)}, u32[]{:S(2)}, u32[]{:S(2)}) collective-permute-start(f32[8,128]{1,0:T(8,128)S(1)} %broadcast_add_fusion), channel_id=1, source_target_pairs={{0,16},{1,17},{2,18},{3,19},{4,20},{5,21},{6,22},{7,23},{8,24},{9,... | collective-permute-start | bytes 12296 | tf_op jit(solution)/shard_map/ppermute | solution.py:688
  245.5 3.7 %collective-permute-start.50 = (f32[8,128]{1,0:T(8,128)S(1)}, f32[8,128]{1,0:T(8,128)S(1)}, u32[]{:S(2)}, u32[]{:S(2)}) collective-permute-start(f32[8,128]{1,0:T(8,128)S(1)} %broadcast_add_fusion), channel_id=1, source_target_pairs={{0,1},{1,0},{2,3},{3,2},{4,5},{5,4},{6,7},{7,6},{8,9},{9,8},{10,11... | collective-permute-start | bytes 12296 | tf_op jit(solution)/shard_map/ppermute | solution.py:688
  246.6 4.5 %collective-permute-start.51 = (f32[8,128]{1,0:T(8,128)S(1)}, f32[8,128]{1,0:T(8,128)S(1)}, u32[]{:S(2)}, u32[]{:S(2)}) collective-permute-start(f32[8,128]{1,0:T(8,128)S(1)} %broadcast_add_fusion), channel_id=1, source_target_pairs={{0,17},{1,16},{2,19},{3,18},{4,21},{5,20},{6,23},{7,22},{8,25},{9,... | collective-permute-start | bytes 12296 | tf_op jit(solution)/shard_map/ppermute | solution.py:688
  251.8 5.5 %collective-permute-start.52 = (f32[8,128]{1,0:T(8,128)S(1)}, f32[8,128]{1,0:T(8,128)S(1)}, u32[]{:S(2)}, u32[]{:S(2)}) collective-permute-start(f32[8,128]{1,0:T(8,128)S(1)} %add_add_fusion.1), channel_id=1, source_target_pairs={{0,2},{1,3},{2,0},{3,1},{4,6},{5,7},{6,4},{7,5},{8,10},{9,11},{10,... | collective-permute-start | bytes 12296 | tf_op jit(solution)/shard_map/ppermute | solution.py:688
  251.9 5.4 %collective-permute-start.53 = (f32[8,128]{1,0:T(8,128)S(1)}, f32[8,128]{1,0:T(8,128)S(1)}, u32[]{:S(2)}, u32[]{:S(2)}) collective-permute-start(f32[8,128]{1,0:T(8,128)S(1)} %add_add_fusion.1), channel_id=1, source_target_pairs={{0,4},{1,5},{2,6},{3,7},{4,0},{5,1},{6,2},{7,3},{8,12},{9,13},{10,... | collective-permute-start | bytes 12296 | tf_op jit(solution)/shard_map/ppermute | solution.py:688
  254.1 5.4 %collective-permute-start.54 = (f32[8,128]{1,0:T(8,128)S(1)}, f32[8,128]{1,0:T(8,128)S(1)}, u32[]{:S(2)}, u32[]{:S(2)}) collective-permute-start(f32[8,128]{1,0:T(8,128)S(1)} %add_add_fusion.1), channel_id=1, source_target_pairs={{0,6},{1,7},{2,4},{3,5},{4,2},{5,3},{6,0},{7,1},{8,14},{9,15},{10,... | collective-permute-start | bytes 12296 | tf_op jit(solution)/shard_map/ppermute | solution.py:688
  (23 other events, 155.1 us)

commit v2 on v1

--- a/solution.py
+++ b/solution.py
@@ -75,12 +75,28 @@
     )
 
 
+VMEM_MIB = {
+    "ada": 14,
+    "agg_fwd": 14,
+    "unpack": 14,
+    "near_attend": 16,
+    "layer_fwd": 24,
+    "mlp_bwd": 16,
+    "query_bwd": 16,
+    "mlp_grads": 12,
+    "near_keys": 16,
+    "keys_bwd": 16,
+    "qkv_grads": 10,
+    "agg_bwd": 14,
+    "pack": 16,
+}
+
 VM = pl.BlockSpec(memory_space=pltpu.VMEM)
 SM = pl.BlockSpec(memory_space=pltpu.SMEM)
 ANY = pl.BlockSpec(memory_space=pl.ANY)
 
 
-def run(kernel, name, outs, ins, in_specs=None, scratch=(), flops=0, out_specs=None, vmem=32):
+def run(kernel, name, outs, ins, in_specs=None, scratch=(), flops=0, out_specs=None):
     if in_specs is None:
         in_specs = [VM] * len(ins)
     nbytes = sum(math.prod(o.shape) * o.dtype.itemsize for o in outs)
@@ -93,7 +109,7 @@
         out_specs=out_specs or [VM] * len(outs),
         scratch_shapes=list(scratch),
         cost_estimate=pl.CostEstimate(flops=flops, bytes_accessed=nbytes, transcendentals=0),
-        compiler_params=pltpu.CompilerParams(vmem_limit_bytes=vmem * 2**20),
+        compiler_params=pltpu.CompilerParams(vmem_limit_bytes=VMEM_MIB[name.rstrip("_0123456789")] * 2**20),
     )(*ins)
 
 
@@ -242,9 +258,12 @@
     sections = refs[: len(meta)]
     targets = refs[len(meta) : len(meta) + 6]
     lines = refs[len(meta) + 6]
+    starts = [o * 2 * HALF + h * HALF for o, h in ENTRIES]
     end = 0
     tile = None
     for i, (base, size) in enumerate(meta):
+        entry = max(e for e, start in enumerate(starts) if start <= base)
+        base = base - starts[entry] + entry * HALF
         if base > end:
             lines[end:base, :] = jnp.zeros((base - end, LANES), bf16)
         copy_lines(sections[i], 0, size, lines, base)
@@ -254,13 +273,9 @@
         end = base + size
     lines[end:, :] = jnp.zeros((lines.shape[0] - end, LANES), bf16)
 
-    def first_line(index):
-        number = jnp.where(index < 7, index, jnp.where(index < 28, index + 8, index + 16))
-        return number * HALF
-
     def body(index, carry):
         code = table[index]
-        at = pl.multiple_of(first_line(index), 16)
+        at = pl.multiple_of(index * HALF, 16)
         for k, target in enumerate(targets):
 
             @pl.when(code // 8 == k)
@@ -418,40 +433,87 @@
     return value * half, slope
 
 
-def layer_fwd_kernel(
-    block_count, limits, *refs
-):
-    hidden = refs[:block_count]
-    (res, mod, mod_next, qkvw, projw, upw, downw) = refs[block_count : block_count + 7]
-    (qkv, att, lse, b1, mid, pre, b2, res_next, hid_next, h_low, a_low) = refs[block_count + 7 :]
-    length = limits[0]
+def pair_columns(pair):
+    return [pl.ds(pl.multiple_of(pair * LANES + i * D, LANES), LANES) for i in range(3)]
+
+
+def key_bias(rels, limits, rows):
+    parts = []
+    for rel in rels:
+        position = (limits[1] ^ rel) * rows + lax.broadcasted_iota(jnp.int32, (1, rows), 1)
+        parts.append(jnp.where(position < limits[0], 0.0, NEG_BIG))
+    return jnp.concatenate(parts, axis=1)
+
+
+def near_attend_kernel(rels, limits, *refs):
+    hidden = refs[: len(rels)]
+    qkvw, qkv, acc, peak, total = refs[len(rels) :]
+    rows = acc.shape[0]
+    for i in range(len(rels)):
+        qkv[i * rows : (i + 1) * rows, :] = nn(hidden[i][...], qkvw[...]).astype(bf16)
+    bias = key_bias(rels, limits, rows)
+    first = lane_half((rows, LANES))
+    lane = lax.broadcasted_iota(jnp.int32, (rows, LANES), 1)
+    peak[...] = jnp.zeros((rows, LANES), f32)
+    total[...] = jnp.zeros((rows, LANES), f32)
+
+    def attend(pair, carry):
+        at, k_at, v_at = pair_columns(pair)
+        query = qkv[:rows, at] * SCORE_SCALE
+        parts = []
+        for half in range(2):
+            scores = nt(half_of(query, half), qkv[:, k_at]) + bias
+            highest = jnp.max(scores, axis=1, keepdims=True)
+            exponent = jnp.exp(scores - highest)
+            parts.append(nn(exponent.astype(bf16), qkv[:, v_at]))
+            here = lane == pair * 2 + half
+            peak[...] = jnp.where(here, highest, peak[...])
+            total[...] = jnp.where(here, jnp.sum(exponent, axis=1, keepdims=True), total[...])
+        acc[:, at] = jnp.where(first, parts[0], parts[1])
+        return carry
+
+    lax.fori_loop(0, HEADS // 2, attend, 0)
+
+
+def layer_fwd_kernel(near, far, limits, *refs):
+    hidden = refs[: len(far)]
+    (qkv_near, acc, peak, near_total, res, mod, mod_next, qkvw, projw, upw, downw) = refs[
+        len(far) : len(far) + 11
+    ]
+    (qkv, att, lse, b1, mid, pre, b2, res_next, hid_next, h_low, a_low, qkv_far) = refs[
+        len(far) + 11 :
+    ]
     mine = limits[1]
     rows = res.shape[0]
-    seq_len = block_count * rows
-    for rel in range(block_count):
+    for i, rel in enumerate(near):
         at = pl.multiple_of((mine ^ rel) * rows, rows)
-        qkv[pl.ds(at, rows), :] = nn(hidden[rel][...], qkvw[...]).astype(bf16)
-    position = lax.broadcasted_iota(jnp.int32, (1, seq_len), 1)
-    bias = jnp.where(position < length, 0.0, NEG_BIG)
-    own = pl.ds(pl.multiple_of(mine * rows, rows), rows)
+        qkv[pl.ds(at, rows), :] = qkv_near[i * rows : (i + 1) * rows, :]
+    for i, rel in enumerate(far):
+        at = pl.multiple_of((mine ^ rel) * rows, rows)
+        block = nn(hidden[i][...], qkvw[...]).astype(bf16)
+        qkv_far[i * rows : (i + 1) * rows, :] = block
+        qkv[pl.ds(at, rows), :] = block
+    bias = key_bias(far, limits, rows)
     first = lane_half((rows, LANES))
     lane = lax.broadcasted_iota(jnp.int32, (rows, LANES), 1)
     lse[...] = jnp.zeros((rows, LANES), f32)
 
     def attend(pair, carry):
-        at, k_at, v_at = (pl.ds(pl.multiple_of(pair * LANES + i * D, LANES), LANES) for i in range(3))
-        query = qkv[own, at] * SCORE_SCALE
-        keys = qkv[:, k_at]
-        values = qkv[:, v_at]
+        at, k_at, v_at = pair_columns(pair)
+        query = qkv_near[:rows, at] * SCORE_SCALE
         parts = []
         for half in range(2):
-            scores = nt(half_of(query, half), keys) + bias
-            highest = jnp.max(scores, axis=1, keepdims=True)
+            here = lane == pair * 2 + half
+            before = jnp.sum(jnp.where(here, peak[...], 0.0), axis=1, keepdims=True)
+            total = jnp.sum(jnp.where(here, near_total[...], 0.0), axis=1, keepdims=True)
+            scores = nt(half_of(query, half), qkv_far[:, k_at]) + bias
+            highest = jnp.maximum(before, jnp.max(scores, axis=1, keepdims=True))
             exponent = jnp.exp(scores - highest)
-            total = jnp.sum(exponent, axis=1, keepdims=True)
-            prob = (exponent * (1.0 / total)).astype(bf16)
-            parts.append(nn(prob, values))
-            lse[...] = jnp.where(lane == pair * 2 + half, highest + jnp.log(total), lse[...])
+            factor = jnp.exp(before - highest)
+            total = total * factor + jnp.sum(exponent, axis=1, keepdims=True)
+            weighted = acc[:, at] * factor + nn(exponent.astype(bf16), qkv_far[:, v_at])
+            parts.append(weighted * (1.0 / total))
+            lse[...] = jnp.where(here, highest + jnp.log(total), lse[...])
         att[:, at] = jnp.where(first, parts[0], parts[1])
         return carry
 
@@ -574,21 +636,13 @@
     lax.fori_loop(0, HEADS // 2, one_pair, 0)
 
 
-def keys_bwd_kernel(block_count, limits, *refs):
-    pieces = refs[:block_count]
-    (qkv, gq, res, mod, qkvw, gmid) = refs[block_count : block_count + 6]
-    (gqkv, go_prev, sums, stats) = refs[block_count + 6 :]
-    length = limits[0]
+def keys_sums(rels, pieces, limits, qkv, stats, rows, store):
     mine = limits[1]
-    rows = res.shape[0]
     own = pl.ds(pl.multiple_of(mine * rows, rows), rows)
-    position = mine * rows + lax.broadcasted_iota(jnp.int32, (rows, 1), 0)
-    bias = jnp.where(position < length, 0.0, NEG_BIG)
     first = lane_half((rows, LANES))
-    for rel in range(block_count):
-        both = pieces[rel][rows : rows + 32, :rows].astype(f32)
-        stats[rel] = both[:16, :] + both[16:, :]
-    gqkv[:, :D] = gq[...]
+    for i in range(len(rels)):
+        both = pieces[i][rows : rows + 32, :rows].astype(f32)
+        stats[i] = both[:16, :] + both[16:, :]
 
     def one_pair(pair, carry):
         at, k_at, v_at = (pl.ds(pl.multiple_of(pair * LANES + i * D, LANES), LANES) for i in range(3))
@@ -602,23 +656,53 @@
             value_half = half_of(values, half)
             key_sum = jnp.zeros((rows, LANES), f32)
             value_sum = jnp.zeros((rows, LANES), f32)
-            for rel in range(block_count):
+            for i, rel in enumerate(rels):
                 there = pl.ds(pl.multiple_of((mine ^ rel) * rows, rows), rows)
                 query = qkv[there, at]
-                grad_pair = pieces[rel][:rows, at]
-                scores = nt(key_half, query) + bias
-                prob = jnp.exp(scores - stats[rel, pl.ds(h, 1), :])
+                grad_pair = pieces[i][:rows, at]
+                prob = jnp.exp(nt(key_half, query) - stats[i, pl.ds(h, 1), :])
                 grad_prob = nt(value_half, grad_pair)
-                grad_score = (prob * (grad_prob - stats[rel, pl.ds(8 + h, 1), :])).astype(bf16)
+                grad_score = (prob * (grad_prob - stats[i, pl.ds(8 + h, 1), :])).astype(bf16)
                 key_sum += nn(grad_score, query)
                 value_sum += nn(prob.astype(bf16), grad_pair)
             key_parts.append(key_sum * SCORE_SCALE)
             value_parts.append(value_sum)
-        gqkv[:, k_at] = jnp.where(first, key_parts[0], key_parts[1]).astype(bf16)
-        gqkv[:, v_at] = jnp.where(first, value_parts[0], value_parts[1]).astype(bf16)
+        store(
+            at,
+            jnp.where(first, key_parts[0], key_parts[1]),
+            jnp.where(first, value_parts[0], value_parts[1]),
+        )
         return carry
 
     lax.fori_loop(0, HEADS // 2, one_pair, 0)
+
+
+def near_keys_kernel(rels, limits, *refs):
+    pieces = refs[: len(rels)]
+    qkv, key_out, value_out, stats = refs[len(rels) :]
+
+    def store(at, key_sum, value_sum):
+        key_out[:, at] = key_sum
+        value_out[:, at] = value_sum
+
+    keys_sums(rels, pieces, limits, qkv, stats, key_out.shape[0], store)
+
+
+def keys_bwd_kernel(rels, limits, *refs):
+    pieces = refs[: len(rels)]
+    (qkv, gq, key_near, value_near, res, mod, qkvw, gmid) = refs[len(rels) : len(rels) + 8]
+    (gqkv, go_prev, sums, stats) = refs[len(rels) + 8 :]
+    rows = res.shape[0]
+    position = limits[1] * rows + lax.broadcasted_iota(jnp.int32, (rows, 1), 0)
+    live = position < limits[0]
+    gqkv[:, :D] = gq[...]
+
+    def store(at, key_sum, value_sum):
+        k_at, v_at = (pl.ds(pl.multiple_of(at.start + i * D, LANES), LANES) for i in (1, 2))
+        gqkv[:, k_at] = jnp.where(live, key_near[:, at] + key_sum, 0.0).astype(bf16)
+        gqkv[:, v_at] = jnp.where(live, value_near[:, at] + value_sum, 0.0).astype(bf16)
+
+    keys_sums(rels, pieces, limits, qkv, stats, rows, store)
     grad_hidden = nt(gqkv[...], qkvw[...])
     normed, inverse = norm_stats(res[...])
     sums[...] = jnp.zeros(sums.shape, f32)
@@ -717,11 +801,17 @@
         self.cube = cube
         x, y, step, pair = cube.dims
         self.pair = pair
-        self.orders = ((x, y, step), (y, step, x), (step, x, y))
-        rows = [self.codes(o) + self.flags(o) for o in range(cube.owners)]
+        self.orders = ((y, x, step), (step, y, x), (step, x, y))
+        self.back_orders = ((y, x, step), (x, step, y), (step, y, x))
+        back = [order[::-1] for order in self.back_orders]
+        rows = [
+            self.codes(o, self.orders) + self.codes(o, back) + self.flags(o)
+            for o in range(cube.owners)
+        ]
         row = jnp.asarray(rows, jnp.int32)[cube.mine()]
         self.table = row[: len(ENTRIES)]
-        self.flag = [row[len(ENTRIES) + i] == 1 for i in range(3)]
+        self.back_table = row[len(ENTRIES) : 2 * len(ENTRIES)]
+        self.flag = [row[2 * len(ENTRIES) + i] == 1 for i in range(3)]
         ones = [o for o in range(cube.owners) if cube.bit(o, cube.core)]
         self.ones_pairs = [(o, cube.partner(o, pair)) for o in ones]
         self.zero_pairs = [(o, cube.partner(o, pair)) for o in NEEDED_ZERO]
@@ -730,7 +820,7 @@
         needed = NEEDED_ZERO.get(device, 0)
         return [self.cube.bit(device, self.cube.core), needed & 1, needed >> 1]
 
-    def codes(self, device):
+    def codes(self, device, orders):
         cube = self.cube
         codes = []
         for owner, half in ENTRIES:
@@ -740,36 +830,49 @@
                 chunk = 0
                 stream = 1 - half
             place = 0
-            for s, dim in enumerate(self.orders[chunk]):
+            for s, dim in enumerate(orders[chunk]):
                 place += (cube.bit(owner, dim) ^ cube.bit(device, dim)) << s
             codes.append(chunk * 16 + (stream ^ cube.bit(device, cube.core)) * 8 + place)
         return codes
 
-    def gather(self, shard, shard_zero, early, first_work, late, last_work):
+    def gather(self, shard, early, sums, first_work, second_work):
         cube = self.cube
         is_one, own_first, own_second = self.flag
+
+        def hop(chunk, step):
+            return cube.hop(current[chunk], self.orders[chunk][step])
+
+        def grow(chunk, got):
+            current[chunk] = jnp.concatenate([current[chunk], got], axis=0)
+
         lower = cube.hop(shard[HALF:], cube.core)
         from_one = cube.send(shard, self.ones_pairs)
-        from_zero = cube.send(shard_zero, self.zero_pairs)
-        from_one, from_zero, early = together((from_one, from_zero, early))
+        from_zero = cube.send(shard, self.zero_pairs)
+        current = [jnp.where(is_one, shard[:HALF], lower)[None], None, None]
+        grow(0, hop(0, 0))
+        from_one, from_zero, current[0], early, sums = together(
+            (from_one, from_zero, current[0], early, sums)
+        )
         first = jnp.where(own_first, shard[:HALF], from_zero[:HALF])
         second = jnp.where(own_second, shard[HALF:], from_zero[HALF:])
-        current = [
-            jnp.where(is_one, shard[:HALF], lower)[None],
-            jnp.where(is_one, from_one[:HALF], first)[None],
-            jnp.where(is_one, from_one[HALF:], second)[None],
-        ]
-        early = first_work(early)
-        for step in range(2):
-            got = [cube.hop(current[q], self.orders[q][step]) for q in range(3)]
-            current = [jnp.concatenate([a, b], axis=0) for a, b in zip(current, got)]
-        current, early, late = together((current, early, late))
-        last = [cube.hop(current[q], self.orders[q][2]) for q in range(3)]
+        current[1] = jnp.where(is_one, from_one[:HALF], first)[None]
+        current[2] = jnp.where(is_one, from_one[HALF:], second)[None]
+        sums = first_work(sums)
+        got = [hop(0, 1), hop(1, 0), hop(2, 0)]
+        for chunk in range(3):
+            grow(chunk, got[chunk])
+        current, sums = together((current, sums))
+        done = second_work(sums)
+        last = [hop(0, 2), None, None]
+        got = [hop(1, 1), hop(2, 1)]
+        for chunk in range(2):
+            grow(chunk + 1, got[chunk])
+        current[1], current[2], done = together((current[1], current[2], done))
+        last[1], last[2] = hop(1, 2), hop(2, 2)
         other = [cube.hop(value, cube.core) for value in current]
-        last, late = together((last, last_work(late)))
         other_last = [cube.hop(value, cube.core) for value in last]
         pieces = [entry for group in zip(current, last, other, other_last) for entry in group]
-        return pieces, early, late
+        return pieces, early, done
 
     def scatter(self, keep, send, late, work):
         cube = self.cube
@@ -779,18 +882,22 @@
         for step in range(3):
             outs = [total_of(part, half, 2 * half).astype(bf16) for part in parts]
             for q in range(3):
-                got = cube.hop(outs[q], self.orders[q][2 - step])
+                got = cube.hop(outs[q], self.back_orders[q][step])
                 parts[q] = [part[:half] for part in parts[q]] + [got]
             half //= 2
         first, second, third = (total_of(part, 0, 1)[0] for part in parts)
-        both = jnp.concatenate([second, third], axis=0)
         back = [(b, a) for a, b in self.ones_pairs + self.zero_pairs]
-        partner = cube.send(both.astype(bf16), back).astype(f32)
-        lower = cube.hop(first.astype(bf16), cube.core).astype(f32)
-        lower, late = together((lower, late))
-        partner, late = together((partner, work(late)))
-        one = jnp.concatenate([first, lower], axis=0)
-        return jnp.where(is_one, one, both) + partner, late
+        low = [second.astype(bf16), third.astype(bf16), first.astype(bf16)]
+        low[1], low[2] = together((low[1], low[2]))
+        partner = [cube.send(part, back).astype(f32) for part in low[:2]]
+        lower, late = together((cube.hop(low[2], cube.core), late))
+        lower = lower.astype(f32)
+        partner[1], late = together((partner[1], work(late)))
+        halves = [
+            jnp.where(is_one, first, second) + partner[0],
+            jnp.where(is_one, lower, third) + partner[1],
+        ]
+        return jnp.concatenate(halves, axis=0), late
 
 
 def flip(value, axis, bit):
@@ -798,17 +905,23 @@
     return lax.ppermute(value, axis, [(i, i ^ bit) for i in range(count)])
 
 
-def gather_blocks(value, extra):
+NEAR = (0, 1)
+
+
+def gather_blocks(value, work):
     count = lax.axis_size("var")
-    pieces = {0: value}
+    pieces = {0: value, 1: flip(value, "var", 1)}
+    done = work([pieces[r] for r in NEAR])
     bit = count // 2
-    while bit:
-        got = {r ^ bit: flip(piece, "var", bit) for r, piece in pieces.items()}
+    while bit > 1:
+        got = {r ^ bit: flip(piece, "var", bit) for r, piece in pieces.items() if r % 2 == 0}
         if bit == 2:
-            got, extra = together((got, extra))
+            got, done = together((got, done))
         pieces.update(got)
         bit //= 2
-    return [pieces[r] for r in range(count)], extra
+    for r in range(2, count, 2):
+        pieces[r + 1] = flip(pieces[r], "var", 1)
+    return [pieces[r] for r in range(count)], done
 
 
 def local(pixels, var_mask, lengths, condition, cotangent, master, moment_one, moment_two):
@@ -840,15 +953,13 @@
         plan = Plan(cube)
         dp_index = lax.axis_index("dp")
         slots = LAYERS * BIAS_LINES
-        x, y, *zs = cube.dims
-        every = [[cube.core], [x, y], zs]
+        x = cube.dims[0]
 
         def to_all(value):
             copies = jnp.broadcast_to(value[None], (dp_count,) + value.shape)
             return lax.all_to_all(copies, "dp", 0, 0, tiled=True)
 
         conds = to_all(cond_low[0].reshape(DB, LANES)).reshape(dp_count, D)
-        shard_zero, conds = together((shard, conds))
         of_slot = jnp.arange(dp_count * slots) // slots
         ada_table, partial = run(
             functools.partial(ada_kernel, shard_lines),
@@ -863,16 +974,14 @@
             [pltpu.VMEM((shard_lines, D), bf16)],
             flops=10**9,
         )
-        partial = lax.all_to_all(
-            partial.reshape(dp_count, slots, LANES), "dp", 0, 0, tiled=True
-        )
-
-        def beside(sums):
+        def first_work(sums):
+            sums = sums.reshape(dp_count, slots, LANES)
+            return jnp.sum(lax.all_to_all(sums, "dp", 0, 0, tiled=True), axis=0)
+
+        def second_work(sums):
             return cube.exchange_sum(sums, [[cube.core], [x]])
 
-        pieces, own, planes = plan.gather(
-            shard, shard_zero, jnp.sum(partial, axis=0), beside, planes, spread
-        )
+        pieces, planes, own = plan.gather(shard, spread(planes), partial, first_work, second_work)
         arrays = [plan.table, *pieces]
         specs = [SM] + [VM] * len(pieces)
         mods = [own[layer * BIAS_LINES : (layer + 1) * BIAS_LINES] for layer in range(LAYERS)]
@@ -925,11 +1034,29 @@
             specs,
             [pltpu.VMEM((end - begin, LANES), f32)],
             flops=10**9,
-            vmem=24,
         )
 
     weights = [None] * LAYERS
-    hidden_blocks, weights[0] = gather_blocks(hidden, unpack_layer(0))
+
+    def begin_layer(layer, value):
+        def work(blocks):
+            weights = unpack_layer(layer)
+            return weights, run(
+                functools.partial(near_attend_kernel, NEAR),
+                f"near_attend_{layer}",
+                [
+                    shape((len(NEAR) * rows, 3 * D), bf16), shape((rows, D), f32),
+                    shape((rows, LANES), f32), shape((rows, LANES), f32),
+                ],
+                [limits, *blocks, weights[0]],
+                [SM] + [VM] * (len(NEAR) + 1),
+                flops=10**9,
+            )
+
+        blocks, (weights[layer], attention) = gather_blocks(value, work)
+        return blocks, attention
+
+    hidden_blocks, partial_attention = begin_layer(0, hidden)
 
     stored = []
     for layer in range(LAYERS):
@@ -942,19 +1069,26 @@
             shape((rows, D), f32), shape((rows, D), f32), shape((rows, FF), f32),
             shape((rows, D), f32), shape((rows, D), f32), shape((rows, D), bf16),
         ]
+        near, far = NEAR, tuple(range(len(NEAR), var_count))
         qkv, att, lse, b1, mid, pre, b2, next_residual, next_hidden = run(
-            functools.partial(layer_fwd_kernel, var_count),
+            functools.partial(layer_fwd_kernel, near, far),
             f"layer_fwd_{layer}",
             outs,
-            [limits, *blocks, residual, mod, mod_next, qkvw, projw, upw, downw],
-            [SM] + [VM] * (var_count + 7),
-            [pltpu.VMEM((rows, D), bf16), pltpu.VMEM((rows, FF), bf16)],
+            [
+                limits, *(blocks[r] for r in far), *partial_attention, residual, mod, mod_next,
+                qkvw, projw, upw, downw,
+            ],
+            [SM] + [VM] * (len(far) + 11),
+            [
+                pltpu.VMEM((rows, D), bf16), pltpu.VMEM((rows, FF), bf16),
+                pltpu.VMEM((len(far) * rows, 3 * D), bf16),
+            ],
             flops=4 * 10**9,
         )
         stored.append((hidden, residual, qkv, att, lse, b1, mid, pre, b2))
         residual, hidden = next_residual, next_hidden
         if layer + 1 < LAYERS:
-            hidden_blocks, weights[layer + 1] = gather_blocks(hidden, unpack_layer(layer + 1))
+            hidden_blocks, partial_attention = begin_layer(layer + 1, hidden)
     output = residual
 
     grad_out = cotangent[0]
@@ -977,15 +1111,27 @@
             [grad_out, mod, pre, mid, b1, b2, att, lse, upw, downw, projw],
             flops=2 * 10**9,
         )
-        (gq,) = run(
-            query_bwd_kernel,
-            f"query_bwd_{layer}",
-            [shape((rows, D), bf16)],
-            [limits, qkv, ga_ext, lse, delta],
-            [SM] + [VM] * 4,
-            flops=4 * 10**9,
-        )
-        blocks, gq = gather_blocks(ga_ext, gq)
+
+        def work(near_blocks, layer=layer, qkv=qkv, ga_ext=ga_ext, lse=lse, delta=delta):
+            (gq,) = run(
+                query_bwd_kernel,
+                f"query_bwd_{layer}",
+                [shape((rows, D), bf16)],
+                [limits, qkv, ga_ext, lse, delta],
+                [SM] + [VM] * 4,
+                flops=4 * 10**9,
+            )
+            return gq, run(
+                functools.partial(near_keys_kernel, NEAR),
+                f"near_keys_{layer}",
+                [shape((rows, D), f32), shape((rows, D), f32)],
+                [limits, *near_blocks, qkv],
+                [SM] + [VM] * (len(NEAR) + 1),
+                [pltpu.VMEM((len(NEAR), 16, rows), f32)],
+                flops=3 * 10**9,
+            )
+
+        blocks, (gq, (key_near, value_near)) = gather_blocks(ga_ext, work)
         start = first_line + ADA_LINES + BIAS_LINES + QKV_LINES
         count = up16(start + PROJ_LINES + 2 * FF_LINES) - down16(start)
         (section,) = run(
@@ -997,14 +1143,18 @@
             flops=2 * 10**9,
         )
         sections.append((start, PROJ_LINES + 2 * FF_LINES, section))
+        far = tuple(range(len(NEAR), var_count))
         gqkv, grad_out, sums_b = run(
-            functools.partial(keys_bwd_kernel, var_count),
+            functools.partial(keys_bwd_kernel, far),
             f"keys_bwd_{layer}",
             [shape((rows, 3 * D), bf16), shape((rows, D), f32), shape((24, LANES), f32)],
-            [limits, *blocks, qkv, gq, residual, mod, qkvw, gmid],
-            [SM] + [VM] * (var_count + 6),
-            [pltpu.VMEM((var_count, 16, rows), f32)],
-            flops=5 * 10**9,
+            [
+                limits, *(blocks[r] for r in far), qkv, gq, key_near, value_near, residual, mod, qkvw,
+                gmid,
+            ],
+            [SM] + [VM] * (len(far) + 8),
+            [pltpu.VMEM((len(far), 16, rows), f32)],
+            flops=3 * 10**9,
         )
         start = first_line + ADA_LINES + BIAS_LINES
         count = up16(start + QKV_LINES) - down16(start)
@@ -1035,8 +1185,7 @@
     )
     sections.append((0, HEAD_LINES, section))
     def unspread(values):
-        values = lax.all_to_all(values, "var", 0, 0, tiled=True)
-        return values.transpose(2, 1, 0, 3).reshape(local_vars, PIX, seq_len)
+        return lax.all_to_all(values, "var", 0, 0, tiled=True)
 
     if planned:
         sections.sort(key=lambda entry: entry[0])
@@ -1048,20 +1197,19 @@
             "pack",
             [shape((8, HALF, LANES), bf16)] * 6,
             [
-                plan.table,
+                plan.back_table,
                 *parts,
             ],
             [SM] + [VM] * len(sections),
-            [pltpu.VMEM((total_lines, LANES), bf16)],
-            vmem=16,
+            [pltpu.VMEM((len(ENTRIES) * HALF, LANES), bf16)],
         )
 
         def beside_scatter(values):
-            grads, own = values
-            return unspread(grads), to_all(own)
-
-        grad_lines, (patch_grads, sums) = plan.scatter(
-            packed[::2], packed[1::2], (pixel_grad, own), beside_scatter
+            own, grads = values
+            return to_all(own), unspread(grads)
+
+        grad_lines, (sums, pixel_grad) = plan.scatter(
+            packed[::2], packed[1::2], (own, pixel_grad), beside_scatter
         )
         sums = sums.reshape(dp_count * slots, LANES)
         high = sums.astype(bf16)
@@ -1073,7 +1221,7 @@
             inside = jnp.logical_and(line >= start, line < start + ADA_LINES + BIAS_LINES)
             grad_lines = jnp.where(inside, ada_lines, grad_lines)
     else:
-        patch_grads = unspread(pixel_grad)
+        pixel_grad = unspread(pixel_grad)
         for layer in range(LAYERS):
             start = HEAD_LINES + layer * LAYER_LINES
             outer = cond_low[0].astype(f32)[:, None, None] * ada_sums[layer][None]
@@ -1094,10 +1242,13 @@
         grad_lines = lax.psum_scatter(
             whole, ("var", "dp"), scatter_dimension=0, tiled=True
         ).astype(f32)
+    patch_grads = pixel_grad.transpose(2, 1, 0, 3).reshape(local_vars, PIX, seq_len)
     grad_shard = grad_lines.reshape(-1)
     squares = jnp.sum(grad_shard * grad_shard)
     if planned:
-        squares = cube.exchange_sum(jnp.broadcast_to(squares, (8, LANES)), every)[0, 0]
+        copies = jnp.broadcast_to(squares, (cube.owners, 1, LANES))
+        copies = lax.all_to_all(copies, ("var", "dp"), 0, 0, tiled=True)
+        squares = jnp.sum(copies, axis=0)[0, 0]
     else:
         squares = lax.psum(squares, ("var", "dp"))
     grad_norm = jnp.sqrt(squares)

time: 270 us -> 259 us (0.959)
  waiting for transfers between devices: 93.5 us -> 79.2 us
  other arithmetic: 13.1 us -> 20 us
    ppermute x43 -> x37, waiting for transfers between devices: 73.4 us -> 57.7 us  [send(): return lax.ppermute(value, ('var', 'dp'), pairs)]
    all_to_all x2 -> x3, starting transfers between devices: 7.01 us -> 14.5 us  [the longest x1 7.24 us: first_work(): return jnp.sum(lax.all_to_all(sums, 'dp', 0, 0, tiled=True), axis=0)]
    all_to_all x2 -> x3, waiting for transfers between devices: 4.87 us -> 11.4 us  [the longest x1 6.51 us: first_work(): return jnp.sum(lax.all_to_all(sums, 'dp', 0, 0, tiled=True), axis=0)]
    all_to_all x2, starting transfers between devices: 12.7 us -> 7.34 us  [to_all(): return lax.all_to_all(copies, 'dp', 0, 0, tiled=True)]
    add x0 -> x2, other arithmetic: none -> 3.78 us  [the longest x1 2.52 us: scatter(): jnp.where(is_one, first, second) + partner[0]]
    convert_element_type x4, other arithmetic: 1.72 us -> 4.67 us  [the longest x3 2.98 us: scatter(): low = [second.astype(bf16), third.astype(bf16), first.astype(bf16)]]
    concatenate x6, other arithmetic: 0.33 us -> 3.14 us  [grow(): current[chunk] = jnp.concatenate([current[chunk], got], axis=0)]
    ppermute x43 -> x37, starting transfers between devices: 39.5 us -> 37.3 us  [send(): return lax.ppermute(value, ('var', 'dp'), pairs)]
  transfers between devices with their start and end apart: 60 -> 55, of which waited for: 39 -> 29; matrix products, arithmetic and copies ran while one was open for 4% -> 8% of each run, Pallas kernels for 10% -> 15%
where the time goes in v2:
time: 259 us; the launch traced here: 255 us
  waiting for transfers between devices  79.2 us (31%)
  Pallas kernels  71 us (27%)
  starting transfers between devices  68.1 us (26%)
  other arithmetic  20 us (8%)
  local copies, waits for them, and re-layouts  9.52 us (4%)
  between operations  5.46 us (2%)
    pallas_call x22, Pallas kernels, run(): pl.pallas_call(kernel, name=name, out_shape=outs, in_specs=in_specs, out_...  71 us
    ppermute x37, waiting for transfers between devices, send(): return lax.ppermute(value, ('var', 'dp'), pairs)  57.7 us
    ppermute x37, starting transfers between devices, send(): return lax.ppermute(value, ('var', 'dp'), pairs)  37.3 us
    all_to_all x2, starting transfers between devices, to_all(): return lax.all_to_all(copies, 'dp', 0, 0, tiled=True)  7.34 us
    all_to_all x1, starting transfers between devices, first_work(): return jnp.sum(lax.all_to_all(sums, 'dp', 0, 0, tiled=True), axis=0)  7.24 us
    all_to_all x1, waiting for transfers between devices, first_work(): return jnp.sum(lax.all_to_all(sums, 'dp', 0, 0, tiled=True), axis=0)  6.51 us
    ppermute x12, starting transfers between devices, flip(): return lax.ppermute(value, axis, [(i, i ^ bit) for i in range(count)])  5.66 us
  transfers between devices with their start and end apart: 55, of which 29 were waited for; matrix products, arithmetic and copies ran while one was open for 8% of the time, Pallas kernels for 15%

profile of v2, /device:TPU:0, one launch (start us, length us, event | category | flops | bytes accessed | tf_op | source)
XLA Modules:
  0.0 254.9 jit_solution(5551980157045459696)
XLA Ops:
  3.3 6.7 %collective-permute-start.1 = (bf16[1440,128]{1,0:T(8,128)(2,1)S(1)}, bf16[1440,128]{1,0:T(8,128)(2,1)}, u32[]{:S(2)}, u32[]{:S(2)}) collective-permute-start(bf16[1440,128]{1,0:T(8,128)(2,1)S(1)} %convert_bitcast_fusion.2.shard), channel_id=1, source_target_pairs={{0,4},{1,5},{2,6},{3,7},{7,3},{16,20},{17,21},{22,18},{23,19}} | collective-permute-start | bytes 1105928 | tf_op jit(solution)/shard_map/ppermute | solution.py:772
  10.8 3.3 %all-to-all-start.1 = ((bf16[8,3,128]{2,1,0:T(4,128)(2,1)}), bf16[8,3,128]{2,1,0:T(4,128)(2,1)S(1)}, u32[]{:S(2)}, u32[]{:S(2)}) async-start(bf16[8,3,128]{2,1,0:T(4,128)(2,1)} %broadcast_in_dim.67), calls=%async_computation.1 | async-start | bytes 16384 | tf_op jit(solution)/shard_map/all_to_all | solution.py:960
  17.1 2.0 collective-permute-start.3
  20.6 3.4 %all-to-all-start = ((bf16[4,5,18,256]{3,2,1,0:T(8,128)(2,1)}), bf16[4,5,18,256]{3,2,1,0:T(8,128)(2,1)S(1)}, u32[]{:S(2)}, u32[]{:S(2)}) async-start(bf16[4,5,18,256]{3,2,1,0:T(8,128)(2,1)} %maximum_bitcast_fusion), calls=%async_computation | async-start | bytes 491520 | tf_op jit(solution)/shard_map/all_to_all | solution.py:946
  24.0 2.4 ada.1
  27.4 2.5 all-to-all-done.refs_13_
  31.2 4.7 %collective-permute-start.6 = (bf16[1,720,128]{2,1,0:T(8,128)(2,1)S(1)}, bf16[1,720,128]{2,1,0:T(8,128)(2,1)S(1)}, u32[]{:S(2)}, u32[]{:S(2)}) collective-permute-start(bf16[1,720,128]{2,1,0:T(8,128)(2,1)S(1)} %get-tuple-element.314), channel_id=1, source_target_pairs={{0,2},{1,3},{2,0},{3,1},{4,6},{5,7},{6,4},{7,5},{8,10},{9,11},{10,... | collective-permute-start | bytes 552968 | tf_op jit(solution)/shard_map/ppermute | solution.py:772
  36.9 7.2 %all-to-all-start.2 = ((f32[8,36,128]{2,1,0:T(8,128)}), f32[8,36,128]{2,1,0:T(8,128)}, u32[]{:S(2)}, u32[]{:S(2)}) async-start(f32[8,36,128]{2,1,0:T(8,128)} %reshape.128), calls=%async_computation.2 | async-start | bytes 327680 | tf_op jit(solution)/shard_map/all_to_all | solution.py:979
  45.3 6.5 %all-to-all-done.2 = f32[8,36,128]{2,1,0:T(8,128)} async-done(((f32[8,36,128]{2,1,0:T(8,128)}), f32[8,36,128]{2,1,0:T(8,128)}, u32[]{:S(2)}, u32[]{:S(2)}) %all-to-all-start.2) | async-done | bytes 147488 | tf_op jit(solution)/shard_map/all_to_all | solution.py:979
  53.8 1.7 collective-permute-start.11
  58.4 4.0 %collective-permute-done.13 = f32[36,128]{1,0:T(8,128)S(1)} collective-permute-done((f32[36,128]{1,0:T(8,128)S(1)}, f32[36,128]{1,0:T(8,128)S(1)}, u32[]{:S(2)}, u32[]{:S(2)}) %collective-permute-start.13) | collective-permute-done | bytes 18464 | tf_op jit(solution)/shard_map/ppermute | solution.py:772
  64.6 10.9 %collective-permute-done.7.refs_2_ = bf16[4,720,128]{2,1,0:T(8,128)(2,1)S(1)} collective-permute-done((bf16[4,720,128]{2,1,0:T(8,128)(2,1)S(1)}, bf16[4,720,128]{2,1,0:T(8,128)(2,1)S(1)}, u32[]{:S(2)}, u32[]{:S(2)}) %collective-permute-start.7) | collective-permute-done | bytes 737312 | tf_op jit(solution)/shard_map/ppermute | solution.py:772
  76.0 2.9 %collective-permute-done.14.refs_6_ = bf16[4,720,128]{2,1,0:T(8,128)(2,1)S(1)} collective-permute-done((bf16[4,720,128]{2,1,0:T(8,128)(2,1)S(1)}, bf16[4,720,128]{2,1,0:T(8,128)(2,1)S(1)}, u32[]{:S(2)}, u32[]{:S(2)}) %collective-permute-start.14) | collective-permute-done | bytes 737312 | tf_op jit(solution)/shard_map/ppermute | solution.py:772
  82.1 5.0 %agg_fwd.1 = (f32[256,384]{1,0:T(8,128)S(1)}, bf16[256,384]{1,0:T(8,128)(2,1)S(1)}, bf16[256,384]{1,0:T(8,128)(2,1)S(1)}, f32[6,72,256]{2,1,0:T(8,128)S(1)}, f32...) custom-call(s32[48]{0:T(128)S(1)} %get-tuple-element.317.refs_0_, ...), custom_call_target="tpu_custom_call" | custom-call | flops 1000000000 | bytes 12707520 | tf_op jit(solution)/shard_map/agg_fwd/pallas_call | solution.py:104
  88.3 3.2 %unpack_0.1 = (bf16[384,1152]{1,0:T(8,128)(2,1)S(1)}, bf16[384,384]{1,0:T(8,128)(2,1)S(1)}, bf16[384,1536]{1,0:T(8,128)(2,1)S(1)}, bf16[1536,384]{1,0:T(8,128)(2,1)S(1)}) custom-call(s32[48]{0:T(128)S(1)} %get-tuple-element.317.refs_0_, bf16[4,720,128]{2,1,0:T(8,128)(2,1)S(1)} %pad_maximum_fusion.refs_1_, ...), custom_call_target="tpu_custom_call" | custom-call | flops 1000000000 | bytes 12386496 | tf_op jit(solution)/shard_map/unpack_0/pallas_call | solution.py:104
  91.5 3.7 %near_attend_0.1 = (bf16[512,1152]{1,0:T(8,128)(2,1)S(1)}, f32[256,384]{1,0:T(8,128)S(1)}, f32[256,128]{1,0:T(8,128)S(1)}, f32[256,128]{1,0:T(8,128)S(1)}) custom-call(s32[2]{0:T(128)S(1)} %pad_add_fusion.limits, bf16[256,384]{1,0:T(8,128)(2,1)S(1)} %get-tuple-element.154.refs_0_.hidden, bf16[256,384]{1,0:T(8,128)(2,1)S(1)} %collective-permute-done.21.refs_1_, ...), custom_call_target="tpu_custom_call" | custom-call | flops 1000000000 | bytes 3112968 | tf_op jit(solution)/shard_map/near_attend_0/pallas_call | solution.py:104
  96.7 5.4 %layer_fwd_0.1 = (bf16[1024,1152]{1,0:T(8,128)(2,1)S(1)}, f32[256,384]{1,0:T(8,128)S(1)}, f32[256,128]{1,0:T(8,128)S(1)}, f32[256,384]{1,0:T(8,128)S(1)}, f32[25...) custom-call(s32[2]{0:T(128)S(1)} %pad_add_fusion.limits, ...), custom_call_target="tpu_custom_call" | custom-call | flops 4000000000 | bytes 12410888 | tf_op jit(solution)/shard_map/layer_fwd_0/pallas_call | solution.py:104
  103.4 3.4 %unpack_1.1 = (bf16[384,1152]{1,0:T(8,128)(2,1)S(1)}, bf16[384,384]{1,0:T(8,128)(2,1)S(1)}, bf16[384,1536]{1,0:T(8,128)(2,1)S(1)}, bf16[1536,384]{1,0:T(8,128)(2,1)S(1)}) custom-call(s32[48]{0:T(128)S(1)} %get-tuple-element.317.refs_0_, bf16[4,720,128]{2,1,0:T(8,128)(2,1)S(1)} %pad_maximum_fusion.refs_1_, ...), custom_call_target="tpu_custom_call" | custom-call | flops 1000000000 | bytes 12386496 | tf_op jit(solution)/shard_map/unpack_1/pallas_call | solution.py:104
  106.8 3.7 %near_attend_1.1 = (bf16[512,1152]{1,0:T(8,128)(2,1)S(1)}, f32[256,384]{1,0:T(8,128)S(1)}, f32[256,128]{1,0:T(8,128)S(1)}, f32[256,128]{1,0:T(8,128)S(1)}) custom-call(s32[2]{0:T(128)S(1)} %pad_add_fusion.limits, bf16[256,384]{1,0:T(8,128)(2,1)S(1)} %get-tuple-element.173.refs_0_.hidden, bf16[256,384]{1,0:T(8,128)(2,1)S(1)} %collective-permute-done.24.refs_1_, ...), custom_call_target="tpu_custom_call" | custom-call | flops 1000000000 | bytes 3112968 | tf_op jit(solution)/shard_map/near_attend_1/pallas_call | solution.py:104
  112.0 6.1 %layer_fwd_1.1 = (bf16[1024,1152]{1,0:T(8,128)(2,1)S(1)}, f32[256,384]{1,0:T(8,128)S(1)}, f32[256,128]{1,0:T(8,128)S(1)}, f32[256,384]{1,0:T(8,128)S(1)}, f32[25...) custom-call(s32[2]{0:T(128)S(1)} %pad_add_fusion.limits, ...), custom_call_target="tpu_custom_call" | custom-call | flops 4000000000 | bytes 12410888 | tf_op jit(solution)/shard_map/layer_fwd_1/pallas_call | solution.py:104
  118.1 2.4 mlp_bwd_1.1
  121.6 3.8 %query_bwd_1.1.refs_3_ = bf16[256,384]{1,0:T(8,128)(2,1)S(1)} custom-call(s32[2]{0:T(128)S(1)} %pad_add_fusion.limits, bf16[1024,1152]{1,0:T(8,128)(2,1)S(1)} %get-tuple-element.200.qkv.refs_2_, bf16[288,384]{1,0:T(8,128)(2,1)S(1)} %get-tuple-element.199.ga_ext.refs_0_, f32[256,128]{1,0:T(8,128)S(1)} %get-tuple-element.198.lse, ...), custom_call_target="tpu_custom_call" | custom-call | flops 4000000000 | bytes 3039240 | tf_op jit(solution)/shard_map/query_bwd_1/pallas_call | solution.py:104
  125.4 3.1 %near_keys_1.1 = (f32[256,384]{1,0:T(8,128)S(1)}, f32[256,384]{1,0:T(8,128)S(1)}) custom-call(s32[2]{0:T(128)S(1)} %pad_add_fusion.limits, bf16[288,384]{1,0:T(8,128)(2,1)S(1)} %get-tuple-element.199.ga_ext.refs_0_, bf16[288,384]{1,0:T(8,128)(2,1)S(1)} %collective-permute-done.27.refs_1_, bf16[1024,1152]{1,0:T(8,128)(2,1)S(1)} %get-tuple-element.200.qkv.refs_2_), custom_call_target="tpu_custom_call" | custom-call | flops 3000000000 | bytes 3588104 | tf_op jit(solution)/shard_map/near_keys_1/pallas_call | solution.py:104
  130.0 4.2 %keys_bwd_1.1 = (bf16[256,1152]{1,0:T(8,128)(2,1)S(1)}, f32[256,384]{1,0:T(8,128)S(1)}, f32[24,128]{1,0:T(8,128)S(1)}) custom-call(s32[2]{0:T(128)S(1)} %pad_add_fusion.limits, bf16[288,384]{1,0:T(8,128)(2,1)S(1)} %collective-permute-done.26.refs_0_, bf16[288,384]{1,0:T(8,128)(2,1)S(1)} %collective-permute-done.28.refs_1_, ...), custom_call_target="tpu_custom_call" | custom-call | flops 3000000000 | bytes 6463496 | tf_op jit(solution)/shard_map/keys_bwd_1/pallas_call | solution.py:104
  134.2 2.3 mlp_bwd_0.1
  138.1 3.8 %query_bwd_0.1.refs_3_ = bf16[256,384]{1,0:T(8,128)(2,1)S(1)} custom-call(s32[2]{0:T(128)S(1)} %pad_add_fusion.limits, bf16[1024,1152]{1,0:T(8,128)(2,1)S(1)} %get-tuple-element.217.qkv.refs_2_, bf16[288,384]{1,0:T(8,128)(2,1)S(1)} %get-tuple-element.216.ga_ext.refs_0_, f32[256,128]{1,0:T(8,128)S(1)} %get-tuple-element.215.lse, ...), custom_call_target="tpu_custom_call" | custom-call | flops 4000000000 | bytes 3039240 | tf_op jit(solution)/shard_map/query_bwd_0/pallas_call | solution.py:104
  143.9 3.1 %near_keys_0.1 = (f32[256,384]{1,0:T(8,128)S(1)}, f32[256,384]{1,0:T(8,128)S(1)}) custom-call(s32[2]{0:T(128)S(1)} %pad_add_fusion.limits, bf16[288,384]{1,0:T(8,128)(2,1)S(1)} %get-tuple-element.216.ga_ext.refs_0_, bf16[288,384]{1,0:T(8,128)(2,1)S(1)} %collective-permute-done.30.refs_1_, bf16[1024,1152]{1,0:T(8,128)(2,1)S(1)} %get-tuple-element.217.qkv.refs_2_), custom_call_target="tpu_custom_call" | custom-call | flops 3000000000 | bytes 3588104 | tf_op jit(solution)/shard_map/near_keys_0/pallas_call | solution.py:104
  147.1 1.5 collective-permute-done.31.refs_1_
  148.6 3.8 %keys_bwd_0.1 = (bf16[256,1152]{1,0:T(8,128)(2,1)S(1)}, f32[256,384]{1,0:T(8,128)S(1)}, f32[24,128]{1,0:T(8,128)S(1)}) custom-call(s32[2]{0:T(128)S(1)} %pad_add_fusion.limits, bf16[288,384]{1,0:T(8,128)(2,1)S(1)} %collective-permute-done.29.refs_0_, bf16[288,384]{1,0:T(8,128)(2,1)S(1)} %collective-permute-done.31.refs_1_, ...), custom_call_target="tpu_custom_call" | custom-call | flops 3000000000 | bytes 6463496 | tf_op jit(solution)/shard_map/keys_bwd_0/pallas_call | solution.py:104
  154.6 3.5 %agg_bwd.1 = (f32[4,4,18,256]{3,2,1,0:T(8,128)S(1)}, bf16[4336,128]{1,0:T(8,128)(2,1)S(1)}) custom-call(f32[256,384]{1,0:T(8,128)S(1)} %get-tuple-element.226.go, bf16[256,384]{1,0:T(8,128)(2,1)S(1)} %get-tuple-element.227.agg_low, f32[6,72,256]{2,1,0:T(8,128)S(1)} %get-tuple-element.228.probs, f32[288,768]{1,0:T(8,128)S(1)} %get-tuple-element.229.w, ...), custom_call_target="tpu_custom_call" | custom-call | flops 1000000000 | bytes 4871680 | tf_op jit(solution)/shard_map/agg_bwd/pallas_call | solution.py:104
  158.1 4.4 %pack.1 = (bf16[8,720,128]{2,1,0:T(8,128)(2,1)S(1)}, bf16[8,720,128]{2,1,0:T(8,128)(2,1)S(1)}, bf16[8,720,128]{2,1,0:T(8,128)(2,1)S(1)}, bf16[8,720,128]{2,1,0:T...) custom-call(s32[48]{0:T(128)S(1)} %get-tuple-element.316.table, ...), custom_call_target="tpu_custom_call" | custom-call | bytes 17051840 | tf_op jit(solution)/shard_map/pack/pallas_call | solution.py:104
  163.2 2.7 %collective-permute-done.38 = bf16[8,720,128]{2,1,0:T(8,128)(2,1)S(1)} collective-permute-done((bf16[8,720,128]{2,1,0:T(8,128)(2,1)S(1)}, bf16[8,720,128]{2,1,0:T(8,128)(2,1)S(1)}, u32[]{:S(2)}, u32[]{:S(2)}) %collective-permute-start.38) | collective-permute-done | bytes 1474592 | tf_op jit(solution)/shard_map/ppermute | solution.py:772
  166.1 1.8 collective-permute-start.39
  171.5 13.2 %collective-permute-done.39 = bf16[4,720,128]{2,1,0:T(8,128)(2,1)S(1)} collective-permute-done((bf16[4,720,128]{2,1,0:T(8,128)(2,1)S(1)}, bf16[4,720,128]{2,1,0:T(8,128)(2,1)S(1)}, u32[]{:S(2)}, u32[]{:S(2)}) %collective-permute-start.39) | collective-permute-done | bytes 737312 | tf_op jit(solution)/shard_map/ppermute | solution.py:772
  187.0 1.8 collective-permute-start.36
  191.0 5.8 %collective-permute-done.40 = bf16[2,720,128]{2,1,0:T(8,128)(2,1)S(1)} collective-permute-done((bf16[2,720,128]{2,1,0:T(8,128)(2,1)S(1)}, bf16[2,720,128]{2,1,0:T(8,128)(2,1)S(1)}, u32[]{:S(2)}, u32[]{:S(2)}) %collective-permute-start.40) | collective-permute-done | bytes 368672 | tf_op jit(solution)/shard_map/ppermute | solution.py:772
  199.5 3.3 %collective-permute-done.41 = bf16[1,720,128]{2,1,0:T(8,128)(2,1)S(1)} collective-permute-done((bf16[1,720,128]{2,1,0:T(8,128)(2,1)S(1)}, bf16[1,720,128]{2,1,0:T(8,128)(2,1)S(1)}, u32[]{:S(2)}, u32[]{:S(2)}) %collective-permute-start.41) | collective-permute-done | bytes 184352 | tf_op jit(solution)/shard_map/ppermute | solution.py:772
  208.8 4.1 %all-to-all-start.4 = ((f32[4,4,18,256]{3,1,2,0:T(4,128)}), f32[4,4,18,256]{3,1,2,0:T(4,128)}, u32[]{:S(2)}, u32[]{:S(2)}) async-start(f32[4,4,18,256]{3,1,2,0:T(4,128)} %copy.32), calls=%async_computation.4 | async-start | bytes 589824 | tf_op jit(solution)/shard_map/all_to_all | solution.py:1188
  212.9 2.0 convert_bitcast_fusion
  216.2 4.2 %collective-permute-done.42 = bf16[720,128]{1,0:T(8,128)(2,1)} collective-permute-done((bf16[720,128]{1,0:T(8,128)(2,1)}, bf16[720,128]{1,0:T(8,128)(2,1)}, u32[]{:S(2)}, u32[]{:S(2)}) %collective-permute-start.42) | collective-permute-done | bytes 184352 | tf_op jit(solution)/shard_map/ppermute | solution.py:772
  220.4 1.7 convert_element_type.249
  222.8 4.0 %all-to-all-start.3 = ((f32[8,36,128]{2,1,0:T(8,128)}), f32[8,36,128]{2,1,0:T(8,128)}, u32[]{:S(2)}, u32[]{:S(2)}) async-start(f32[8,36,128]{2,1,0:T(8,128)} %broadcast_in_dim.71), calls=%async_computation.3 | async-start | bytes 327680 | tf_op jit(solution)/shard_map/all_to_all | solution.py:960
  226.8 3.0 %collective-permute-done.48 = bf16[720,128]{1,0:T(8,128)(2,1)} collective-permute-done((bf16[720,128]{1,0:T(8,128)(2,1)}, bf16[720,128]{1,0:T(8,128)(2,1)}, u32[]{:S(2)}, u32[]{:S(2)}) %collective-permute-start.48) | collective-permute-done | bytes 184352 | tf_op jit(solution)/shard_map/ppermute | solution.py:772
  229.8 2.5 bitcast_add_fusion
  232.4 3.1 %all-to-all-done.3 = f32[8,36,128]{2,1,0:T(8,128)} async-done(((f32[8,36,128]{2,1,0:T(8,128)}), f32[8,36,128]{2,1,0:T(8,128)}, u32[]{:S(2)}, u32[]{:S(2)}) %all-to-all-start.3) | async-done | bytes 147488 | tf_op jit(solution)/shard_map/all_to_all | solution.py:960
  241.4 3.1 %all-to-all-start.5 = ((f32[32,1,128]{2,1,0:T(1,128)}), f32[32,1,128]{2,1,0:T(1,128)S(1)}, u32[]{:S(2)}, u32[]{:S(2)}) async-start(f32[32,1,128]{2,1,0:T(1,128)} %broadcast_in_dim.74), calls=%async_computation.5 | async-start | bytes 32768 | tf_op jit(solution)/shard_map/all_to_all | solution.py:1250
  246.6 4.9 %all-to-all-done.5 = f32[32,1,128]{2,1,0:T(1,128)S(1)} async-done(((f32[32,1,128]{2,1,0:T(1,128)}), f32[32,1,128]{2,1,0:T(1,128)S(1)}, u32[]{:S(2)}, u32[]{:S(2)}) %all-to-all-start.5) | async-done | bytes 16416 | tf_op jit(solution)/shard_map/all_to_all | solution.py:1250
  251.7 1.9 fusion.16
  (196 shorter events, 61.9 us)
Async XLA Ops:
  1.9 28.0 %collective-permute-start = (bf16[1440,128]{1,0:T(8,128)(2,1)S(1)}, bf16[1440,128]{1,0:T(8,128)(2,1)}, u32[]{:S(2)}, u32[]{:S(2)}) collective-permute-start(bf16[1440,128]{1,0:T(8,128)(2,1)S(1)} %convert_bitcast_fusion.2.shard), channel_id=1, source_target_pairs={{8,12},{9,13},{10,14},{11,15},{12,8},{13,9},{14,10},{15,11},{24,28... | collective-permute-start | bytes 1105928 | tf_op jit(solution)/shard_map/ppermute | solution.py:772
  3.3 26.6 %collective-permute-start.1 = (bf16[1440,128]{1,0:T(8,128)(2,1)S(1)}, bf16[1440,128]{1,0:T(8,128)(2,1)}, u32[]{:S(2)}, u32[]{:S(2)}) collective-permute-start(bf16[1440,128]{1,0:T(8,128)(2,1)S(1)} %convert_bitcast_fusion.2.shard), channel_id=1, source_target_pairs={{0,4},{1,5},{2,6},{3,7},{7,3},{16,20},{17,21},{22,18},{23,19}} | collective-permute-start | bytes 1105928 | tf_op jit(solution)/shard_map/ppermute | solution.py:772
  10.1 7.0 %collective-permute-start.2 = (bf16[720,128]{1,0:T(8,128)(2,1)S(1)}, bf16[720,128]{1,0:T(8,128)(2,1)S(1)}, u32[]{:S(2)}, u32[]{:S(2)}) collective-permute-start(bf16[720,128]{1,0:T(8,128)(2,1)S(1)} %slice_bitcast_fusion), channel_id=1, source_target_pairs={{0,8},{1,9},{2,10},{3,11},{4,12},{5,13},{6,14},{7,15},{8,0},{9,1},... | collective-permute-start | bytes 552968 | tf_op jit(solution)/shard_map/ppermute | solution.py:772
  10.8 9.8 %all-to-all-start.1 = ((bf16[8,3,128]{2,1,0:T(4,128)(2,1)}), bf16[8,3,128]{2,1,0:T(4,128)(2,1)S(1)}, u32[]{:S(2)}, u32[]{:S(2)}) async-start(bf16[8,3,128]{2,1,0:T(4,128)(2,1)} %broadcast_in_dim.67), calls=%async_computation.1 | async-start | bytes 16384 | tf_op jit(solution)/shard_map/all_to_all | solution.py:960
  17.1 9.3 %collective-permute-start.3 = (bf16[1,720,128]{2,1,0:T(8,128)(2,1)S(1)}, bf16[1,720,128]{2,1,0:T(8,128)(2,1)}, u32[]{:S(2)}, u32[]{:S(2)}) collective-permute-start(bf16[1,720,128]{2,1,0:T(8,128)(2,1)S(1)} %select_bitcast_fusion.2), channel_id=1, source_target_pairs={{0,1},{1,0},{2,3},{3,2},{4,5},{5,4},{6,7},{7,6},{8,9},{9,8},{10,11... | collective-permute-start | bytes 552968 | tf_op jit(solution)/shard_map/ppermute | solution.py:772
  20.6 9.3 %all-to-all-start = ((bf16[4,5,18,256]{3,2,1,0:T(8,128)(2,1)}), bf16[4,5,18,256]{3,2,1,0:T(8,128)(2,1)S(1)}, u32[]{:S(2)}, u32[]{:S(2)}) async-start(bf16[4,5,18,256]{3,2,1,0:T(8,128)(2,1)} %maximum_bitcast_fusion), calls=%async_computation | async-start | bytes 491520 | tf_op jit(solution)/shard_map/all_to_all | solution.py:946
  31.2 13.0 %collective-permute-start.6 = (bf16[1,720,128]{2,1,0:T(8,128)(2,1)S(1)}, bf16[1,720,128]{2,1,0:T(8,128)(2,1)S(1)}, u32[]{:S(2)}, u32[]{:S(2)}) collective-permute-start(bf16[1,720,128]{2,1,0:T(8,128)(2,1)S(1)} %get-tuple-element.314), channel_id=1, source_target_pairs={{0,2},{1,3},{2,0},{3,1},{4,6},{5,7},{6,4},{7,5},{8,10},{9,11},{10,... | collective-permute-start | bytes 552968 | tf_op jit(solution)/shard_map/ppermute | solution.py:772
  35.8 16.9 %collective-permute-start.4 = (bf16[2,720,128]{2,1,0:T(8,128)(2,1)S(1)}, bf16[2,720,128]{2,1,0:T(8,128)(2,1)}, u32[]{:S(2)}, u32[]{:S(2)}) collective-permute-start(bf16[2,720,128]{2,1,0:T(8,128)(2,1)S(1)} %pad_maximum_fusion.3), channel_id=1, source_target_pairs={{0,16},{1,17},{2,18},{3,19},{4,20},{5,21},{6,22},{7,23},{8,24},{9,... | collective-permute-start | bytes 1105928 | tf_op jit(solution)/shard_map/ppermute | solution.py:772
  36.2 8.1 %collective-permute-start.5 = (bf16[1,720,128]{2,1,0:T(8,128)(2,1)S(1)}, bf16[1,720,128]{2,1,0:T(8,128)(2,1)}, u32[]{:S(2)}, u32[]{:S(2)}) collective-permute-start(bf16[1,720,128]{2,1,0:T(8,128)(2,1)S(1)} %get-tuple-element.315), channel_id=1, source_target_pairs={{0,2},{1,3},{2,0},{3,1},{4,6},{5,7},{6,4},{7,5},{8,10},{9,11},{10,... | collective-permute-start | bytes 552968 | tf_op jit(solution)/shard_map/ppermute | solution.py:772
  36.9 14.9 %all-to-all-start.2 = ((f32[8,36,128]{2,1,0:T(8,128)}), f32[8,36,128]{2,1,0:T(8,128)}, u32[]{:S(2)}, u32[]{:S(2)}) async-start(f32[8,36,128]{2,1,0:T(8,128)} %reshape.128), calls=%async_computation.2 | async-start | bytes 327680 | tf_op jit(solution)/shard_map/all_to_all | solution.py:979
  53.8 8.7 %collective-permute-start.11 = (bf16[2,720,128]{2,1,0:T(8,128)(2,1)S(1)}, bf16[2,720,128]{2,1,0:T(8,128)(2,1)S(1)}, u32[]{:S(2)}, u32[]{:S(2)}) collective-permute-start(bf16[2,720,128]{2,1,0:T(8,128)(2,1)S(1)} %pad_maximum_fusion.5), channel_id=1, source_target_pairs={{0,16},{1,17},{2,18},{3,19},{4,20},{5,21},{6,22},{7,23},{8,24},{9,... | collective-permute-start | bytes 1105928 | tf_op jit(solution)/shard_map/ppermute | solution.py:772
  55.5 7.7 %collective-permute-start.10 = (bf16[2,720,128]{2,1,0:T(8,128)(2,1)S(1)}, bf16[2,720,128]{2,1,0:T(8,128)(2,1)S(1)}, u32[]{:S(2)}, u32[]{:S(2)}) collective-permute-start(bf16[2,720,128]{2,1,0:T(8,128)(2,1)S(1)} %pad_maximum_fusion.4), channel_id=1, source_target_pairs={{0,1},{1,0},{2,3},{3,2},{4,5},{5,4},{6,7},{7,6},{8,9},{9,8},{10,11... | collective-permute-start | bytes 1105928 | tf_op jit(solution)/shard_map/ppermute | solution.py:772
  56.8 5.6 %collective-permute-start.13 = (f32[36,128]{1,0:T(8,128)S(1)}, f32[36,128]{1,0:T(8,128)S(1)}, u32[]{:S(2)}, u32[]{:S(2)}) collective-permute-start(f32[36,128]{1,0:T(8,128)S(1)} %add.182), channel_id=1, source_target_pairs={{0,16},{1,17},{2,18},{3,19},{4,20},{5,21},{6,22},{7,23},{8,24},{9,... | collective-permute-start | bytes 55304 | tf_op jit(solution)/shard_map/ppermute | solution.py:772
  57.2 18.3 %collective-permute-start.7 = (bf16[4,720,128]{2,1,0:T(8,128)(2,1)S(1)}, bf16[4,720,128]{2,1,0:T(8,128)(2,1)S(1)}, u32[]{:S(2)}, u32[]{:S(2)}) collective-permute-start(bf16[4,720,128]{2,1,0:T(8,128)(2,1)S(1)} %pad_maximum_fusion.refs_1_), channel_id=1, source_target_pairs={{0,2},{1,3},{2,0},{3,1},{4,6},{5,7},{6,4},{7,5},{8,10},{9,11},{10,... | collective-permute-start | bytes 2211848 | tf_op jit(solution)/shard_map/ppermute | solution.py:772
  58.4 17.1 %collective-permute-start.8 = (bf16[4,720,128]{2,1,0:T(8,128)(2,1)S(1)}, bf16[4,720,128]{2,1,0:T(8,128)(2,1)S(1)}, u32[]{:S(2)}, u32[]{:S(2)}) collective-permute-start(bf16[4,720,128]{2,1,0:T(8,128)(2,1)S(1)} %pad_maximum_fusion.refs_1_), channel_id=1, source_target_pairs={{0,8},{1,9},{2,10},{3,11},{4,12},{5,13},{6,14},{7,15},{8,0},{9,1},... | collective-permute-start | bytes 2211848 | tf_op jit(solution)/shard_map/ppermute | solution.py:772
  63.3 15.6 %collective-permute-start.14 = (bf16[4,720,128]{2,1,0:T(8,128)(2,1)S(1)}, bf16[4,720,128]{2,1,0:T(8,128)(2,1)S(1)}, u32[]{:S(2)}, u32[]{:S(2)}) collective-permute-start(bf16[4,720,128]{2,1,0:T(8,128)(2,1)S(1)} %pad_maximum_fusion.1.refs_5_), channel_id=1, source_target_pairs={{0,16},{1,17},{2,18},{3,19},{4,20},{5,21},{6,22},{7,23},{8,24},{9,... | collective-permute-start | bytes 2211848 | tf_op jit(solution)/shard_map/ppermute | solution.py:772
  64.6 14.5 %collective-permute-start.17 = (bf16[4,720,128]{2,1,0:T(8,128)(2,1)S(1)}, bf16[4,720,128]{2,1,0:T(8,128)(2,1)S(1)}, u32[]{:S(2)}, u32[]{:S(2)}) collective-permute-start(bf16[4,720,128]{2,1,0:T(8,128)(2,1)S(1)} %pad_maximum_fusion.2.refs_9_), channel_id=1, source_target_pairs={{0,1},{1,0},{2,3},{3,2},{4,5},{5,4},{6,7},{7,6},{8,9},{9,8},{10,11... | collective-permute-start | bytes 2211848 | tf_op jit(solution)/shard_map/ppermute | solution.py:772
  64.6 15.6 %collective-permute-start.15 = (bf16[4,720,128]{2,1,0:T(8,128)(2,1)S(1)}, bf16[4,720,128]{2,1,0:T(8,128)(2,1)S(1)}, u32[]{:S(2)}, u32[]{:S(2)}) collective-permute-start(bf16[4,720,128]{2,1,0:T(8,128)(2,1)S(1)} %pad_maximum_fusion.1.refs_5_), channel_id=1, source_target_pairs={{0,8},{1,9},{2,10},{3,11},{4,12},{5,13},{6,14},{7,15},{8,0},{9,1},... | collective-permute-start | bytes 2211848 | tf_op jit(solution)/shard_map/ppermute | solution.py:772
  75.5 4.7 %collective-permute-start.18 = (bf16[4,720,128]{2,1,0:T(8,128)(2,1)S(1)}, bf16[4,720,128]{2,1,0:T(8,128)(2,1)S(1)}, u32[]{:S(2)}, u32[]{:S(2)}) collective-permute-start(bf16[4,720,128]{2,1,0:T(8,128)(2,1)S(1)} %pad_maximum_fusion.2.refs_9_), channel_id=1, source_target_pairs={{0,8},{1,9},{2,10},{3,11},{4,12},{5,13},{6,14},{7,15},{8,0},{9,1},... | collective-permute-start | bytes 2211848 | tf_op jit(solution)/shard_map/ppermute | solution.py:772
  75.5 4.7 %collective-permute-start.9 = (bf16[4,720,128]{2,1,0:T(8,128)(2,1)S(1)}, bf16[4,720,128]{2,1,0:T(8,128)(2,1)S(1)}, u32[]{:S(2)}, u32[]{:S(2)}) collective-permute-start(bf16[4,720,128]{2,1,0:T(8,128)(2,1)S(1)} %collective-permute-done.7.refs_2_), channel_id=1, source_target_pairs={{0,8},{1,9},{2,10},{3,11},{4,12},{5,13},{6,14},{7,15},{8,0},{9,1},... | collective-permute-start | bytes 2211848 | tf_op jit(solution)/shard_map/ppermute | solution.py:772
  79.1 3.0 %collective-permute-start.19 = (bf16[4,720,128]{2,1,0:T(8,128)(2,1)S(1)}, bf16[4,720,128]{2,1,0:T(8,128)(2,1)S(1)}, u32[]{:S(2)}, u32[]{:S(2)}) collective-permute-start(bf16[4,720,128]{2,1,0:T(8,128)(2,1)S(1)} %collective-permute-done.17.refs_10_), channel_id=1, source_target_pairs={{0,8},{1,9},{2,10},{3,11},{4,12},{5,13},{6,14},{7,15},{8,0},{9,1},... | collective-permute-start | bytes 2211848 | tf_op jit(solution)/shard_map/ppermute | solution.py:772
  87.1 4.3 %collective-permute-start.21 = (bf16[256,384]{1,0:T(8,128)(2,1)S(1)}, bf16[256,384]{1,0:T(8,128)(2,1)S(1)}, u32[]{:S(2)}, u32[]{:S(2)}) collective-permute-start(bf16[256,384]{1,0:T(8,128)(2,1)S(1)} %get-tuple-element.154.refs_0_.hidden), channel_id=1, source_target_pairs={{0,8},{8,0},{16,24},{24,16},{1,9},{9,1},{17,25},{25,17},{2,10},{10... | collective-permute-start | bytes 589832 | tf_op jit(solution)/shard_map/ppermute | solution.py:905
  87.3 7.9 %collective-permute-start.20 = (bf16[256,384]{1,0:T(8,128)(2,1)S(1)}, bf16[256,384]{1,0:T(8,128)(2,1)S(1)}, u32[]{:S(2)}, u32[]{:S(2)}) collective-permute-start(bf16[256,384]{1,0:T(8,128)(2,1)S(1)} %get-tuple-element.154.refs_0_.hidden), channel_id=1, source_target_pairs={{0,16},{8,24},{16,0},{24,8},{1,17},{9,25},{17,1},{25,9},{2,18},{10... | collective-permute-start | bytes 589832 | tf_op jit(solution)/shard_map/ppermute | solution.py:905
  102.0 4.8 %collective-permute-start.24 = (bf16[256,384]{1,0:T(8,128)(2,1)S(1)}, bf16[256,384]{1,0:T(8,128)(2,1)S(1)}, u32[]{:S(2)}, u32[]{:S(2)}) collective-permute-start(bf16[256,384]{1,0:T(8,128)(2,1)S(1)} %get-tuple-element.173.refs_0_.hidden), channel_id=1, source_target_pairs={{0,8},{8,0},{16,24},{24,16},{1,9},{9,1},{17,25},{25,17},{2,10},{10... | collective-permute-start | bytes 589832 | tf_op jit(solution)/shard_map/ppermute | solution.py:905
  102.3 8.3 %collective-permute-start.23 = (bf16[256,384]{1,0:T(8,128)(2,1)S(1)}, bf16[256,384]{1,0:T(8,128)(2,1)S(1)}, u32[]{:S(2)}, u32[]{:S(2)}) collective-permute-start(bf16[256,384]{1,0:T(8,128)(2,1)S(1)} %get-tuple-element.173.refs_0_.hidden), channel_id=1, source_target_pairs={{0,16},{8,24},{16,0},{24,8},{1,17},{9,25},{17,1},{25,9},{2,18},{10... | collective-permute-start | bytes 589832 | tf_op jit(solution)/shard_map/ppermute | solution.py:905
  120.5 4.9 %collective-permute-start.27 = (bf16[288,384]{1,0:T(8,128)(2,1)S(1)}, bf16[288,384]{1,0:T(8,128)(2,1)S(1)}, u32[]{:S(2)}, u32[]{:S(2)}) collective-permute-start(bf16[288,384]{1,0:T(8,128)(2,1)S(1)} %get-tuple-element.199.ga_ext.refs_0_), channel_id=1, source_target_pairs={{0,8},{8,0},{16,24},{24,16},{1,9},{9,1},{17,25},{25,17},{2,10},{10... | collective-permute-start | bytes 663560 | tf_op jit(solution)/shard_map/ppermute | solution.py:905
  120.7 7.8 %collective-permute-start.26 = (bf16[288,384]{1,0:T(8,128)(2,1)S(1)}, bf16[288,384]{1,0:T(8,128)(2,1)S(1)}, u32[]{:S(2)}, u32[]{:S(2)}) collective-permute-start(bf16[288,384]{1,0:T(8,128)(2,1)S(1)} %get-tuple-element.199.ga_ext.refs_0_), channel_id=1, source_target_pairs={{0,16},{8,24},{16,0},{24,8},{1,17},{9,25},{17,1},{25,9},{2,18},{10... | collective-permute-start | bytes 663560 | tf_op jit(solution)/shard_map/ppermute | solution.py:905
  136.5 7.4 %collective-permute-start.30 = (bf16[288,384]{1,0:T(8,128)(2,1)S(1)}, bf16[288,384]{1,0:T(8,128)(2,1)S(1)}, u32[]{:S(2)}, u32[]{:S(2)}) collective-permute-start(bf16[288,384]{1,0:T(8,128)(2,1)S(1)} %get-tuple-element.216.ga_ext.refs_0_), channel_id=1, source_target_pairs={{0,8},{8,0},{16,24},{24,16},{1,9},{9,1},{17,25},{25,17},{2,10},{10... | collective-permute-start | bytes 663560 | tf_op jit(solution)/shard_map/ppermute | solution.py:905
  137.0 10.1 %collective-permute-start.29 = (bf16[288,384]{1,0:T(8,128)(2,1)S(1)}, bf16[288,384]{1,0:T(8,128)(2,1)S(1)}, u32[]{:S(2)}, u32[]{:S(2)}) collective-permute-start(bf16[288,384]{1,0:T(8,128)(2,1)S(1)} %get-tuple-element.216.ga_ext.refs_0_), channel_id=1, source_target_pairs={{0,16},{8,24},{16,0},{24,8},{1,17},{9,25},{17,1},{25,9},{2,18},{10... | collective-permute-start | bytes 663560 | tf_op jit(solution)/shard_map/ppermute | solution.py:905
  153.7 4.4 %collective-permute-start.33 = (f32[36,128]{1,0:T(8,128)S(1)}, f32[36,128]{1,0:T(8,128)S(1)}, u32[]{:S(2)}, u32[]{:S(2)}) collective-permute-start(f32[36,128]{1,0:T(8,128)S(1)} %fusion.21), channel_id=1, source_target_pairs={{0,16},{1,17},{2,18},{3,19},{4,20},{5,21},{6,22},{7,23},{8,24},{9,... | collective-permute-start | bytes 55304 | tf_op jit(solution)/shard_map/ppermute | solution.py:772
  162.6 3.3 %collective-permute-start.38 = (bf16[8,720,128]{2,1,0:T(8,128)(2,1)S(1)}, bf16[8,720,128]{2,1,0:T(8,128)(2,1)S(1)}, u32[]{:S(2)}, u32[]{:S(2)}) collective-permute-start(bf16[8,720,128]{2,1,0:T(8,128)(2,1)S(1)} %get-tuple-element.261), channel_id=1, source_target_pairs={{0,8},{1,9},{2,10},{3,11},{4,12},{5,13},{6,14},{7,15},{8,0},{9,1},... | collective-permute-start | bytes 4423688 | tf_op jit(solution)/shard_map/ppermute | solution.py:772
  162.6 5.4 %collective-permute-start.34 = (bf16[8,720,128]{2,1,0:T(8,128)(2,1)S(1)}, bf16[8,720,128]{2,1,0:T(8,128)(2,1)S(1)}, u32[]{:S(2)}, u32[]{:S(2)}) collective-permute-start(bf16[8,720,128]{2,1,0:T(8,128)(2,1)S(1)} %get-tuple-element.259), channel_id=1, source_target_pairs={{0,8},{1,9},{2,10},{3,11},{4,12},{5,13},{6,14},{7,15},{8,0},{9,1},... | collective-permute-start | bytes 4423688 | tf_op jit(solution)/shard_map/ppermute | solution.py:772
  163.1 7.0 %collective-permute-start.44 = (bf16[8,720,128]{2,1,0:T(8,128)(2,1)S(1)}, bf16[8,720,128]{2,1,0:T(8,128)(2,1)S(1)}, u32[]{:S(2)}, u32[]{:S(2)}) collective-permute-start(bf16[8,720,128]{2,1,0:T(8,128)(2,1)S(1)} %get-tuple-element.272), channel_id=1, source_target_pairs={{0,8},{1,9},{2,10},{3,11},{4,12},{5,13},{6,14},{7,15},{8,0},{9,1},... | collective-permute-start | bytes 4423688 | tf_op jit(solution)/shard_map/ppermute | solution.py:772
  166.1 18.6 %collective-permute-start.39 = (bf16[4,720,128]{2,1,0:T(8,128)(2,1)S(1)}, bf16[4,720,128]{2,1,0:T(8,128)(2,1)S(1)}, u32[]{:S(2)}, u32[]{:S(2)}) collective-permute-start(bf16[4,720,128]{2,1,0:T(8,128)(2,1)S(1)} %add_convert_fusion.1), channel_id=1, source_target_pairs={{0,1},{1,0},{2,3},{3,2},{4,5},{5,4},{6,7},{7,6},{8,9},{9,8},{10,11... | collective-permute-start | bytes 2211848 | tf_op jit(solution)/shard_map/ppermute | solution.py:772
  168.2 18.6 %collective-permute-start.35 = (bf16[4,720,128]{2,1,0:T(8,128)(2,1)S(1)}, bf16[4,720,128]{2,1,0:T(8,128)(2,1)S(1)}, u32[]{:S(2)}, u32[]{:S(2)}) collective-permute-start(bf16[4,720,128]{2,1,0:T(8,128)(2,1)S(1)} %add_convert_fusion.2), channel_id=1, source_target_pairs={{0,2},{1,3},{2,0},{3,1},{4,6},{5,7},{6,4},{7,5},{8,10},{9,11},{10,... | collective-permute-start | bytes 2211848 | tf_op jit(solution)/shard_map/ppermute | solution.py:772
  170.3 19.4 %collective-permute-start.45 = (bf16[4,720,128]{2,1,0:T(8,128)(2,1)S(1)}, bf16[4,720,128]{2,1,0:T(8,128)(2,1)S(1)}, u32[]{:S(2)}, u32[]{:S(2)}) collective-permute-start(bf16[4,720,128]{2,1,0:T(8,128)(2,1)S(1)} %add_convert_fusion), channel_id=1, source_target_pairs={{0,16},{1,17},{2,18},{3,19},{4,20},{5,21},{6,22},{7,23},{8,24},{9,... | collective-permute-start | bytes 2211848 | tf_op jit(solution)/shard_map/ppermute | solution.py:772
  184.9 11.9 %collective-permute-start.40 = (bf16[2,720,128]{2,1,0:T(8,128)(2,1)S(1)}, bf16[2,720,128]{2,1,0:T(8,128)(2,1)S(1)}, u32[]{:S(2)}, u32[]{:S(2)}) collective-permute-start(bf16[2,720,128]{2,1,0:T(8,128)(2,1)S(1)} %add_convert_fusion.4), channel_id=1, source_target_pairs={{0,16},{1,17},{2,18},{3,19},{4,20},{5,21},{6,22},{7,23},{8,24},{9,... | collective-permute-start | bytes 1105928 | tf_op jit(solution)/shard_map/ppermute | solution.py:772
  187.0 11.1 %collective-permute-start.36 = (bf16[2,720,128]{2,1,0:T(8,128)(2,1)S(1)}, bf16[2,720,128]{2,1,0:T(8,128)(2,1)S(1)}, u32[]{:S(2)}, u32[]{:S(2)}) collective-permute-start(bf16[2,720,128]{2,1,0:T(8,128)(2,1)S(1)} %add_convert_fusion.5), channel_id=1, source_target_pairs={{0,1},{1,0},{2,3},{3,2},{4,5},{5,4},{6,7},{7,6},{8,9},{9,8},{10,11... | collective-permute-start | bytes 1105928 | tf_op jit(solution)/shard_map/ppermute | solution.py:772
  189.9 14.8 %collective-permute-start.46 = (bf16[2,720,128]{2,1,0:T(8,128)(2,1)S(1)}, bf16[2,720,128]{2,1,0:T(8,128)(2,1)S(1)}, u32[]{:S(2)}, u32[]{:S(2)}) collective-permute-start(bf16[2,720,128]{2,1,0:T(8,128)(2,1)S(1)} %add_convert_fusion.3), channel_id=1, source_target_pairs={{0,2},{1,3},{2,0},{3,1},{4,6},{5,7},{6,4},{7,5},{8,10},{9,11},{10,... | collective-permute-start | bytes 1105928 | tf_op jit(solution)/shard_map/ppermute | solution.py:772
  196.9 6.0 %collective-permute-start.41 = (bf16[1,720,128]{2,1,0:T(8,128)(2,1)S(1)}, bf16[1,720,128]{2,1,0:T(8,128)(2,1)S(1)}, u32[]{:S(2)}, u32[]{:S(2)}) collective-permute-start(bf16[1,720,128]{2,1,0:T(8,128)(2,1)S(1)} %add_convert_fusion.7), channel_id=1, source_target_pairs={{0,2},{1,3},{2,0},{3,1},{4,6},{5,7},{6,4},{7,5},{8,10},{9,11},{10,... | collective-permute-start | bytes 552968 | tf_op jit(solution)/shard_map/ppermute | solution.py:772
  198.2 5.6 %collective-permute-start.37 = (bf16[1,720,128]{2,1,0:T(8,128)(2,1)S(1)}, bf16[1,720,128]{2,1,0:T(8,128)(2,1)S(1)}, u32[]{:S(2)}, u32[]{:S(2)}) collective-permute-start(bf16[1,720,128]{2,1,0:T(8,128)(2,1)S(1)} %add_convert_fusion.8), channel_id=1, source_target_pairs={{0,16},{1,17},{2,18},{3,19},{4,20},{5,21},{6,22},{7,23},{8,24},{9,... | collective-permute-start | bytes 552968 | tf_op jit(solution)/shard_map/ppermute | solution.py:772
  204.6 3.3 %collective-permute-start.43 = (bf16[720,128]{1,0:T(8,128)(2,1)S(1)}, bf16[720,128]{1,0:T(8,128)(2,1)}, u32[]{:S(2)}, u32[]{:S(2)}) collective-permute-start(bf16[720,128]{1,0:T(8,128)(2,1)S(1)} %convert_bitcast_fusion.1), channel_id=1, source_target_pairs={{0,8},{1,9},{2,10},{3,11},{4,12},{5,13},{6,14},{7,15},{8,0},{9,1},... | collective-permute-start | bytes 552968 | tf_op jit(solution)/shard_map/ppermute | solution.py:772
  205.5 7.4 %collective-permute-start.47 = (bf16[1,720,128]{2,1,0:T(8,128)(2,1)}, bf16[1,720,128]{2,1,0:T(8,128)(2,1)}, u32[]{:S(2)}, u32[]{:S(2)}) collective-permute-start(bf16[1,720,128]{2,1,0:T(8,128)(2,1)} %add_convert_fusion.6), channel_id=1, source_target_pairs={{0,1},{1,0},{2,3},{3,2},{4,5},{5,4},{6,7},{7,6},{8,9},{9,8},{10,11... | collective-permute-start | bytes 552968 | tf_op jit(solution)/shard_map/ppermute | solution.py:772
  206.6 13.8 %collective-permute-start.42 = (bf16[720,128]{1,0:T(8,128)(2,1)}, bf16[720,128]{1,0:T(8,128)(2,1)}, u32[]{:S(2)}, u32[]{:S(2)}) collective-permute-start(bf16[720,128]{1,0:T(8,128)(2,1)} %bitcast_convert_fusion), channel_id=1, source_target_pairs={{12,8},{13,9},{14,10},{15,11},{8,12},{9,13},{10,14},{11,15},{28,24... | collective-permute-start | bytes 552968 | tf_op jit(solution)/shard_map/ppermute | solution.py:772
  208.8 13.4 %all-to-all-start.4 = ((f32[4,4,18,256]{3,1,2,0:T(4,128)}), f32[4,4,18,256]{3,1,2,0:T(4,128)}, u32[]{:S(2)}, u32[]{:S(2)}) async-start(f32[4,4,18,256]{3,1,2,0:T(4,128)} %copy.32), calls=%async_computation.4 | async-start | bytes 589824 | tf_op jit(solution)/shard_map/all_to_all | solution.py:1188
  214.9 14.9 %collective-permute-start.48 = (bf16[720,128]{1,0:T(8,128)(2,1)}, bf16[720,128]{1,0:T(8,128)(2,1)}, u32[]{:S(2)}, u32[]{:S(2)}) collective-permute-start(bf16[720,128]{1,0:T(8,128)(2,1)} %convert_bitcast_fusion), channel_id=1, source_target_pairs={{12,8},{13,9},{14,10},{15,11},{8,12},{9,13},{10,14},{11,15},{28,24... | collective-permute-start | bytes 552968 | tf_op jit(solution)/shard_map/ppermute | solution.py:772
  222.8 12.7 %all-to-all-start.3 = ((f32[8,36,128]{2,1,0:T(8,128)}), f32[8,36,128]{2,1,0:T(8,128)}, u32[]{:S(2)}, u32[]{:S(2)}) async-start(f32[8,36,128]{2,1,0:T(8,128)} %broadcast_in_dim.71), calls=%async_computation.3 | async-start | bytes 327680 | tf_op jit(solution)/shard_map/all_to_all | solution.py:960
  241.4 10.2 %all-to-all-start.5 = ((f32[32,1,128]{2,1,0:T(1,128)}), f32[32,1,128]{2,1,0:T(1,128)S(1)}, u32[]{:S(2)}, u32[]{:S(2)}) async-start(f32[32,1,128]{2,1,0:T(1,128)} %broadcast_in_dim.74), calls=%async_computation.5 | async-start | bytes 32768 | tf_op jit(solution)/shard_map/all_to_all | solution.py:1250
  (31 other events, 371.1 us)

commit v3 on v2

--- a/solution.py
+++ b/solution.py
@@ -835,7 +835,7 @@
             codes.append(chunk * 16 + (stream ^ cube.bit(device, cube.core)) * 8 + place)
         return codes
 
-    def gather(self, shard, early, sums, first_work, second_work):
+    def gather(self, shard, sums, first_work, planes, second_work):
         cube = self.cube
         is_one, own_first, own_second = self.flag
 
@@ -850,9 +850,7 @@
         from_zero = cube.send(shard, self.zero_pairs)
         current = [jnp.where(is_one, shard[:HALF], lower)[None], None, None]
         grow(0, hop(0, 0))
-        from_one, from_zero, current[0], early, sums = together(
-            (from_one, from_zero, current[0], early, sums)
-        )
+        from_one, from_zero, current[0], sums = together((from_one, from_zero, current[0], sums))
         first = jnp.where(own_first, shard[:HALF], from_zero[:HALF])
         second = jnp.where(own_second, shard[HALF:], from_zero[HALF:])
         current[1] = jnp.where(is_one, from_one[:HALF], first)[None]
@@ -861,8 +859,8 @@
         got = [hop(0, 1), hop(1, 0), hop(2, 0)]
         for chunk in range(3):
             grow(chunk, got[chunk])
-        current, sums = together((current, sums))
-        done = second_work(sums)
+        current, sums, planes = together((current, sums, planes))
+        done = second_work(planes, sums)
         last = [hop(0, 2), None, None]
         got = [hop(1, 1), hop(2, 1)]
         for chunk in range(2):
@@ -872,7 +870,7 @@
         other = [cube.hop(value, cube.core) for value in current]
         other_last = [cube.hop(value, cube.core) for value in last]
         pieces = [entry for group in zip(current, last, other, other_last) for entry in group]
-        return pieces, early, done
+        return pieces, done
 
     def scatter(self, keep, send, late, work):
         cube = self.cube
@@ -978,10 +976,10 @@
             sums = sums.reshape(dp_count, slots, LANES)
             return jnp.sum(lax.all_to_all(sums, "dp", 0, 0, tiled=True), axis=0)
 
-        def second_work(sums):
-            return cube.exchange_sum(sums, [[cube.core], [x]])
-
-        pieces, planes, own = plan.gather(shard, spread(planes), partial, first_work, second_work)
+        def second_work(these, sums):
+            return spread(these), cube.exchange_sum(sums, [[cube.core], [x]])
+
+        pieces, (planes, own) = plan.gather(shard, partial, first_work, planes, second_work)
         arrays = [plan.table, *pieces]
         specs = [SM] + [VM] * len(pieces)
         mods = [own[layer * BIAS_LINES : (layer + 1) * BIAS_LINES] for layer in range(LAYERS)]

time: 259 us -> 260 us (level)
  waiting for transfers between devices: 79.2 us -> 83.7 us
  starting transfers between devices: 68.1 us -> 64.6 us
  other arithmetic: 20 us -> 17 us
  transfers between devices with their start and end apart: 55 -> 55, of which waited for: 29 -> 28; matrix products, arithmetic and copies ran while one was open for 8% -> 7% of each run, Pallas kernels for 15% -> 15%
where the time goes in v3:
time: 260 us; the launch traced here: 255 us
  waiting for transfers between devices  83.7 us (32%)
  Pallas kernels  72.8 us (28%)
  starting transfers between devices  64.6 us (25%)
  other arithmetic  17 us (7%)
  local copies, waits for them, and re-layouts  9.52 us (4%)
  between operations  5.51 us (2%)
    pallas_call x22, Pallas kernels, run(): pl.pallas_call(kernel, name=name, out_shape=outs, in_specs=in_specs, out_...  72.8 us
    ppermute x37, waiting for transfers between devices, send(): return lax.ppermute(value, ('var', 'dp'), pairs)  59.5 us
    ppermute x37, starting transfers between devices, send(): return lax.ppermute(value, ('var', 'dp'), pairs)  35.2 us
    all_to_all x2, starting transfers between devices, to_all(): return lax.all_to_all(copies, 'dp', 0, 0, tiled=True)  7.93 us
    all_to_all x1, waiting for transfers between devices, first_work(): return jnp.sum(lax.all_to_all(sums, 'dp', 0, 0, tiled=True), axis=0)  6.66 us
    all_to_all x1, starting transfers between devices, first_work(): return jnp.sum(lax.all_to_all(sums, 'dp', 0, 0, tiled=True), axis=0)  6.38 us
    all_to_all x1, waiting for transfers between devices, local(): copies = lax.all_to_all(copies, ('var', 'dp'), 0, 0, tiled=True)  5.84 us
    ppermute x12, starting transfers between devices, flip(): return lax.ppermute(value, axis, [(i, i ^ bit) for i in range(count)])  5.55 us
  transfers between devices with their start and end apart: 55, of which 28 were waited for; matrix products, arithmetic and copies ran while one was open for 7% of the time, Pallas kernels for 15%

profile of v3, /device:TPU:0, one launch (start us, length us, event | category | flops | bytes accessed | tf_op | source)
XLA Modules:
  0.0 254.7 jit_solution(15568577165756465071)
XLA Ops:
  2.6 6.0 %collective-permute-start.1 = (bf16[1440,128]{1,0:T(8,128)(2,1)S(1)}, bf16[1440,128]{1,0:T(8,128)(2,1)S(1)}, u32[]{:S(2)}, u32[]{:S(2)}) collective-permute-start(bf16[1440,128]{1,0:T(8,128)(2,1)S(1)} %convert_bitcast_fusion.2.shard), channel_id=1, source_target_pairs={{0,4},{1,5},{2,6},{3,7},{7,3},{16,20},{17,21},{22,18},{23,19}} | collective-permute-start | bytes 1105928 | tf_op jit(solution)/shard_map/ppermute | solution.py:772
  9.4 3.8 %all-to-all-start = ((bf16[8,3,128]{2,1,0:T(4,128)(2,1)}), bf16[8,3,128]{2,1,0:T(4,128)(2,1)S(1)}, u32[]{:S(2)}, u32[]{:S(2)}) async-start(bf16[8,3,128]{2,1,0:T(4,128)(2,1)} %broadcast_in_dim.64), calls=%async_computation | async-start | bytes 16384 | tf_op jit(solution)/shard_map/all_to_all | solution.py:958
  15.2 2.1 collective-permute-start.3
  19.7 2.4 ada.1
  23.4 5.6 %collective-permute-start.6 = (bf16[1,720,128]{2,1,0:T(8,128)(2,1)S(1)}, bf16[1,720,128]{2,1,0:T(8,128)(2,1)S(1)}, u32[]{:S(2)}, u32[]{:S(2)}) collective-permute-start(bf16[1,720,128]{2,1,0:T(8,128)(2,1)S(1)} %get-tuple-element.316), channel_id=1, source_target_pairs={{0,2},{1,3},{2,0},{3,1},{4,6},{5,7},{6,4},{7,5},{8,10},{9,11},{10,... | collective-permute-start | bytes 552968 | tf_op jit(solution)/shard_map/ppermute | solution.py:772
  30.5 6.4 %all-to-all-start.1 = ((f32[8,36,128]{2,1,0:T(8,128)}), f32[8,36,128]{2,1,0:T(8,128)S(1)}, u32[]{:S(2)}, u32[]{:S(2)}) async-start(f32[8,36,128]{2,1,0:T(8,128)} %reshape.128), calls=%async_computation.1 | async-start | bytes 327680 | tf_op jit(solution)/shard_map/all_to_all | solution.py:977
  37.8 6.7 %all-to-all-done.1 = f32[8,36,128]{2,1,0:T(8,128)S(1)} async-done(((f32[8,36,128]{2,1,0:T(8,128)}), f32[8,36,128]{2,1,0:T(8,128)S(1)}, u32[]{:S(2)}, u32[]{:S(2)}) %all-to-all-start.1) | async-done | bytes 147488 | tf_op jit(solution)/shard_map/all_to_all | solution.py:977
  44.6 2.1 collective-permute-start.11
  49.3 3.6 %all-to-all-start.2 = ((bf16[4,5,18,256]{3,2,1,0:T(8,128)(2,1)}), bf16[4,5,18,256]{3,2,1,0:T(8,128)(2,1)S(1)}, u32[]{:S(2)}, u32[]{:S(2)}) async-start(bf16[4,5,18,256]{3,2,1,0:T(8,128)(2,1)} %maximum_bitcast_fusion), calls=%async_computation.2 | async-start | bytes 491520 | tf_op jit(solution)/shard_map/all_to_all | solution.py:944
  56.1 2.9 %all-to-all-done.2.refs_13_ = bf16[4,5,18,256]{3,2,1,0:T(8,128)(2,1)S(1)} async-done(((bf16[4,5,18,256]{3,2,1,0:T(8,128)(2,1)}), bf16[4,5,18,256]{3,2,1,0:T(8,128)(2,1)S(1)}, u32[]{:S(2)}, u32[]{:S(2)}) %all-to-all-start.2) | async-done | bytes 184352 | tf_op jit(solution)/shard_map/all_to_all | solution.py:944
  59.9 6.7 %collective-permute-done.7.refs_2_ = bf16[4,720,128]{2,1,0:T(8,128)(2,1)S(1)} collective-permute-done((bf16[4,720,128]{2,1,0:T(8,128)(2,1)S(1)}, bf16[4,720,128]{2,1,0:T(8,128)(2,1)S(1)}, u32[]{:S(2)}, u32[]{:S(2)}) %collective-permute-start.7) | collective-permute-done | bytes 737312 | tf_op jit(solution)/shard_map/ppermute | solution.py:772
  67.1 10.2 %collective-permute-done.14.refs_6_ = bf16[4,720,128]{2,1,0:T(8,128)(2,1)S(1)} collective-permute-done((bf16[4,720,128]{2,1,0:T(8,128)(2,1)S(1)}, bf16[4,720,128]{2,1,0:T(8,128)(2,1)S(1)}, u32[]{:S(2)}, u32[]{:S(2)}) %collective-permute-start.14) | collective-permute-done | bytes 737312 | tf_op jit(solution)/shard_map/ppermute | solution.py:772
  80.5 5.6 %agg_fwd.1 = (f32[256,384]{1,0:T(8,128)S(1)}, bf16[256,384]{1,0:T(8,128)(2,1)S(1)}, bf16[256,384]{1,0:T(8,128)(2,1)S(1)}, f32[6,72,256]{2,1,0:T(8,128)S(1)}, f32...) custom-call(s32[48]{0:T(128)S(1)} %get-tuple-element.319.refs_0_, ...), custom_call_target="tpu_custom_call" | custom-call | flops 1000000000 | bytes 12707520 | tf_op jit(solution)/shard_map/agg_fwd/pallas_call | solution.py:104
  87.1 3.8 %unpack_0.1 = (bf16[384,1152]{1,0:T(8,128)(2,1)S(1)}, bf16[384,384]{1,0:T(8,128)(2,1)S(1)}, bf16[384,1536]{1,0:T(8,128)(2,1)S(1)}, bf16[1536,384]{1,0:T(8,128)(2,1)S(1)}) custom-call(s32[48]{0:T(128)S(1)} %get-tuple-element.319.refs_0_, bf16[4,720,128]{2,1,0:T(8,128)(2,1)S(1)} %pad_maximum_fusion.refs_1_, ...), custom_call_target="tpu_custom_call" | custom-call | flops 1000000000 | bytes 12386496 | tf_op jit(solution)/shard_map/unpack_0/pallas_call | solution.py:104
  90.8 3.7 %near_attend_0.1 = (bf16[512,1152]{1,0:T(8,128)(2,1)S(1)}, f32[256,384]{1,0:T(8,128)S(1)}, f32[256,128]{1,0:T(8,128)S(1)}, f32[256,128]{1,0:T(8,128)S(1)}) custom-call(s32[2]{0:T(128)S(1)} %pad_add_fusion.limits, bf16[256,384]{1,0:T(8,128)(2,1)S(1)} %get-tuple-element.156.refs_0_.hidden, bf16[256,384]{1,0:T(8,128)(2,1)S(1)} %collective-permute-done.21.refs_1_, ...), custom_call_target="tpu_custom_call" | custom-call | flops 1000000000 | bytes 3112968 | tf_op jit(solution)/shard_map/near_attend_0/pallas_call | solution.py:104
  96.0 5.4 %layer_fwd_0.1 = (bf16[1024,1152]{1,0:T(8,128)(2,1)S(1)}, f32[256,384]{1,0:T(8,128)S(1)}, f32[256,128]{1,0:T(8,128)S(1)}, f32[256,384]{1,0:T(8,128)S(1)}, f32[25...) custom-call(s32[2]{0:T(128)S(1)} %pad_add_fusion.limits, ...), custom_call_target="tpu_custom_call" | custom-call | flops 4000000000 | bytes 12410888 | tf_op jit(solution)/shard_map/layer_fwd_0/pallas_call | solution.py:104
  103.0 3.8 %unpack_1.1 = (bf16[384,1152]{1,0:T(8,128)(2,1)S(1)}, bf16[384,384]{1,0:T(8,128)(2,1)S(1)}, bf16[384,1536]{1,0:T(8,128)(2,1)S(1)}, bf16[1536,384]{1,0:T(8,128)(2,1)S(1)}) custom-call(s32[48]{0:T(128)S(1)} %get-tuple-element.319.refs_0_, bf16[4,720,128]{2,1,0:T(8,128)(2,1)S(1)} %pad_maximum_fusion.refs_1_, ...), custom_call_target="tpu_custom_call" | custom-call | flops 1000000000 | bytes 12386496 | tf_op jit(solution)/shard_map/unpack_1/pallas_call | solution.py:104
  106.7 3.9 %near_attend_1.1 = (bf16[512,1152]{1,0:T(8,128)(2,1)S(1)}, f32[256,384]{1,0:T(8,128)S(1)}, f32[256,128]{1,0:T(8,128)S(1)}, f32[256,128]{1,0:T(8,128)S(1)}) custom-call(s32[2]{0:T(128)S(1)} %pad_add_fusion.limits, bf16[256,384]{1,0:T(8,128)(2,1)S(1)} %get-tuple-element.175.refs_0_.hidden, bf16[256,384]{1,0:T(8,128)(2,1)S(1)} %collective-permute-done.24.refs_1_, ...), custom_call_target="tpu_custom_call" | custom-call | flops 1000000000 | bytes 3112968 | tf_op jit(solution)/shard_map/near_attend_1/pallas_call | solution.py:104
  112.1 6.0 %layer_fwd_1.1 = (bf16[1024,1152]{1,0:T(8,128)(2,1)S(1)}, f32[256,384]{1,0:T(8,128)S(1)}, f32[256,128]{1,0:T(8,128)S(1)}, f32[256,384]{1,0:T(8,128)S(1)}, f32[25...) custom-call(s32[2]{0:T(128)S(1)} %pad_add_fusion.limits, ...), custom_call_target="tpu_custom_call" | custom-call | flops 4000000000 | bytes 12410888 | tf_op jit(solution)/shard_map/layer_fwd_1/pallas_call | solution.py:104
  118.2 2.3 mlp_bwd_1.1
  121.4 3.8 %query_bwd_1.1.refs_3_ = bf16[256,384]{1,0:T(8,128)(2,1)S(1)} custom-call(s32[2]{0:T(128)S(1)} %pad_add_fusion.limits, bf16[1024,1152]{1,0:T(8,128)(2,1)S(1)} %get-tuple-element.202.qkv.refs_2_, bf16[288,384]{1,0:T(8,128)(2,1)S(1)} %get-tuple-element.201.ga_ext.refs_0_, f32[256,128]{1,0:T(8,128)S(1)} %get-tuple-element.200.lse, ...), custom_call_target="tpu_custom_call" | custom-call | flops 4000000000 | bytes 3039240 | tf_op jit(solution)/shard_map/query_bwd_1/pallas_call | solution.py:104
  125.2 3.1 %near_keys_1.1 = (f32[256,384]{1,0:T(8,128)S(1)}, f32[256,384]{1,0:T(8,128)S(1)}) custom-call(s32[2]{0:T(128)S(1)} %pad_add_fusion.limits, bf16[288,384]{1,0:T(8,128)(2,1)S(1)} %get-tuple-element.201.ga_ext.refs_0_, bf16[288,384]{1,0:T(8,128)(2,1)S(1)} %collective-permute-done.27.refs_1_, bf16[1024,1152]{1,0:T(8,128)(2,1)S(1)} %get-tuple-element.202.qkv.refs_2_), custom_call_target="tpu_custom_call" | custom-call | flops 3000000000 | bytes 3588104 | tf_op jit(solution)/shard_map/near_keys_1/pallas_call | solution.py:104
  129.9 4.2 %keys_bwd_1.1 = (bf16[256,1152]{1,0:T(8,128)(2,1)S(1)}, f32[256,384]{1,0:T(8,128)S(1)}, f32[24,128]{1,0:T(8,128)S(1)}) custom-call(s32[2]{0:T(128)S(1)} %pad_add_fusion.limits, bf16[288,384]{1,0:T(8,128)(2,1)S(1)} %collective-permute-done.26.refs_0_, bf16[288,384]{1,0:T(8,128)(2,1)S(1)} %collective-permute-done.28.refs_1_, ...), custom_call_target="tpu_custom_call" | custom-call | flops 3000000000 | bytes 6463496 | tf_op jit(solution)/shard_map/keys_bwd_1/pallas_call | solution.py:104
  134.1 2.4 mlp_bwd_0.1
  138.2 3.8 %query_bwd_0.1.refs_3_ = bf16[256,384]{1,0:T(8,128)(2,1)S(1)} custom-call(s32[2]{0:T(128)S(1)} %pad_add_fusion.limits, bf16[1024,1152]{1,0:T(8,128)(2,1)S(1)} %get-tuple-element.219.qkv.refs_2_, bf16[288,384]{1,0:T(8,128)(2,1)S(1)} %get-tuple-element.218.ga_ext.refs_0_, f32[256,128]{1,0:T(8,128)S(1)} %get-tuple-element.217.lse, ...), custom_call_target="tpu_custom_call" | custom-call | flops 4000000000 | bytes 3039240 | tf_op jit(solution)/shard_map/query_bwd_0/pallas_call | solution.py:104
  144.0 3.1 %near_keys_0.1 = (f32[256,384]{1,0:T(8,128)S(1)}, f32[256,384]{1,0:T(8,128)S(1)}) custom-call(s32[2]{0:T(128)S(1)} %pad_add_fusion.limits, bf16[288,384]{1,0:T(8,128)(2,1)S(1)} %get-tuple-element.218.ga_ext.refs_0_, bf16[288,384]{1,0:T(8,128)(2,1)S(1)} %collective-permute-done.30.refs_1_, bf16[1024,1152]{1,0:T(8,128)(2,1)S(1)} %get-tuple-element.219.qkv.refs_2_), custom_call_target="tpu_custom_call" | custom-call | flops 3000000000 | bytes 3588104 | tf_op jit(solution)/shard_map/near_keys_0/pallas_call | solution.py:104
  147.2 1.5 collective-permute-done.31.refs_1_
  148.7 3.8 %keys_bwd_0.1 = (bf16[256,1152]{1,0:T(8,128)(2,1)S(1)}, f32[256,384]{1,0:T(8,128)S(1)}, f32[24,128]{1,0:T(8,128)S(1)}) custom-call(s32[2]{0:T(128)S(1)} %pad_add_fusion.limits, bf16[288,384]{1,0:T(8,128)(2,1)S(1)} %collective-permute-done.29.refs_0_, bf16[288,384]{1,0:T(8,128)(2,1)S(1)} %collective-permute-done.31.refs_1_, ...), custom_call_target="tpu_custom_call" | custom-call | flops 3000000000 | bytes 6463496 | tf_op jit(solution)/shard_map/keys_bwd_0/pallas_call | solution.py:104
  154.5 3.5 %agg_bwd.1 = (f32[4,4,18,256]{3,2,1,0:T(8,128)S(1)}, bf16[4336,128]{1,0:T(8,128)(2,1)S(1)}) custom-call(f32[256,384]{1,0:T(8,128)S(1)} %get-tuple-element.228.go, bf16[256,384]{1,0:T(8,128)(2,1)S(1)} %get-tuple-element.229.agg_low, f32[6,72,256]{2,1,0:T(8,128)S(1)} %get-tuple-element.230.probs, f32[288,768]{1,0:T(8,128)S(1)} %get-tuple-element.231.w, ...), custom_call_target="tpu_custom_call" | custom-call | flops 1000000000 | bytes 4871680 | tf_op jit(solution)/shard_map/agg_bwd/pallas_call | solution.py:104
  158.1 4.4 %pack.1 = (bf16[8,720,128]{2,1,0:T(8,128)(2,1)S(1)}, bf16[8,720,128]{2,1,0:T(8,128)(2,1)S(1)}, bf16[8,720,128]{2,1,0:T(8,128)(2,1)S(1)}, bf16[8,720,128]{2,1,0:T...) custom-call(s32[48]{0:T(128)S(1)} %get-tuple-element.318.table, ...), custom_call_target="tpu_custom_call" | custom-call | bytes 17051840 | tf_op jit(solution)/shard_map/pack/pallas_call | solution.py:104
  163.1 2.7 %collective-permute-done.38 = bf16[8,720,128]{2,1,0:T(8,128)(2,1)S(1)} collective-permute-done((bf16[8,720,128]{2,1,0:T(8,128)(2,1)S(1)}, bf16[8,720,128]{2,1,0:T(8,128)(2,1)S(1)}, u32[]{:S(2)}, u32[]{:S(2)}) %collective-permute-start.38) | collective-permute-done | bytes 1474592 | tf_op jit(solution)/shard_map/ppermute | solution.py:772
  170.2 1.4 collective-permute-start.45
  171.6 13.0 %collective-permute-done.39 = bf16[4,720,128]{2,1,0:T(8,128)(2,1)S(1)} collective-permute-done((bf16[4,720,128]{2,1,0:T(8,128)(2,1)S(1)}, bf16[4,720,128]{2,1,0:T(8,128)(2,1)S(1)}, u32[]{:S(2)}, u32[]{:S(2)}) %collective-permute-start.39) | collective-permute-done | bytes 737312 | tf_op jit(solution)/shard_map/ppermute | solution.py:772
  184.8 1.4 collective-permute-start.40
  187.9 1.7 collective-permute-done.45
  190.8 5.9 %collective-permute-done.40 = bf16[2,720,128]{2,1,0:T(8,128)(2,1)S(1)} collective-permute-done((bf16[2,720,128]{2,1,0:T(8,128)(2,1)S(1)}, bf16[2,720,128]{2,1,0:T(8,128)(2,1)S(1)}, u32[]{:S(2)}, u32[]{:S(2)}) %collective-permute-start.40) | collective-permute-done | bytes 368672 | tf_op jit(solution)/shard_map/ppermute | solution.py:772
  199.2 3.6 %collective-permute-done.41 = bf16[1,720,128]{2,1,0:T(8,128)(2,1)S(1)} collective-permute-done((bf16[1,720,128]{2,1,0:T(8,128)(2,1)S(1)}, bf16[1,720,128]{2,1,0:T(8,128)(2,1)S(1)}, u32[]{:S(2)}, u32[]{:S(2)}) %collective-permute-start.41) | collective-permute-done | bytes 184352 | tf_op jit(solution)/shard_map/ppermute | solution.py:772
  205.3 1.7 collective-permute-start.47
  209.1 3.5 %all-to-all-start.4 = ((f32[4,4,18,256]{3,1,2,0:T(4,128)}), f32[4,4,18,256]{3,1,2,0:T(4,128)S(1)}, u32[]{:S(2)}, u32[]{:S(2)}) async-start(f32[4,4,18,256]{3,1,2,0:T(4,128)} %copy.32), calls=%async_computation.4 | async-start | bytes 589824 | tf_op jit(solution)/shard_map/all_to_all | solution.py:1186
  212.6 2.0 convert_bitcast_fusion
  215.9 4.6 %collective-permute-done.42 = bf16[720,128]{1,0:T(8,128)(2,1)} collective-permute-done((bf16[720,128]{1,0:T(8,128)(2,1)}, bf16[720,128]{1,0:T(8,128)(2,1)}, u32[]{:S(2)}, u32[]{:S(2)}) %collective-permute-start.42) | collective-permute-done | bytes 184352 | tf_op jit(solution)/shard_map/ppermute | solution.py:772
  222.2 4.1 %all-to-all-start.3 = ((f32[8,36,128]{2,1,0:T(8,128)}), f32[8,36,128]{2,1,0:T(8,128)}, u32[]{:S(2)}, u32[]{:S(2)}) async-start(f32[8,36,128]{2,1,0:T(8,128)} %broadcast_in_dim.71), calls=%async_computation.3 | async-start | bytes 327680 | tf_op jit(solution)/shard_map/all_to_all | solution.py:958
  226.4 3.2 %collective-permute-done.48 = bf16[720,128]{1,0:T(8,128)(2,1)} collective-permute-done((bf16[720,128]{1,0:T(8,128)(2,1)}, bf16[720,128]{1,0:T(8,128)(2,1)}, u32[]{:S(2)}, u32[]{:S(2)}) %collective-permute-start.48) | collective-permute-done | bytes 184352 | tf_op jit(solution)/shard_map/ppermute | solution.py:772
  229.6 1.8 bitcast_add_fusion
  231.4 3.3 %all-to-all-done.3 = f32[8,36,128]{2,1,0:T(8,128)} async-done(((f32[8,36,128]{2,1,0:T(8,128)}), f32[8,36,128]{2,1,0:T(8,128)}, u32[]{:S(2)}, u32[]{:S(2)}) %all-to-all-start.3) | async-done | bytes 147488 | tf_op jit(solution)/shard_map/all_to_all | solution.py:958
  240.4 2.5 all-to-all-start.5
  244.1 5.8 %all-to-all-done.5 = f32[32,1,128]{2,1,0:T(1,128)S(1)} async-done(((f32[32,1,128]{2,1,0:T(1,128)}), f32[32,1,128]{2,1,0:T(1,128)S(1)}, u32[]{:S(2)}, u32[]{:S(2)}) %all-to-all-start.5) | async-done | bytes 16416 | tf_op jit(solution)/shard_map/all_to_all | solution.py:1248
  250.1 3.2 %fusion.16 = (bf16[184320]{0:T(1024)(128)(2,1)}, f32[184320]{0:T(1024)}, f32[184320]{0:T(1024)}, f32[184320]{0:T(1024)}) fusion(f32[184320]{0:T(1024)S(1)} %copy-done.6, f32[1440,128]{1,0:T(8,128)S(1)} %get-tuple-element.324, f32[]{:T(128)S(6)} %div.28, f32[184320]{0:T(1024)} %param.15, f32[184320]{0:T(1024)} %param.16), kind=kLoop, calls=%fused_computation.71 | loop fusion | flops 2949120 | bytes 5529604 | tf_op jit(solution)/shard_map/convert_element_type | solution.py:1268
  (200 shorter events, 57.6 us)
Async XLA Ops:
  1.9 21.4 %collective-permute-start = (bf16[1440,128]{1,0:T(8,128)(2,1)S(1)}, bf16[1440,128]{1,0:T(8,128)(2,1)S(1)}, u32[]{:S(2)}, u32[]{:S(2)}) collective-permute-start(bf16[1440,128]{1,0:T(8,128)(2,1)S(1)} %convert_bitcast_fusion.2.shard), channel_id=1, source_target_pairs={{8,12},{9,13},{10,14},{11,15},{12,8},{13,9},{14,10},{15,11},{24,28... | collective-permute-start | bytes 1105928 | tf_op jit(solution)/shard_map/ppermute | solution.py:772
  2.6 20.7 %collective-permute-start.1 = (bf16[1440,128]{1,0:T(8,128)(2,1)S(1)}, bf16[1440,128]{1,0:T(8,128)(2,1)S(1)}, u32[]{:S(2)}, u32[]{:S(2)}) collective-permute-start(bf16[1440,128]{1,0:T(8,128)(2,1)S(1)} %convert_bitcast_fusion.2.shard), channel_id=1, source_target_pairs={{0,4},{1,5},{2,6},{3,7},{7,3},{16,20},{17,21},{22,18},{23,19}} | collective-permute-start | bytes 1105928 | tf_op jit(solution)/shard_map/ppermute | solution.py:772
  8.6 6.5 %collective-permute-start.2 = (bf16[720,128]{1,0:T(8,128)(2,1)S(1)}, bf16[720,128]{1,0:T(8,128)(2,1)S(1)}, u32[]{:S(2)}, u32[]{:S(2)}) collective-permute-start(bf16[720,128]{1,0:T(8,128)(2,1)S(1)} %slice_bitcast_fusion), channel_id=1, source_target_pairs={{0,8},{1,9},{2,10},{3,11},{4,12},{5,13},{6,14},{7,15},{8,0},{9,1},... | collective-permute-start | bytes 552968 | tf_op jit(solution)/shard_map/ppermute | solution.py:772
  9.4 10.4 %all-to-all-start = ((bf16[8,3,128]{2,1,0:T(4,128)(2,1)}), bf16[8,3,128]{2,1,0:T(4,128)(2,1)S(1)}, u32[]{:S(2)}, u32[]{:S(2)}) async-start(bf16[8,3,128]{2,1,0:T(4,128)(2,1)} %broadcast_in_dim.64), calls=%async_computation | async-start | bytes 16384 | tf_op jit(solution)/shard_map/all_to_all | solution.py:958
  15.2 8.1 %collective-permute-start.3 = (bf16[1,720,128]{2,1,0:T(8,128)(2,1)S(1)}, bf16[1,720,128]{2,1,0:T(8,128)(2,1)S(1)}, u32[]{:S(2)}, u32[]{:S(2)}) collective-permute-start(bf16[1,720,128]{2,1,0:T(8,128)(2,1)S(1)} %select_bitcast_fusion.2), channel_id=1, source_target_pairs={{0,1},{1,0},{2,3},{3,2},{4,5},{5,4},{6,7},{7,6},{8,9},{9,8},{10,11... | collective-permute-start | bytes 552968 | tf_op jit(solution)/shard_map/ppermute | solution.py:772
  23.4 14.3 %collective-permute-start.6 = (bf16[1,720,128]{2,1,0:T(8,128)(2,1)S(1)}, bf16[1,720,128]{2,1,0:T(8,128)(2,1)S(1)}, u32[]{:S(2)}, u32[]{:S(2)}) collective-permute-start(bf16[1,720,128]{2,1,0:T(8,128)(2,1)S(1)} %get-tuple-element.316), channel_id=1, source_target_pairs={{0,2},{1,3},{2,0},{3,1},{4,6},{5,7},{6,4},{7,5},{8,10},{9,11},{10,... | collective-permute-start | bytes 552968 | tf_op jit(solution)/shard_map/ppermute | solution.py:772
  28.9 15.5 %collective-permute-start.4 = (bf16[2,720,128]{2,1,0:T(8,128)(2,1)S(1)}, bf16[2,720,128]{2,1,0:T(8,128)(2,1)S(1)}, u32[]{:S(2)}, u32[]{:S(2)}) collective-permute-start(bf16[2,720,128]{2,1,0:T(8,128)(2,1)S(1)} %pad_maximum_fusion.3), channel_id=1, source_target_pairs={{0,16},{1,17},{2,18},{3,19},{4,20},{5,21},{6,22},{7,23},{8,24},{9,... | collective-permute-start | bytes 1105928 | tf_op jit(solution)/shard_map/ppermute | solution.py:772
  29.1 8.7 %collective-permute-start.5 = (bf16[1,720,128]{2,1,0:T(8,128)(2,1)S(1)}, bf16[1,720,128]{2,1,0:T(8,128)(2,1)S(1)}, u32[]{:S(2)}, u32[]{:S(2)}) collective-permute-start(bf16[1,720,128]{2,1,0:T(8,128)(2,1)S(1)} %get-tuple-element.317), channel_id=1, source_target_pairs={{0,2},{1,3},{2,0},{3,1},{4,6},{5,7},{6,4},{7,5},{8,10},{9,11},{10,... | collective-permute-start | bytes 552968 | tf_op jit(solution)/shard_map/ppermute | solution.py:772
  30.5 13.9 %all-to-all-start.1 = ((f32[8,36,128]{2,1,0:T(8,128)}), f32[8,36,128]{2,1,0:T(8,128)S(1)}, u32[]{:S(2)}, u32[]{:S(2)}) async-start(f32[8,36,128]{2,1,0:T(8,128)} %reshape.128), calls=%async_computation.1 | async-start | bytes 327680 | tf_op jit(solution)/shard_map/all_to_all | solution.py:977
  44.6 9.2 %collective-permute-start.11 = (bf16[2,720,128]{2,1,0:T(8,128)(2,1)S(1)}, bf16[2,720,128]{2,1,0:T(8,128)(2,1)}, u32[]{:S(2)}, u32[]{:S(2)}) collective-permute-start(bf16[2,720,128]{2,1,0:T(8,128)(2,1)S(1)} %pad_maximum_fusion.5), channel_id=1, source_target_pairs={{0,16},{1,17},{2,18},{3,19},{4,20},{5,21},{6,22},{7,23},{8,24},{9,... | collective-permute-start | bytes 1105928 | tf_op jit(solution)/shard_map/ppermute | solution.py:772
  46.7 8.2 %collective-permute-start.10 = (bf16[2,720,128]{2,1,0:T(8,128)(2,1)S(1)}, bf16[2,720,128]{2,1,0:T(8,128)(2,1)}, u32[]{:S(2)}, u32[]{:S(2)}) collective-permute-start(bf16[2,720,128]{2,1,0:T(8,128)(2,1)S(1)} %pad_maximum_fusion.4), channel_id=1, source_target_pairs={{0,1},{1,0},{2,3},{3,2},{4,5},{5,4},{6,7},{7,6},{8,9},{9,8},{10,11... | collective-permute-start | bytes 1105928 | tf_op jit(solution)/shard_map/ppermute | solution.py:772
  48.0 5.8 %collective-permute-start.13 = (f32[36,128]{1,0:T(8,128)S(1)}, f32[36,128]{1,0:T(8,128)S(1)}, u32[]{:S(2)}, u32[]{:S(2)}) collective-permute-start(f32[36,128]{1,0:T(8,128)S(1)} %add.182), channel_id=1, source_target_pairs={{0,16},{1,17},{2,18},{3,19},{4,20},{5,21},{6,22},{7,23},{8,24},{9,... | collective-permute-start | bytes 55304 | tf_op jit(solution)/shard_map/ppermute | solution.py:772
  48.2 18.4 %collective-permute-start.7 = (bf16[4,720,128]{2,1,0:T(8,128)(2,1)S(1)}, bf16[4,720,128]{2,1,0:T(8,128)(2,1)S(1)}, u32[]{:S(2)}, u32[]{:S(2)}) collective-permute-start(bf16[4,720,128]{2,1,0:T(8,128)(2,1)S(1)} %pad_maximum_fusion.refs_1_), channel_id=1, source_target_pairs={{0,2},{1,3},{2,0},{3,1},{4,6},{5,7},{6,4},{7,5},{8,10},{9,11},{10,... | collective-permute-start | bytes 2211848 | tf_op jit(solution)/shard_map/ppermute | solution.py:772
  49.3 17.3 %collective-permute-start.8 = (bf16[4,720,128]{2,1,0:T(8,128)(2,1)S(1)}, bf16[4,720,128]{2,1,0:T(8,128)(2,1)}, u32[]{:S(2)}, u32[]{:S(2)}) collective-permute-start(bf16[4,720,128]{2,1,0:T(8,128)(2,1)S(1)} %pad_maximum_fusion.refs_1_), channel_id=1, source_target_pairs={{0,8},{1,9},{2,10},{3,11},{4,12},{5,13},{6,14},{7,15},{8,0},{9,1},... | collective-permute-start | bytes 2211848 | tf_op jit(solution)/shard_map/ppermute | solution.py:772
  49.3 9.7 %all-to-all-start.2 = ((bf16[4,5,18,256]{3,2,1,0:T(8,128)(2,1)}), bf16[4,5,18,256]{3,2,1,0:T(8,128)(2,1)S(1)}, u32[]{:S(2)}, u32[]{:S(2)}) async-start(bf16[4,5,18,256]{3,2,1,0:T(8,128)(2,1)} %maximum_bitcast_fusion), calls=%async_computation.2 | async-start | bytes 491520 | tf_op jit(solution)/shard_map/all_to_all | solution.py:944
  59.0 18.3 %collective-permute-start.14 = (bf16[4,720,128]{2,1,0:T(8,128)(2,1)S(1)}, bf16[4,720,128]{2,1,0:T(8,128)(2,1)S(1)}, u32[]{:S(2)}, u32[]{:S(2)}) collective-permute-start(bf16[4,720,128]{2,1,0:T(8,128)(2,1)S(1)} %pad_maximum_fusion.1.refs_5_), channel_id=1, source_target_pairs={{0,16},{1,17},{2,18},{3,19},{4,20},{5,21},{6,22},{7,23},{8,24},{9,... | collective-permute-start | bytes 2211848 | tf_op jit(solution)/shard_map/ppermute | solution.py:772
  59.0 18.2 %collective-permute-start.17 = (bf16[4,720,128]{2,1,0:T(8,128)(2,1)S(1)}, bf16[4,720,128]{2,1,0:T(8,128)(2,1)S(1)}, u32[]{:S(2)}, u32[]{:S(2)}) collective-permute-start(bf16[4,720,128]{2,1,0:T(8,128)(2,1)S(1)} %pad_maximum_fusion.2.refs_9_), channel_id=1, source_target_pairs={{0,1},{1,0},{2,3},{3,2},{4,5},{5,4},{6,7},{7,6},{8,9},{9,8},{10,11... | collective-permute-start | bytes 2211848 | tf_op jit(solution)/shard_map/ppermute | solution.py:772
  59.9 18.7 %collective-permute-start.15 = (bf16[4,720,128]{2,1,0:T(8,128)(2,1)S(1)}, bf16[4,720,128]{2,1,0:T(8,128)(2,1)S(1)}, u32[]{:S(2)}, u32[]{:S(2)}) collective-permute-start(bf16[4,720,128]{2,1,0:T(8,128)(2,1)S(1)} %pad_maximum_fusion.1.refs_5_), channel_id=1, source_target_pairs={{0,8},{1,9},{2,10},{3,11},{4,12},{5,13},{6,14},{7,15},{8,0},{9,1},... | collective-permute-start | bytes 2211848 | tf_op jit(solution)/shard_map/ppermute | solution.py:772
  66.6 12.0 %collective-permute-start.18 = (bf16[4,720,128]{2,1,0:T(8,128)(2,1)S(1)}, bf16[4,720,128]{2,1,0:T(8,128)(2,1)S(1)}, u32[]{:S(2)}, u32[]{:S(2)}) collective-permute-start(bf16[4,720,128]{2,1,0:T(8,128)(2,1)S(1)} %pad_maximum_fusion.2.refs_9_), channel_id=1, source_target_pairs={{0,8},{1,9},{2,10},{3,11},{4,12},{5,13},{6,14},{7,15},{8,0},{9,1},... | collective-permute-start | bytes 2211848 | tf_op jit(solution)/shard_map/ppermute | solution.py:772
  66.6 12.0 %collective-permute-start.9 = (bf16[4,720,128]{2,1,0:T(8,128)(2,1)S(1)}, bf16[4,720,128]{2,1,0:T(8,128)(2,1)S(1)}, u32[]{:S(2)}, u32[]{:S(2)}) collective-permute-start(bf16[4,720,128]{2,1,0:T(8,128)(2,1)S(1)} %collective-permute-done.7.refs_2_), channel_id=1, source_target_pairs={{0,8},{1,9},{2,10},{3,11},{4,12},{5,13},{6,14},{7,15},{8,0},{9,1},... | collective-permute-start | bytes 2211848 | tf_op jit(solution)/shard_map/ppermute | solution.py:772
  77.2 3.3 %collective-permute-start.19 = (bf16[4,720,128]{2,1,0:T(8,128)(2,1)S(1)}, bf16[4,720,128]{2,1,0:T(8,128)(2,1)S(1)}, u32[]{:S(2)}, u32[]{:S(2)}) collective-permute-start(bf16[4,720,128]{2,1,0:T(8,128)(2,1)S(1)} %collective-permute-done.17.refs_10_), channel_id=1, source_target_pairs={{0,8},{1,9},{2,10},{3,11},{4,12},{5,13},{6,14},{7,15},{8,0},{9,1},... | collective-permute-start | bytes 2211848 | tf_op jit(solution)/shard_map/ppermute | solution.py:772
  86.1 4.7 %collective-permute-start.21 = (bf16[256,384]{1,0:T(8,128)(2,1)S(1)}, bf16[256,384]{1,0:T(8,128)(2,1)S(1)}, u32[]{:S(2)}, u32[]{:S(2)}) collective-permute-start(bf16[256,384]{1,0:T(8,128)(2,1)S(1)} %get-tuple-element.156.refs_0_.hidden), channel_id=1, source_target_pairs={{0,8},{8,0},{16,24},{24,16},{1,9},{9,1},{17,25},{25,17},{2,10},{10... | collective-permute-start | bytes 589832 | tf_op jit(solution)/shard_map/ppermute | solution.py:903
  86.3 8.3 %collective-permute-start.20 = (bf16[256,384]{1,0:T(8,128)(2,1)S(1)}, bf16[256,384]{1,0:T(8,128)(2,1)S(1)}, u32[]{:S(2)}, u32[]{:S(2)}) collective-permute-start(bf16[256,384]{1,0:T(8,128)(2,1)S(1)} %get-tuple-element.156.refs_0_.hidden), channel_id=1, source_target_pairs={{0,16},{8,24},{16,0},{24,8},{1,17},{9,25},{17,1},{25,9},{2,18},{10... | collective-permute-start | bytes 589832 | tf_op jit(solution)/shard_map/ppermute | solution.py:903
  101.4 5.3 %collective-permute-start.24 = (bf16[256,384]{1,0:T(8,128)(2,1)S(1)}, bf16[256,384]{1,0:T(8,128)(2,1)S(1)}, u32[]{:S(2)}, u32[]{:S(2)}) collective-permute-start(bf16[256,384]{1,0:T(8,128)(2,1)S(1)} %get-tuple-element.175.refs_0_.hidden), channel_id=1, source_target_pairs={{0,8},{8,0},{16,24},{24,16},{1,9},{9,1},{17,25},{25,17},{2,10},{10... | collective-permute-start | bytes 589832 | tf_op jit(solution)/shard_map/ppermute | solution.py:903
  101.6 9.0 %collective-permute-start.23 = (bf16[256,384]{1,0:T(8,128)(2,1)S(1)}, bf16[256,384]{1,0:T(8,128)(2,1)S(1)}, u32[]{:S(2)}, u32[]{:S(2)}) collective-permute-start(bf16[256,384]{1,0:T(8,128)(2,1)S(1)} %get-tuple-element.175.refs_0_.hidden), channel_id=1, source_target_pairs={{0,16},{8,24},{16,0},{24,8},{1,17},{9,25},{17,1},{25,9},{2,18},{10... | collective-permute-start | bytes 589832 | tf_op jit(solution)/shard_map/ppermute | solution.py:903
  120.5 4.7 %collective-permute-start.27 = (bf16[288,384]{1,0:T(8,128)(2,1)S(1)}, bf16[288,384]{1,0:T(8,128)(2,1)S(1)}, u32[]{:S(2)}, u32[]{:S(2)}) collective-permute-start(bf16[288,384]{1,0:T(8,128)(2,1)S(1)} %get-tuple-element.201.ga_ext.refs_0_), channel_id=1, source_target_pairs={{0,8},{8,0},{16,24},{24,16},{1,9},{9,1},{17,25},{25,17},{2,10},{10... | collective-permute-start | bytes 663560 | tf_op jit(solution)/shard_map/ppermute | solution.py:903
  120.7 7.7 %collective-permute-start.26 = (bf16[288,384]{1,0:T(8,128)(2,1)S(1)}, bf16[288,384]{1,0:T(8,128)(2,1)S(1)}, u32[]{:S(2)}, u32[]{:S(2)}) collective-permute-start(bf16[288,384]{1,0:T(8,128)(2,1)S(1)} %get-tuple-element.201.ga_ext.refs_0_), channel_id=1, source_target_pairs={{0,16},{8,24},{16,0},{24,8},{1,17},{9,25},{17,1},{25,9},{2,18},{10... | collective-permute-start | bytes 663560 | tf_op jit(solution)/shard_map/ppermute | solution.py:903
  136.4 7.6 %collective-permute-start.30 = (bf16[288,384]{1,0:T(8,128)(2,1)S(1)}, bf16[288,384]{1,0:T(8,128)(2,1)S(1)}, u32[]{:S(2)}, u32[]{:S(2)}) collective-permute-start(bf16[288,384]{1,0:T(8,128)(2,1)S(1)} %get-tuple-element.218.ga_ext.refs_0_), channel_id=1, source_target_pairs={{0,8},{8,0},{16,24},{24,16},{1,9},{9,1},{17,25},{25,17},{2,10},{10... | collective-permute-start | bytes 663560 | tf_op jit(solution)/shard_map/ppermute | solution.py:903
  136.9 10.2 %collective-permute-start.29 = (bf16[288,384]{1,0:T(8,128)(2,1)S(1)}, bf16[288,384]{1,0:T(8,128)(2,1)S(1)}, u32[]{:S(2)}, u32[]{:S(2)}) collective-permute-start(bf16[288,384]{1,0:T(8,128)(2,1)S(1)} %get-tuple-element.218.ga_ext.refs_0_), channel_id=1, source_target_pairs={{0,16},{8,24},{16,0},{24,8},{1,17},{9,25},{17,1},{25,9},{2,18},{10... | collective-permute-start | bytes 663560 | tf_op jit(solution)/shard_map/ppermute | solution.py:903
  153.8 4.3 %collective-permute-start.33 = (f32[36,128]{1,0:T(8,128)S(1)}, f32[36,128]{1,0:T(8,128)S(1)}, u32[]{:S(2)}, u32[]{:S(2)}) collective-permute-start(f32[36,128]{1,0:T(8,128)S(1)} %fusion.21), channel_id=1, source_target_pairs={{0,16},{1,17},{2,18},{3,19},{4,20},{5,21},{6,22},{7,23},{8,24},{9,... | collective-permute-start | bytes 55304 | tf_op jit(solution)/shard_map/ppermute | solution.py:772
  162.5 3.3 %collective-permute-start.38 = (bf16[8,720,128]{2,1,0:T(8,128)(2,1)S(1)}, bf16[8,720,128]{2,1,0:T(8,128)(2,1)S(1)}, u32[]{:S(2)}, u32[]{:S(2)}) collective-permute-start(bf16[8,720,128]{2,1,0:T(8,128)(2,1)S(1)} %get-tuple-element.263), channel_id=1, source_target_pairs={{0,8},{1,9},{2,10},{3,11},{4,12},{5,13},{6,14},{7,15},{8,0},{9,1},... | collective-permute-start | bytes 4423688 | tf_op jit(solution)/shard_map/ppermute | solution.py:772
  162.6 5.4 %collective-permute-start.34 = (bf16[8,720,128]{2,1,0:T(8,128)(2,1)S(1)}, bf16[8,720,128]{2,1,0:T(8,128)(2,1)S(1)}, u32[]{:S(2)}, u32[]{:S(2)}) collective-permute-start(bf16[8,720,128]{2,1,0:T(8,128)(2,1)S(1)} %get-tuple-element.261), channel_id=1, source_target_pairs={{0,8},{1,9},{2,10},{3,11},{4,12},{5,13},{6,14},{7,15},{8,0},{9,1},... | collective-permute-start | bytes 4423688 | tf_op jit(solution)/shard_map/ppermute | solution.py:772
  163.1 7.0 %collective-permute-start.44 = (bf16[8,720,128]{2,1,0:T(8,128)(2,1)S(1)}, bf16[8,720,128]{2,1,0:T(8,128)(2,1)S(1)}, u32[]{:S(2)}, u32[]{:S(2)}) collective-permute-start(bf16[8,720,128]{2,1,0:T(8,128)(2,1)S(1)} %get-tuple-element.274), channel_id=1, source_target_pairs={{0,8},{1,9},{2,10},{3,11},{4,12},{5,13},{6,14},{7,15},{8,0},{9,1},... | collective-permute-start | bytes 4423688 | tf_op jit(solution)/shard_map/ppermute | solution.py:772
  166.0 18.6 %collective-permute-start.39 = (bf16[4,720,128]{2,1,0:T(8,128)(2,1)S(1)}, bf16[4,720,128]{2,1,0:T(8,128)(2,1)S(1)}, u32[]{:S(2)}, u32[]{:S(2)}) collective-permute-start(bf16[4,720,128]{2,1,0:T(8,128)(2,1)S(1)} %add_convert_fusion.1), channel_id=1, source_target_pairs={{0,1},{1,0},{2,3},{3,2},{4,5},{5,4},{6,7},{7,6},{8,9},{9,8},{10,11... | collective-permute-start | bytes 2211848 | tf_op jit(solution)/shard_map/ppermute | solution.py:772
  168.1 18.6 %collective-permute-start.35 = (bf16[4,720,128]{2,1,0:T(8,128)(2,1)S(1)}, bf16[4,720,128]{2,1,0:T(8,128)(2,1)S(1)}, u32[]{:S(2)}, u32[]{:S(2)}) collective-permute-start(bf16[4,720,128]{2,1,0:T(8,128)(2,1)S(1)} %add_convert_fusion.2), channel_id=1, source_target_pairs={{0,2},{1,3},{2,0},{3,1},{4,6},{5,7},{6,4},{7,5},{8,10},{9,11},{10,... | collective-permute-start | bytes 2211848 | tf_op jit(solution)/shard_map/ppermute | solution.py:772
  170.2 19.4 %collective-permute-start.45 = (bf16[4,720,128]{2,1,0:T(8,128)(2,1)S(1)}, bf16[4,720,128]{2,1,0:T(8,128)(2,1)S(1)}, u32[]{:S(2)}, u32[]{:S(2)}) collective-permute-start(bf16[4,720,128]{2,1,0:T(8,128)(2,1)S(1)} %add_convert_fusion), channel_id=1, source_target_pairs={{0,16},{1,17},{2,18},{3,19},{4,20},{5,21},{6,22},{7,23},{8,24},{9,... | collective-permute-start | bytes 2211848 | tf_op jit(solution)/shard_map/ppermute | solution.py:772
  184.8 12.0 %collective-permute-start.40 = (bf16[2,720,128]{2,1,0:T(8,128)(2,1)S(1)}, bf16[2,720,128]{2,1,0:T(8,128)(2,1)S(1)}, u32[]{:S(2)}, u32[]{:S(2)}) collective-permute-start(bf16[2,720,128]{2,1,0:T(8,128)(2,1)S(1)} %add_convert_fusion.4), channel_id=1, source_target_pairs={{0,16},{1,17},{2,18},{3,19},{4,20},{5,21},{6,22},{7,23},{8,24},{9,... | collective-permute-start | bytes 1105928 | tf_op jit(solution)/shard_map/ppermute | solution.py:772
  186.9 11.0 %collective-permute-start.36 = (bf16[2,720,128]{2,1,0:T(8,128)(2,1)S(1)}, bf16[2,720,128]{2,1,0:T(8,128)(2,1)S(1)}, u32[]{:S(2)}, u32[]{:S(2)}) collective-permute-start(bf16[2,720,128]{2,1,0:T(8,128)(2,1)S(1)} %add_convert_fusion.5), channel_id=1, source_target_pairs={{0,1},{1,0},{2,3},{3,2},{4,5},{5,4},{6,7},{7,6},{8,9},{9,8},{10,11... | collective-permute-start | bytes 1105928 | tf_op jit(solution)/shard_map/ppermute | solution.py:772
  189.8 14.7 %collective-permute-start.46 = (bf16[2,720,128]{2,1,0:T(8,128)(2,1)S(1)}, bf16[2,720,128]{2,1,0:T(8,128)(2,1)S(1)}, u32[]{:S(2)}, u32[]{:S(2)}) collective-permute-start(bf16[2,720,128]{2,1,0:T(8,128)(2,1)S(1)} %add_convert_fusion.3), channel_id=1, source_target_pairs={{0,2},{1,3},{2,0},{3,1},{4,6},{5,7},{6,4},{7,5},{8,10},{9,11},{10,... | collective-permute-start | bytes 1105928 | tf_op jit(solution)/shard_map/ppermute | solution.py:772
  196.8 6.0 %collective-permute-start.41 = (bf16[1,720,128]{2,1,0:T(8,128)(2,1)S(1)}, bf16[1,720,128]{2,1,0:T(8,128)(2,1)S(1)}, u32[]{:S(2)}, u32[]{:S(2)}) collective-permute-start(bf16[1,720,128]{2,1,0:T(8,128)(2,1)S(1)} %add_convert_fusion.7), channel_id=1, source_target_pairs={{0,2},{1,3},{2,0},{3,1},{4,6},{5,7},{6,4},{7,5},{8,10},{9,11},{10,... | collective-permute-start | bytes 552968 | tf_op jit(solution)/shard_map/ppermute | solution.py:772
  198.0 5.6 %collective-permute-start.37 = (bf16[1,720,128]{2,1,0:T(8,128)(2,1)S(1)}, bf16[1,720,128]{2,1,0:T(8,128)(2,1)S(1)}, u32[]{:S(2)}, u32[]{:S(2)}) collective-permute-start(bf16[1,720,128]{2,1,0:T(8,128)(2,1)S(1)} %add_convert_fusion.8), channel_id=1, source_target_pairs={{0,16},{1,17},{2,18},{3,19},{4,20},{5,21},{6,22},{7,23},{8,24},{9,... | collective-permute-start | bytes 552968 | tf_op jit(solution)/shard_map/ppermute | solution.py:772
  204.4 3.9 %collective-permute-start.43 = (bf16[720,128]{1,0:T(8,128)(2,1)S(1)}, bf16[720,128]{1,0:T(8,128)(2,1)}, u32[]{:S(2)}, u32[]{:S(2)}) collective-permute-start(bf16[720,128]{1,0:T(8,128)(2,1)S(1)} %convert_bitcast_fusion.1), channel_id=1, source_target_pairs={{0,8},{1,9},{2,10},{3,11},{4,12},{5,13},{6,14},{7,15},{8,0},{9,1},... | collective-permute-start | bytes 552968 | tf_op jit(solution)/shard_map/ppermute | solution.py:772
  205.3 7.3 %collective-permute-start.47 = (bf16[1,720,128]{2,1,0:T(8,128)(2,1)}, bf16[1,720,128]{2,1,0:T(8,128)(2,1)}, u32[]{:S(2)}, u32[]{:S(2)}) collective-permute-start(bf16[1,720,128]{2,1,0:T(8,128)(2,1)} %add_convert_fusion.6), channel_id=1, source_target_pairs={{0,1},{1,0},{2,3},{3,2},{4,5},{5,4},{6,7},{7,6},{8,9},{9,8},{10,11... | collective-permute-start | bytes 552968 | tf_op jit(solution)/shard_map/ppermute | solution.py:772
  207.0 13.5 %collective-permute-start.42 = (bf16[720,128]{1,0:T(8,128)(2,1)}, bf16[720,128]{1,0:T(8,128)(2,1)}, u32[]{:S(2)}, u32[]{:S(2)}) collective-permute-start(bf16[720,128]{1,0:T(8,128)(2,1)} %bitcast_convert_fusion), channel_id=1, source_target_pairs={{12,8},{13,9},{14,10},{15,11},{8,12},{9,13},{10,14},{11,15},{28,24... | collective-permute-start | bytes 552968 | tf_op jit(solution)/shard_map/ppermute | solution.py:772
  209.1 12.4 %all-to-all-start.4 = ((f32[4,4,18,256]{3,1,2,0:T(4,128)}), f32[4,4,18,256]{3,1,2,0:T(4,128)S(1)}, u32[]{:S(2)}, u32[]{:S(2)}) async-start(f32[4,4,18,256]{3,1,2,0:T(4,128)} %copy.32), calls=%async_computation.4 | async-start | bytes 589824 | tf_op jit(solution)/shard_map/all_to_all | solution.py:1186
  214.6 15.0 %collective-permute-start.48 = (bf16[720,128]{1,0:T(8,128)(2,1)}, bf16[720,128]{1,0:T(8,128)(2,1)}, u32[]{:S(2)}, u32[]{:S(2)}) collective-permute-start(bf16[720,128]{1,0:T(8,128)(2,1)} %convert_bitcast_fusion), channel_id=1, source_target_pairs={{12,8},{13,9},{14,10},{15,11},{8,12},{9,13},{10,14},{11,15},{28,24... | collective-permute-start | bytes 552968 | tf_op jit(solution)/shard_map/ppermute | solution.py:772
  222.2 12.4 %all-to-all-start.3 = ((f32[8,36,128]{2,1,0:T(8,128)}), f32[8,36,128]{2,1,0:T(8,128)}, u32[]{:S(2)}, u32[]{:S(2)}) async-start(f32[8,36,128]{2,1,0:T(8,128)} %broadcast_in_dim.71), calls=%async_computation.3 | async-start | bytes 327680 | tf_op jit(solution)/shard_map/all_to_all | solution.py:958
  240.4 9.6 %all-to-all-start.5 = ((f32[32,1,128]{2,1,0:T(1,128)}), f32[32,1,128]{2,1,0:T(1,128)S(1)}, u32[]{:S(2)}, u32[]{:S(2)}) async-start(f32[32,1,128]{2,1,0:T(1,128)} %broadcast_in_dim.74), calls=%async_computation.5 | async-start | bytes 32768 | tf_op jit(solution)/shard_map/all_to_all | solution.py:1248
  (33 other events, 389.3 us)
